TPU v7x, 512 devices: a whole 4x8x8 slice. The times are simulated.
512 devices in a mesh: bg: 128 (over y, z, core), sp: 4 (over x).
Axes of the slice: x: 4, y: 8, z: 8, core: 2. Of those that a mesh axis runs over, the one named last changes fastest.
Arguments:
- covariates: bfloat16 [65536, 256], P(('bg', 'sp')), may hold values from -6 to 6
- first_weight: bfloat16 [8, 128, 128], replicated, may hold values from -0.5 to 0.5
- first_bias: float32 [1024], replicated, may hold values from -3 to 3
- first_index: int32 [8], replicated, may hold values from 0 to 1
- second_weight: bfloat16 [8, 128, 128], replicated, may hold values from -0.5 to 0.5
- second_bias: float32 [1024], replicated, may hold values from -3 to 3
- second_index: int32 [8], replicated, may hold values from 0 to 7
- head_weight: bfloat16 [80, 64, 128], P('sp'), may hold values from -150 to 150
- clade_block: int32 [80], P('sp'), may hold values from 0 to 15
- presence: int32 [10240, 16], P('sp'), may hold values from 0 to 65535, as said below
Outputs:
- species_loss: float32 [10240], P('sp')
- head_grad: float32 [80, 64, 128], P('sp')
- first_grad: float32 [8, 128, 128], replicated
- first_bias_grad: float32 [1024], replicated
- second_grad: float32 [8, 128, 128], replicated
- second_bias_grad: float32 [1024], replicated
Inputs may be any that keep to these rules, and one draw needn't show every extreme that they name: `presence`: the records of one species lie within 128 consecutive cells; cells may repeat.
All inputs are finite; a program needn't handle non-finite values.
Results may differ from a plain program's by a relative error of at most 0.014.
Values may be sent and summed in bfloat16 or wider, within the bound.
No kernel may reach another device: no remote copies, remote signals or barrier semaphores. Data moves between devices by JAX's collectives and lax.ppermute only.
A program may use at most 64 MiB of HBM per device.

v0:
```python
import math

import jax
import jax.numpy as jnp
from jax import lax
from jax.sharding import PartitionSpec as P


def silu_slope(values):
    sigma = jax.nn.sigmoid(values)
    return sigma * (1.0 + values * (1.0 - sigma))


def trunk_forward(
    covariates, first_weight, first_bias, first_index, second_weight, second_bias, second_index
):
    row_count = covariates.shape[0]
    blocks = first_weight.shape[0]
    tile_size = first_weight.shape[1]
    inputs = jnp.take(covariates.reshape(row_count, -1, tile_size), first_index, axis=1)
    first_pre = jnp.einsum(
        "rot,oti->roi", inputs, first_weight, preferred_element_type=jnp.float32
    ) + first_bias.reshape(blocks, tile_size)
    first_act = jax.nn.silu(first_pre).astype(jnp.bfloat16)
    middle = jnp.take(first_act, second_index, axis=1)
    second_pre = jnp.einsum(
        "rot,oti->roi", middle, second_weight, preferred_element_type=jnp.float32
    ) + second_bias.reshape(blocks, tile_size)
    features = jax.nn.silu(second_pre).astype(jnp.bfloat16).reshape(row_count, blocks * tile_size)
    return (inputs, first_pre, middle, second_pre, features)


def trunk_backward(
    feature_grad, inputs, first_pre, middle, second_pre, second_weight, second_index
):
    row_count, blocks, tile_size = first_pre.shape
    second_dz = (
        feature_grad.reshape(row_count, blocks, tile_size) * silu_slope(second_pre)
    ).astype(jnp.bfloat16)
    second_grad = jnp.einsum("rot,roi->oti", middle, second_dz, preferred_element_type=jnp.float32)
    second_bias_grad = jnp.sum(second_dz, axis=0, dtype=jnp.float32).reshape(-1)
    spread = jnp.einsum(
        "roi,oti->rot", second_dz, second_weight, preferred_element_type=jnp.float32
    )
    onehot = (second_index[:, None] == jnp.arange(blocks, dtype=jnp.int32)[None, :]).astype(
        jnp.float32
    )
    first_act_grad = jnp.einsum("rot,op->rpt", spread, onehot, precision=lax.Precision.HIGHEST)
    first_dz = (first_act_grad * silu_slope(first_pre)).astype(jnp.bfloat16)
    first_grad = jnp.einsum("rot,roi->oti", inputs, first_dz, preferred_element_type=jnp.float32)
    first_bias_grad = jnp.sum(first_dz, axis=0, dtype=jnp.float32).reshape(-1)
    return (first_grad, first_bias_grad, second_grad, second_bias_grad)


def body(
    covariates,
    first_weight,
    first_bias,
    first_index,
    second_weight,
    second_bias,
    second_index,
    head_weight,
    clade_block,
    presence,
):
    inputs, first_pre, middle, second_pre, own_features = trunk_forward(
        covariates, first_weight, first_bias, first_index, second_weight, second_bias, second_index
    )
    features = lax.all_gather(own_features, "sp", axis=0, tiled=True)
    cell_count = features.shape[0]
    feature_width = features.shape[1]
    block_count = head_weight.shape[0]
    slab_width = head_weight.shape[1]
    block_species = head_weight.shape[2]
    records = presence.shape[1]
    first_cell = lax.axis_index("bg") * cell_count
    local_presence = presence - first_cell
    row_ids = jnp.arange(cell_count, dtype=jnp.int32)
    block_ids = jnp.arange(block_count, dtype=jnp.int32)

    def logits_of(block):
        feature_slab = lax.dynamic_slice_in_dim(
            features, clade_block[block] * slab_width, slab_width, 1
        )
        return (
            feature_slab,
            jnp.dot(feature_slab, head_weight[block], preferred_element_type=jnp.float32),
        )

    def hits_of(block):
        block_records = lax.dynamic_slice_in_dim(
            local_presence, block * block_species, block_species, 0
        )
        return jnp.sum(
            row_ids[:, None, None] == block_records[None, :, :], axis=2, dtype=jnp.float32
        )

    def max_look(block):
        feature_slab, logits = logits_of(block)
        return (jnp.max(logits, axis=0), jnp.sum(hits_of(block) * logits, axis=0))

    local_high, local_hits = lax.map(max_look, block_ids)
    highest = lax.pmax(local_high, "bg")

    def sum_look(block):
        feature_slab, logits = logits_of(block)
        return jnp.sum(jnp.exp(logits - highest[block][None, :]), axis=0)

    local_sum = lax.map(sum_look, block_ids)
    partition, presence_sum = lax.psum((local_sum, local_hits), "bg")
    total_cells = cell_count * lax.axis_size("bg")
    species_loss = (
        highest + jnp.log(partition) - math.log(total_cells) - presence_sum / records
    ).reshape(-1)
    inverse = 1.0 / partition

    def grad_step(accumulated, block):
        feature_slab, logits = logits_of(block)
        weight_cells = (
            jnp.exp(logits - highest[block][None, :]) * inverse[block][None, :]
            - hits_of(block) / records
        ).astype(jnp.bfloat16)
        block_grad = jnp.einsum(
            "cf,cs->fs", feature_slab, weight_cells, preferred_element_type=jnp.float32
        )
        feature_back = jnp.einsum(
            "cs,fs->cf", weight_cells, head_weight[block], preferred_element_type=jnp.float32
        )
        column_start = clade_block[block] * slab_width
        current = lax.dynamic_slice_in_dim(accumulated, column_start, slab_width, 1)
        accumulated = lax.dynamic_update_slice_in_dim(
            accumulated, current + feature_back, column_start, 1
        )
        return (accumulated, block_grad)

    group_back, head_terms = lax.scan(
        grad_step, jnp.zeros((cell_count, feature_width), jnp.float32), block_ids
    )
    head_grad = lax.psum(head_terms, "bg")
    feature_grad = lax.psum_scatter(
        group_back.astype(jnp.bfloat16), "sp", scatter_dimension=0, tiled=True
    ).astype(jnp.float32)
    first_grad, first_bias_grad, second_grad, second_bias_grad = trunk_backward(
        feature_grad, inputs, first_pre, middle, second_pre, second_weight, second_index
    )
    first_grad, first_bias_grad, second_grad, second_bias_grad = lax.psum(
        (first_grad, first_bias_grad, second_grad, second_bias_grad), ("bg", "sp")
    )
    return (species_loss, head_grad, first_grad, first_bias_grad, second_grad, second_bias_grad)


def solution(mesh):
    placed = (
        P(("bg", "sp"), None),
        P(),
        P(),
        P(),
        P(),
        P(),
        P(),
        P("sp", None, None),
        P("sp"),
        P("sp", None),
    )
    return jax.shard_map(
        body,
        mesh=mesh,
        in_specs=placed,
        out_specs=(P("sp"), P("sp", None, None), P(), P(), P(), P()),
        check_vma=False,
    )
```

profile of v0, /device:TPU:1, one launch (start us, length us, event | category | flops | bytes accessed | tf_op | source)
XLA Modules:
  0.0 1961.2 jit_solution(6626273520599481264)
XLA Ops:
  11.6 2.1 multiply_convert_fusion.2
  14.4 1.1 multiply_convert_fusion.1
  16.5 35.8 %all-gather.2.cloned.1.call-done = bf16[512,1024]{0,1:T(8,128)(2,1)} async-done(((bf16[128,1024]{0,1:T(8,128)(2,1)}), bf16[512,1024]{0,1:T(8,128)(2,1)}) %all-gather.2.cloned.1.call-update) | async-done | bytes 1048592 | tf_op jit(solution)/shard_map/all_gather | solution.py:70
  52.3 1.5 copy.70
  53.9 132.0 %while.37 = (s32[]{:T(128)}, f32[20,128]{1,0:T(8,128)S(1)}, f32[20,128]{1,0:T(8,128)S(1)}, s32[20]{0:T(128)S(1)}, s32[20]{0:T(128)S(1)}, /*index=5*/bf16[512,102...) while((s32[]{:T(128)}, f32[20,128]{1,0:T(8,128)S(1)}, ...), condition=%wide.region_4.5_spmd.clone, body=%wide.region_0.4_spmd.clone.sunk | while | flops 12713741 | bytes 699711 | solution.py:103
  58.3 1.1 convert_reduce_fusion.6
  64.9 1.1 convert_reduce_fusion.6
  71.5 1.1 convert_reduce_fusion.6
  78.1 1.1 convert_reduce_fusion.6
  84.7 1.1 convert_reduce_fusion.6
  91.3 1.1 convert_reduce_fusion.6
  117.7 1.1 convert_reduce_fusion.6
  144.2 1.1 convert_reduce_fusion.6
  170.6 1.1 convert_reduce_fusion.6
  185.9 491.5 %pmax.7 = f32[20,128]{1,0:T(8,128)S(1)} all-reduce(f32[20,128]{1,0:T(8,128)S(1)} %get-tuple-element.149), channel_id=1, replica_groups=mesh['bg'=128,'sp'=4] {'bg'}, use_global_device_ids=true, to_apply=%region_5.6 | all-reduce | flops 2560 | bytes 20480 | tf_op jit(solution)/shard_map/pmax | solution.py:104
  677.5 97.0 %while.36 = (s32[]{:T(128)}, f32[20,128]{1,0:T(8,128)S(1)}, s32[20]{0:T(128)S(1)}, s32[20]{0:T(128)S(1)}, bf16[512,1024]{1,0:T(8,128)(2,1)S(1)}, /*index=5*/bf16...) while((s32[]{:T(128)}, f32[20,128]{1,0:T(8,128)S(1)}, ...), condition=%wide.region_8.9_spmd, body=%wide.region_6.8_spmd.sunk | while | flops 8519561 | bytes 150773 | solution.py:110
  774.5 490.9 %all-reduce.2 = (f32[20,128]{1,0:T(8,128)S(1)}, f32[20,128]{1,0:T(8,128)S(1)}) all-reduce(f32[20,128]{1,0:T(8,128)S(1)} %get-tuple-element.151, f32[20,128]{1,0:T(8,128)S(1)} %get-tuple-element.150), channel_id=1, replica_groups=mesh['bg'=128,'sp'=4] {'bg'}, use_global_device_ids=true, to_apply=%region_10.11 | all-reduce | flops 5120 | bytes 40960 | tf_op jit(solution)/shard_map/psum | solution.py:111
  1266.3 180.6 %while.38 = (s32[]{:T(128)}, f32[512,1024]{0,1:T(8,128)S(1)}, f32[20,64,128]{2,1,0:T(8,128)}, s32[20]{0:T(128)S(1)}, s32[20]{0:T(128)S(1)}, /*index=5*/bf16[512,...) while((s32[]{:T(128)}, f32[512,1024]{0,1:T(8,128)S(1)}, ...), condition=%wide.region_13.14_spmd.clone, body=%wide.region_11.13_spmd.clone.sunk | while | flops 29655052 | bytes 1535323 | solution.py:137
  1271.5 1.1 convert_reduce_fusion.7
  1280.5 1.1 convert_reduce_fusion.7
  1289.5 1.1 convert_reduce_fusion.7
  1298.6 1.1 convert_reduce_fusion.7
  1307.6 1.1 convert_reduce_fusion.7
  1316.6 1.1 convert_reduce_fusion.7
  1325.7 1.1 convert_reduce_fusion.7
  1334.7 1.1 convert_reduce_fusion.7
  1343.7 1.1 convert_reduce_fusion.7
  1352.8 1.1 convert_reduce_fusion.7
  1361.8 1.1 convert_reduce_fusion.7
  1370.8 1.1 convert_reduce_fusion.7
  1379.8 1.1 convert_reduce_fusion.7
  1388.9 1.1 convert_reduce_fusion.7
  1397.9 1.1 convert_reduce_fusion.7
  1406.9 1.1 convert_reduce_fusion.7
  1416.0 1.1 convert_reduce_fusion.7
  1425.0 1.1 convert_reduce_fusion.7
  1434.0 1.1 convert_reduce_fusion.7
  1443.0 1.1 convert_reduce_fusion.7
  1447.1 1.3 copy.82
  1449.2 25.2 %reduce-scatter.4.cloned.1.call-done = bf16[128,1024]{1,0:T(8,128)(2,1)} async-done(((bf16[512,1024]{1,0:T(8,128)(2,1)}), bf16[128,1024]{1,0:T(8,128)(2,1)}) %reduce-scatter.4.cloned.1.call-update) | async-done | bytes 262160
  1474.4 1.1 copy.83
  1477.2 1.1 fusion.38
  1478.3 1.1 fusion.41
  1479.5 99.2 %all-reduce = (f32[1024]{0:T(1024)}, f32[1024]{0:T(1024)}) all-reduce(f32[1024]{0:T(1024)S(1)} %bitcast.121, f32[1024]{0:T(1024)S(1)} %bitcast.120), channel_id=1, replica_groups=mesh['bg'=128,'sp'=4] {'bg','sp'}, use_global_device_ids=true, to_apply=%region_18.19 | all-reduce | flops 2048 | bytes 16384 | tf_op jit(solution)/shard_map/psum | solution.py:147
  1578.7 94.6 %all-reduce.6.cloned.1.call-done = f32[20,64,128]{2,1,0:T(8,128)} async-done(((f32[20,64,128]{2,1,0:T(8,128)}), f32[20,64,128]{2,1,0:T(8,128)}) %all-reduce.6.cloned.1.call-update) | async-done | bytes 655376 | tf_op jit(solution)/shard_map/psum | solution.py:140
  1673.3 276.7 %all-reduce.8.cloned.1.call-done = (f32[8,128,128]{2,1,0:T(8,128)}, f32[8,128,128]{2,1,0:T(8,128)}) async-done(((f32[8,128,128]{2,1,0:T(8,128)}, f32[8,128,128]{2,1,0:T(8,128)}), (f32[8,128,128]{2,1,0:T(8,128)}, f32[8,128,128]{2,1,0:T(8,128)})) %all-reduce.8.cloned.1.call-update) | async-done | bytes 1048592 | tf_op jit(solution)/shard_map/psum | solution.py:147
  1950.0 2.0 copy.120
  1952.0 1.9 copy.121
  (433 shorter events, 205.2 us)
Async XLA Ops:
  7.2 7.2 copy-start
  7.2 45.2 %all-gather.2.cloned.1.call-start = ((), (), s32[]{:S(2)}) async-start(), calls=%async_computation.1 | async-start | bytes 1310720 | tf_op jit(solution)/shard_map/all_gather | solution.py:70
  11.0 3.4 copy-start.11
  11.6 3.9 copy-start.1
  13.8 2.7 copy-start.9
  14.4 2.1 copy-start.3
  15.5 38.4 %copy-start.12 = (s32[20]{0:T(128)S(1)}, s32[20]{0:T(128)}, u32[]{:S(2)}) copy-start(s32[20]{0:T(128)} %param.24) | copy-start | bytes 244
  16.4 1458.0 %reduce-scatter.4.cloned.1.call-start = ((), (), s32[]{:S(2)}) async-start(), calls=%async_computation.3 | async-start | bytes 1310720
  185.9 1080.1 %copy-start.8 = (s32[2560,16]{0,1:T(8,128)}, s32[2560,16]{0,1:T(8,128)S(1)}, u32[]{:S(2)}) copy-start(s32[2560,16]{0,1:T(8,128)S(1)} %get-tuple-element.686) | copy-start | bytes 491524
  1447.1 28.6 %copy-start.6 = (f32[128,8,128]{2,0,1:T(8,128)S(1)}, f32[128,8,128]{2,0,1:T(8,128)}, u32[]{:S(2)}) copy-start(f32[128,8,128]{2,0,1:T(8,128)} %get-tuple-element.363) | copy-start | bytes 1572868
  1448.4 224.8 %all-reduce.6.cloned.1.call-start = ((), (), s32[]{:S(2)}) async-start(), calls=%async_computation.2 | async-start | bytes 1310720 | tf_op jit(solution)/shard_map/psum | solution.py:140
  1448.5 27.8 %copy-start.10 = (s32[8]{0:T(128)S(1)}, s32[8]{0:T(128)}, u32[]{:S(2)}) copy-start(s32[8]{0:T(128)} %param.22) | copy-start | bytes 100
  1449.2 500.8 %all-reduce.8.cloned.1.call-start = ((), (), s32[]{:S(2)}) async-start(), calls=%async_computation.4 | async-start | bytes 2097152 | tf_op jit(solution)/shard_map/psum | solution.py:147
  1475.5 1.4 copy-start.5
  1475.7 1.5 copy-start.4
  1475.9 2.4 copy-start.2
  1949.9 3.9 copy-start.7
Sparse Core Ops, SparseCore 0:
  16.5 35.7 all-gather.1
  1448.5 25.7 reduce-scatter.3
  1478.6 194.6 all-reduce.5
  1679.8 270.0 all-reduce.7
where the time goes:
time: 1970 us; the launch traced here: 1960 us
  blocking collectives  1080 us (55%)
  waiting for transfers between devices  433 us (22%)
  loops' own time  184 us (9%)
  matrix products  102 us (5%)
  local copies, waits for them, and re-layouts  99.6 us (5%)
  other arithmetic  46.5 us (2%)
    pmax x1, blocking collectives, body(): highest = lax.pmax(local_high, 'bg')  492 us
    psum x1, blocking collectives, body(): partition, presence_sum = lax.psum((local_sum, local_hits), 'bg')  491 us
    psum x1, waiting for transfers between devices, body(): lax.psum((first_grad, first_bias_grad, second_grad, second_bias_grad), ('...  277 us
    psum x1, blocking collectives, body(): lax.psum((first_grad, first_bias_grad, second_grad, second_bias_grad), ('...  99.2 us
    psum x1, waiting for transfers between devices, body(): head_grad = lax.psum(head_terms, 'bg')  94.6 us
    another operation x1, loops' own time, body(): lax.scan(grad_step, jnp.zeros((cell_count, feature_width), jnp.float32),...  65.7 us
    another operation x1, loops' own time, body(): local_high, local_hits = lax.map(max_look, block_ids)  65.6 us
    dot_general x60, matrix products, logits_of(): jnp.dot(feature_slab, head_weight[block], preferred_element_type=jnp.floa...  60 us
  transfers between devices with their start and end apart: 4, of which 4 were waited for; matrix products, arithmetic and copies ran while one was open for 0% of the time, Pallas kernels for 0%

commit v1 on v0

v1 whole, which is shorter than its diff:
```python
import math

import jax
import jax.numpy as jnp
from jax import lax
from jax.experimental import pallas as pl
from jax.experimental.pallas import tpu as pltpu
from jax.sharding import Mesh, PartitionSpec as P

BF16 = jnp.bfloat16
F32 = jnp.float32
CHUNK = 128
LINK = BF16
VMEM = pl.BlockSpec(memory_space=pltpu.VMEM)
SMEM = pl.BlockSpec(memory_space=pltpu.SMEM)
PARAMS = pltpu.CompilerParams(vmem_limit_bytes=56 << 20)


def dot(a, b):
    return jnp.dot(a, b, preferred_element_type=F32)


def dot_t(a, b):
    return lax.dot_general(a, b, (((1,), (1,)), ((), ())), preferred_element_type=F32)


def hits_of(presence_ref, lanes, first_row):
    rows = first_row + lax.broadcasted_iota(jnp.int32, (CHUNK, lanes.size), 0)
    hits = jnp.zeros((CHUNK, lanes.size), F32)
    for record in range(presence_ref.shape[0]):
        hits += jnp.where(rows == presence_ref[record : record + 1, lanes], 1.0, 0.0)
    return hits


def forward_kernel(
    first_index,
    second_index,
    clade,
    busy,
    place,
    covariates,
    first_weight,
    first_bias,
    second_weight,
    second_bias,
    head_weight,
    presence,
    shifted,
    high,
    local_lse,
    hit_sum,
    features,
    first_act,
    first_slope,
    second_slope,
    wide_weight,
    logits,
):
    blocks, cells, tile = features.shape
    block_count, slab, _ = head_weight.shape
    first_cell = place[0]

    def layer(pre, act_ref, slope_ref, o):
        sigma = 1.0 / (1.0 + jnp.exp(-pre))
        act_ref[o] = (pre * sigma).astype(BF16)
        slope_ref[o] = sigma * (1.0 + pre * (1.0 - sigma))

    for o in range(blocks):
        columns = pl.ds(pl.multiple_of(first_index[o] * tile, tile), tile)
        pre = dot(covariates[:, columns], first_weight[o]) + first_bias[o : o + 1, :]
        layer(pre, first_act, first_slope, o)
    for o in range(blocks):
        pre = dot(first_act[second_index[o]], second_weight[o]) + second_bias[o : o + 1, :]
        layer(pre, features, second_slope, o)

    hit_sum[...] = jnp.zeros_like(hit_sum)
    wide_weight[...] = jnp.zeros_like(wide_weight)

    def step(b, carry):
        spot = clade[b]
        half = pl.ds(pl.multiple_of((spot % 2) * slab, slab), slab)
        lanes = pl.ds(pl.multiple_of(b * tile, tile), tile)
        row = pl.ds(b, 1)
        wide_weight[b, half, :] = head_weight[b]
        logits[...] = dot(features[spot // 2], wide_weight[b])
        top = jnp.max(logits[...], axis=0, keepdims=True)
        terms = jnp.exp(logits[...] - top)
        shifted[b] = terms
        high[row, :] = top
        local_lse[row, :] = top + jnp.log(jnp.sum(terms, axis=0, keepdims=True))
        for k in range(cells // CHUNK):

            @pl.when(busy[b * (cells // CHUNK) + k] > 0)
            def _():
                hits = hits_of(presence, lanes, first_cell + k * CHUNK)
                part = hits * logits[k * CHUNK : (k + 1) * CHUNK, :]
                hit_sum[row, :] += jnp.sum(part, axis=0, keepdims=True)

        return carry

    lax.fori_loop(0, block_count, step, 0)


def backward_kernel(
    first_index,
    second_index,
    clade,
    busy,
    place,
    covariates,
    second_weight,
    presence,
    shifted,
    high,
    lse,
    hit_sum,
    features,
    first_act,
    first_slope,
    second_slope,
    wide_weight,
    keep,
    send,
    packed,
    features_t,
    first_act_t,
    covariates_t,
    weight_cells,
    slab_grad,
    group_back,
    act_grad,
):
    blocks, cells, tile = features.shape
    block_count = wide_weight.shape[0]
    slab = tile // 2
    records = presence.shape[0]
    first_cell = place[0]
    parts = packed.shape[0]
    head_rows = block_count * slab // parts
    piece = math.gcd(slab, head_rows)

    for o in range(blocks):
        features_t[o] = features[o].T
        first_act_t[o] = first_act[o].T
    for o in range(covariates.shape[1] // tile):
        covariates_t[o] = covariates[:, o * tile : (o + 1) * tile].T
    group_back[...] = jnp.zeros_like(group_back)
    act_grad[...] = jnp.zeros_like(act_grad)

    def step(b, carry):
        spot = clade[b]
        lanes = pl.ds(pl.multiple_of(b * tile, tile), tile)
        row = pl.ds(b, 1)
        scale = jnp.exp(high[row, :] - lse[row, :])
        weight_cells[...] = (shifted[b] * scale).astype(BF16)
        for k in range(cells // CHUNK):

            @pl.when(busy[b * (cells // CHUNK) + k] > 0)
            def _():
                hits = hits_of(presence, lanes, first_cell + k * CHUNK)
                rows = slice(k * CHUNK, (k + 1) * CHUNK)
                weights = shifted[b, rows, :] * scale - hits * (1.0 / records)
                weight_cells[rows, :] = weights.astype(BF16)

        slab_grad[...] = dot(features_t[spot // 2], weight_cells[...])
        for j in range(slab // piece):
            q = b * (slab // piece) + j
            source = pl.ds(pl.multiple_of((spot % 2) * slab + j * piece, piece), piece)
            target = pl.ds(pl.multiple_of(tile + (q % (head_rows // piece)) * piece, piece), piece)
            packed[q // (head_rows // piece), target, :] = slab_grad[source, :]
        group_back[spot // 2] += dot_t(weight_cells[...], wide_weight[b])
        return carry

    lax.fori_loop(0, block_count, step, 0)

    bias_row = tile + head_rows
    packed[:, bias_row:, :] = jnp.zeros((parts, packed.shape[1] - bias_row, tile), F32)
    for o in range(blocks):
        dz = (group_back[o] * second_slope[o]).astype(BF16)
        packed[blocks + o, :tile, :] = dot(first_act_t[second_index[o]], dz)
        packed[blocks + o, bias_row : bias_row + 1, :] = jnp.sum(
            dz.astype(F32), axis=0, keepdims=True
        )
        act_grad[second_index[o]] += dot_t(dz, second_weight[o])
    for o in range(blocks):
        dz = (act_grad[o] * first_slope[o]).astype(BF16)
        packed[o, :tile, :] = dot(covariates_t[first_index[o]], dz)
        packed[o, bias_row : bias_row + 1, :] = jnp.sum(dz.astype(F32), axis=0, keepdims=True)
    for b in range(block_count):
        spot = bias_row + 1 + b % 2
        packed[b // 2, spot : spot + 1, :] = hit_sum[b : b + 1, :]

    core = place[1]
    for o in range(blocks):
        keep[o] = packed[core * blocks + o]
        send[o] = packed[(1 - core) * blocks + o]


def spread(value, axis, size):
    return lax.all_to_all(jnp.broadcast_to(value[None], (size, *value.shape)), axis, 0, 0)


def join(parts):
    top = jnp.max(parts, axis=0)
    return top + jnp.log(jnp.sum(jnp.exp(parts - top), axis=0))


def body(
    covariates,
    first_weight,
    first_bias,
    first_index,
    second_weight,
    second_bias,
    second_index,
    head_weight,
    clade_block,
    presence,
):
    ny, nz, nx = lax.axis_size("y"), lax.axis_size("z"), lax.axis_size("x")
    core, mine = lax.axis_index("c"), lax.axis_index("x")
    swap = [(0, 1), (1, 0)]
    blocks, tile, _ = first_weight.shape
    block_count, slab, species = head_weight.shape
    records = presence.shape[1]
    own_cells, width = covariates.shape
    cells = own_cells * nx
    first_cell = ((lax.axis_index("y") * nz + lax.axis_index("z")) * 2 + core) * cells
    total_cells = ny * nz * 2 * cells

    presence_t = presence.T
    chunk_of = lax.shift_right_arithmetic(presence_t - first_cell, int(math.log2(CHUNK)))
    chunk_of = chunk_of.reshape(records, block_count, species)
    busy = jnp.stack(
        [jnp.any(chunk_of == k, axis=(0, 2)) for k in range(cells // CHUNK)], axis=1
    )
    busy = busy.astype(jnp.int32).reshape(-1)
    place = jnp.stack([first_cell, core]).astype(jnp.int32)
    scalars = (first_index, second_index, clade_block, busy, place)

    all_covariates = spread(covariates, "x", nx).reshape(cells, width)
    by_block = (blocks, cells, tile)
    shape = jax.ShapeDtypeStruct
    shifted, high, local_lse, hit_sum, features, first_act, first_slope, second_slope, wide = (
        pl.pallas_call(
            forward_kernel,
            name="forward",
            out_shape=(
                shape((block_count, cells, species), F32),
                shape((block_count, species), F32),
                shape((block_count, species), F32),
                shape((block_count, species), F32),
                shape(by_block, BF16),
                shape(by_block, BF16),
                shape(by_block, F32),
                shape(by_block, F32),
                shape((block_count, tile, species), BF16),
            ),
            in_specs=[SMEM] * 5 + [VMEM] * 7,
            out_specs=[VMEM] * 9,
            scratch_shapes=[pltpu.VMEM((cells, species), F32)],
            compiler_params=PARAMS,
        )(
            *scalars,
            all_covariates,
            first_weight,
            first_bias.reshape(blocks, tile),
            second_weight,
            second_bias.reshape(blocks, tile),
            head_weight,
            presence_t,
        )
    )

    lse = join(jnp.stack([local_lse, lax.ppermute(local_lse, "c", swap)]))
    lse = join(spread(lse, "y", ny))
    lse = join(spread(lse, "z", nz))

    parts = 2 * ny
    head_rows = block_count * slab // parts
    part_rows = -(-(tile + head_rows + 3) // 8) * 8
    keep, send = pl.pallas_call(
        backward_kernel,
        name="backward",
        out_shape=(
            shape((ny, part_rows, tile), F32),
            shape((ny, part_rows, tile), F32),
        ),
        in_specs=[SMEM] * 5 + [VMEM] * 12,
        out_specs=[VMEM] * 2,
        scratch_shapes=[
            pltpu.VMEM((parts, part_rows, tile), F32),
            pltpu.VMEM((blocks, tile, cells), BF16),
            pltpu.VMEM((blocks, tile, cells), BF16),
            pltpu.VMEM((width // tile, tile, cells), BF16),
            pltpu.VMEM((cells, species), BF16),
            pltpu.VMEM((tile, species), F32),
            pltpu.VMEM(by_block, F32),
            pltpu.VMEM(by_block, F32),
        ],
        compiler_params=PARAMS,
    )(
        *scalars,
        all_covariates,
        second_weight,
        presence_t,
        shifted,
        high,
        lse,
        hit_sum,
        features,
        first_act,
        first_slope,
        second_slope,
        wide,
    )

    total = keep + lax.ppermute(send, "c", swap)
    rounded = lax.reduce_precision(total, 8, 7)
    rest = (total - rounded)[:, tile : tile + head_rows]
    total = jnp.concatenate([rounded.astype(LINK), rest.astype(LINK)], axis=1)
    total = jnp.sum(lax.all_to_all(total, "y", 0, 0).astype(F32), axis=0)
    total_head = (total[tile : tile + head_rows] + total[part_rows:]).astype(LINK)
    total = total[:part_rows].astype(LINK)
    trunk_cut, head_cut = tile // (nz * nx), head_rows // nz
    pieces = [
        total[:tile].reshape(nz, nx, trunk_cut, tile),
        jnp.broadcast_to(
            total_head.reshape(nz, 1, head_cut, tile),
            (nz, nx, head_cut, tile),
        ),
        jnp.broadcast_to(total[tile + head_rows :], (nz, nx, part_rows - tile - head_rows, tile)),
    ]
    cut = jnp.concatenate(pieces, axis=2)
    cut_rows = -(-cut.shape[2] // 8) * 8
    cut = jnp.pad(cut, ((0, 0), (0, 0), (0, cut_rows - cut.shape[2]), (0, 0)))
    cut = lax.all_to_all(cut.reshape(nz * nx, cut_rows, tile), ("z", "x"), 0, 0)
    cut = cut.reshape(nz, nx, cut_rows, tile).astype(F32)
    over_z = jnp.sum(lax.dynamic_index_in_dim(cut, mine, 1, False), axis=0)
    over_both = jnp.sum(cut, axis=(0, 1))
    bias_row = trunk_cut + head_cut
    bias = over_both[bias_row : bias_row + 1]
    hit_part = over_z[bias_row + 1 : bias_row + 3]

    done = jnp.concatenate([over_both[:trunk_cut], over_z[trunk_cut:bias_row]])
    done = jnp.pad(done, ((0, -bias_row % 8), (0, 0))).astype(LINK)
    done = spread(done, ("z", "x"), nz * nx).reshape(nz, nx, -1, tile)
    trunk = done[:, :, :trunk_cut].reshape(tile, tile)
    head = lax.dynamic_index_in_dim(done, mine, 1, False)[:, trunk_cut:bias_row]
    rows = jnp.concatenate(
        [trunk, head.reshape(head_rows, tile), bias.astype(LINK), hit_part.astype(LINK)]
    )
    rows = jnp.pad(rows, ((0, part_rows - rows.shape[0]), (0, 0)))
    rows = spread(rows, "y", ny)
    other = lax.ppermute(rows, "c", swap)
    low = jnp.where(core == 0, rows, other).astype(F32)
    upper = jnp.where(core == 0, other, rows).astype(F32)
    both = jnp.concatenate([low, upper])
    head_grad = both[:, tile : tile + head_rows].reshape(block_count, slab, species)
    hit_total = both[:, tile + head_rows + 1 : tile + head_rows + 3].reshape(parts * 2, tile)
    hit_total = hit_total[:block_count]
    species_loss = (lse - math.log(total_cells) - hit_total / records).reshape(-1)
    return (
        species_loss,
        head_grad,
        low[:, :tile],
        low[:, tile + head_rows].reshape(-1),
        upper[:, :tile],
        upper[:, tile + head_rows].reshape(-1),
    )


def solution(mesh):
    devices = mesh.devices.reshape(8, mesh.shape["bg"] // 16, 2, mesh.shape["sp"])
    torus = Mesh(devices, ("y", "z", "c", "x"))
    placed = (
        P(("y", "z", "c", "x"), None),
        P(),
        P(),
        P(),
        P(),
        P(),
        P(),
        P("x", None, None),
        P("x"),
        P("x", None),
    )
    return jax.shard_map(
        body,
        mesh=torus,
        in_specs=placed,
        out_specs=(P("x"), P("x", None, None), P(), P(), P(), P()),
        check_vma=False,
    )
```

time: 1970 us -> 176 us (0.09)
  blocking collectives: 1080 us -> 64.2 us
  waiting for transfers between devices: 433 us -> 27.2 us
  loops' own time: 184 us -> 0 us
  matrix products: 102 us -> 0 us
  local copies, waits for them, and re-layouts: 99.6 us -> 6.76 us
  other arithmetic: 46.5 us -> 8.11 us
  Pallas kernels: 0 us -> 36.2 us
  starting transfers between devices: 0.16 us -> 31.6 us
    psum x2 -> x0, blocking collectives: 590 us -> none  [the longest x1 491 us: body(): partition, presence_sum = lax.psum((local_sum, local_hits), 'bg')]
    pmax x1 -> x0, blocking collectives: 492 us -> none  [body(): highest = lax.pmax(local_high, 'bg')]
    psum x2 -> x0, waiting for transfers between devices: 371 us -> none  [the longest x1 277 us: body(): lax.psum((first_grad, first_bias_grad, second_grad, second_bias_grad), ('...]
    another operation x3 -> x0, loops' own time: 184 us -> none  [the longest x1 65.7 us: body(): lax.scan(grad_step, jnp.zeros((cell_count, feature_width), jnp.float32),...]
    dot_general x106 -> x0, matrix products: 102 us -> none  [the longest x60 60 us: logits_of(): jnp.dot(feature_slab, head_weight[block], preferred_element_type=jnp.floa...]
    dynamic_slice x160 -> x0, local copies, waits for them, and re-layouts: 84.8 us -> none  [the longest x60 35.2 us: body(): local_high, local_hits = lax.map(max_look, block_ids)]
    all_to_all x0 -> x4, blocking collectives: none -> 64.2 us  [the longest x3 42.1 us: spread(): lax.all_to_all(jnp.broadcast_to(value[None], (size, *value.shape)), axis,...]
    reduce_sum x42 -> x6, other arithmetic: 43.1 us -> 0.92 us  [the longest x3 0.78 us: join(): return top + jnp.log(jnp.sum(jnp.exp(parts - top), axis=0))]
  transfers between devices with their start and end apart: 4 -> 6, of which waited for: 4 -> 6; matrix products, arithmetic and copies ran while one was open for 0% -> 2% of each run, Pallas kernels for 0% -> 0%
where the time goes in v1:
time: 176 us; the launch traced here: 175 us
  blocking collectives  64.2 us (36%)
  Pallas kernels  36.2 us (21%)
  starting transfers between devices  31.6 us (18%)
  waiting for transfers between devices  27.2 us (15%)
  other arithmetic  8.11 us (5%)
  local copies, waits for them, and re-layouts  6.76 us (4%)
    all_to_all x3, blocking collectives, spread(): lax.all_to_all(jnp.broadcast_to(value[None], (size, *value.shape)), axis,...  42.1 us
    all_to_all x1, blocking collectives, body(): total = jnp.sum(lax.all_to_all(total, 'y', 0, 0).astype(F32), axis=0)  22.1 us
    pallas_call x1, Pallas kernels, body(): pl.pallas_call(forward_kernel, name='forward', out_shape=(shape((block_co...  18.5 us
    pallas_call x1, Pallas kernels, body(): pl.pallas_call(backward_kernel, name='backward', out_shape=(shape((ny, pa...  17.7 us
    all_to_all x2, waiting for transfers between devices, spread(): lax.all_to_all(jnp.broadcast_to(value[None], (size, *value.shape)), axis,...  12.1 us
    all_to_all x1, waiting for transfers between devices, body(): cut = lax.all_to_all(cut.reshape(nz * nx, cut_rows, tile), ('z', 'x'), 0, 0)  10.5 us
    all_to_all x2, starting transfers between devices, spread(): lax.all_to_all(jnp.broadcast_to(value[None], (size, *value.shape)), axis,...  9.04 us
    ppermute x1, starting transfers between devices, body(): lse = join(jnp.stack([local_lse, lax.ppermute(local_lse, 'c', swap)]))  7.59 us
  transfers between devices with their start and end apart: 6, of which 6 were waited for; matrix products, arithmetic and copies ran while one was open for 2% of the time, Pallas kernels for 0%

profile of v1, /device:TPU:1, one launch (start us, length us, event | category | flops | bytes accessed | tf_op | source)
XLA Modules:
  0.0 175.0 jit_solution(1656487546244381707)
XLA Ops:
  0.6 1.6 broadcast_in_dim.16
  2.2 4.8 %all-to-all-start = ((bf16[4,128,256]{2,1,0:T(8,128)(2,1)}), bf16[4,128,256]{2,1,0:T(8,128)(2,1)S(1)}, u32[]{:S(2)}, u32[]{:S(2)}) async-start(bf16[4,128,256]{2,1,0:T(8,128)(2,1)} %broadcast_in_dim.16), calls=%async_computation | async-start | bytes 524288 | tf_op jit(solution)/shard_map/all_to_all | solution.py:200
  7.0 1.0 compare_reduce_fusion.3
  8.1 0.1 bitcast_reduce_fusion.2
  8.2 0.1 bitcast_reduce_fusion
  8.3 0.1 copy.21
  8.4 0.7 reshape.93.busy
  9.1 0.7 pad_add_fusion.place
  9.8 2.8 %all-to-all-done = bf16[4,128,256]{2,1,0:T(8,128)(2,1)S(1)} async-done(((bf16[4,128,256]{2,1,0:T(8,128)(2,1)}), bf16[4,128,256]{2,1,0:T(8,128)(2,1)S(1)}, u32[]{:S(2)}, u32[]{:S(2)}) %all-to-all-start) | async-done | bytes 262176 | tf_op jit(solution)/shard_map/all_to_all | solution.py:200
  12.6 0.0 copy-start
  12.6 0.7 copy-done
  13.3 18.5 %forward.1 = (f32[20,512,128]{2,1,0:T(8,128)}, f32[20,128]{1,0:T(8,128)}, f32[20,128]{1,0:T(8,128)}, f32[20,128]{1,0:T(8,128)}, bf16[8,512,128]{2,1,0:T(8,128)(2...) custom-call(s32[8]{0:T(128)} %first_index.3, ...), custom_call_target="tpu_custom_call" | custom-call | tf_op jit(solution)/shard_map/forward/pallas_call | solution.py:245
  31.8 7.6 %collective-permute-start = (f32[20,128]{1,0:T(8,128)}, f32[20,128]{1,0:T(8,128)S(1)}, u32[]{:S(2)}, u32[]{:S(2)}) collective-permute-start(f32[20,128]{1,0:T(8,128)} %get-tuple-element.17), channel_id=1, source_target_pairs={{0,4},{4,0},{1,5},{5,1},{2,6},{6,2},{3,7},{7,3},{8,12},{12,8},{9,1... | collective-permute-start | bytes 30728 | tf_op jit(solution)/shard_map/ppermute | solution.py:275
  39.4 1.0 collective-permute-done
  40.4 0.7 reduce_max.28
  41.1 0.7 fusion.15
  41.8 9.8 %all_to_all.35 = f32[8,20,128]{2,1,0:T(8,128)S(1)} all-to-all(f32[8,20,128]{2,1,0:T(8,128)S(1)} %broadcast_in_dim.17), channel_id=1, replica_groups=mesh['y'=8,'z'=8,'c'=2,'x'=4] {'y'}, dimensions={0} | all-to-all | bytes 163840 | tf_op jit(solution)/shard_map/all_to_all | solution.py:200
  51.8 17.8 %all_to_all.36 = f32[8,20,128]{2,1,0:T(8,128)S(1)} all-to-all(f32[8,20,128]{2,1,0:T(8,128)S(1)} %broadcast_in_dim.18), channel_id=1, replica_groups=mesh['y'=8,'z'=8,'c'=2,'x'=4] {'z'}, dimensions={0} | all-to-all | bytes 163840 | tf_op jit(solution)/shard_map/all_to_all | solution.py:200
  69.6 0.6 log_add_fusion.lse
  70.2 17.7 %backward.1 = (f32[8,216,128]{2,1,0:T(8,128)}, f32[8,216,128]{2,1,0:T(8,128)}) custom-call(s32[8]{0:T(128)} %first_index.3, s32[8]{0:T(128)} %second_index.3, s32[20]{0:T(128)} %clade.3, s32[80]{0:T(128)} %reshape.93.busy, s32[2]{0:T(128)} %pad_add_fusion.place, bf16[512,256]{1,0:T(8,128)(2,1)} %bitcast.40, bf16[8,128,128]{2,1,0:T(8,128)(2,1)} %second_weight.3, ...), custom_call_target="tpu_custom_call" | custom-call | tf_op jit(solution)/shard_map/backward/pallas_call | solution.py:282
  87.9 4.5 %collective-permute-start.1 = (f32[8,216,128]{2,1,0:T(8,128)}, f32[8,216,128]{2,1,0:T(8,128)S(1)}, u32[]{:S(2)}, u32[]{:S(2)}) collective-permute-start(f32[8,216,128]{2,1,0:T(8,128)} %get-tuple-element.27), channel_id=1, source_target_pairs={{0,4},{4,0},{1,5},{5,1},{2,6},{6,2},{3,7},{7,3},{8,12},{12,8},{9,1... | collective-permute-start | bytes 2654216 | tf_op jit(solution)/shard_map/ppermute | solution.py:318
  92.4 2.2 %collective-permute-done.1 = f32[8,216,128]{2,1,0:T(8,128)S(1)} collective-permute-done((f32[8,216,128]{2,1,0:T(8,128)}, f32[8,216,128]{2,1,0:T(8,128)S(1)}, u32[]{:S(2)}, u32[]{:S(2)}) %collective-permute-start.1) | collective-permute-done | bytes 884768 | tf_op jit(solution)/shard_map/ppermute | solution.py:318
  94.6 1.3 reduce-precision_convert_fusion
  95.9 0.1 reduce_precision.3
  96.1 22.1 %all_to_all.37 = bf16[8,296,128]{2,1,0:T(8,128)(2,1)S(1)} all-to-all(bf16[8,296,128]{2,1,0:T(8,128)(2,1)S(1)} %pad_maximum_fusion.1), channel_id=1, replica_groups=mesh['y'=8,'z'=8,'c'=2,'x'=4] {'y'}, dimensions={0} | all-to-all | bytes 1212416 | tf_op jit(solution)/shard_map/all_to_all | solution.py:322
  118.2 0.1 convert_reduce_fusion
  118.4 0.8 fusion.5
  119.2 3.9 %all-to-all-start.4 = ((bf16[32,24,128]{2,1,0:T(8,128)(2,1)}), bf16[32,24,128]{2,1,0:T(8,128)(2,1)S(1)}, u32[]{:S(2)}, u32[]{:S(2)}) async-start(bf16[32,24,128]{2,1,0:T(8,128)(2,1)} %bitcast.18), calls=%async_computation.4 | async-start | bytes 393216 | tf_op jit(solution)/shard_map/all_to_all | solution.py:337
  123.1 10.5 %all-to-all-done.4 = bf16[32,24,128]{2,1,0:T(8,128)(2,1)S(1)} async-done(((bf16[32,24,128]{2,1,0:T(8,128)(2,1)}), bf16[32,24,128]{2,1,0:T(8,128)(2,1)S(1)}, u32[]{:S(2)}, u32[]{:S(2)}) %all-to-all-start.4) | async-done | bytes 196640 | tf_op jit(solution)/shard_map/all_to_all | solution.py:337
  133.7 0.7 broadcast_in_dim.22
  134.4 4.2 %all-to-all-start.5 = ((bf16[32,16,128]{2,1,0:T(8,128)(2,1)}), bf16[32,16,128]{2,1,0:T(8,128)(2,1)S(1)}, u32[]{:S(2)}, u32[]{:S(2)}) async-start(bf16[32,16,128]{2,1,0:T(8,128)(2,1)} %broadcast_in_dim.22), calls=%async_computation.5 | async-start | bytes 262144 | tf_op jit(solution)/shard_map/all_to_all | solution.py:200
  138.6 9.3 %all-to-all-done.5 = bf16[32,16,128]{2,1,0:T(8,128)(2,1)S(1)} async-done(((bf16[32,16,128]{2,1,0:T(8,128)(2,1)}), bf16[32,16,128]{2,1,0:T(8,128)(2,1)S(1)}, u32[]{:S(2)}, u32[]{:S(2)}) %all-to-all-start.5) | async-done | bytes 131104 | tf_op jit(solution)/shard_map/all_to_all | solution.py:200
  148.0 0.1 broadcast_in_dim.23
  148.1 14.4 %all_to_all.38 = bf16[8,216,128]{2,1,0:T(8,128)(2,1)S(1)} all-to-all(bf16[8,216,128]{2,1,0:T(8,128)(2,1)S(1)} %broadcast_in_dim.23), channel_id=1, replica_groups=mesh['y'=8,'z'=8,'c'=2,'x'=4] {'y'}, dimensions={0} | all-to-all | bytes 884736 | tf_op jit(solution)/shard_map/all_to_all | solution.py:200
  162.5 6.5 %collective-permute-start.2 = (bf16[8,216,128]{2,1,0:T(8,128)(2,1)S(1)}, bf16[8,216,128]{2,1,0:T(8,128)(2,1)S(1)}, u32[]{:S(2)}, u32[]{:S(2)}) collective-permute-start(bf16[8,216,128]{2,1,0:T(8,128)(2,1)S(1)} %all_to_all.38), channel_id=1, source_target_pairs={{0,4},{4,0},{1,5},{5,1},{2,6},{6,2},{3,7},{7,3},{8,12},{12,8},{9,1... | collective-permute-start | bytes 1327112 | tf_op jit(solution)/shard_map/ppermute | solution.py:355
  169.1 1.4 collective-permute-done.2
  170.5 0.1 select_convert_fusion.1
  170.6 0.6 slice.93
  171.2 0.6 slice.95
  171.8 0.8 slice.92
  172.6 0.0 copy-start.1
  172.6 0.9 pad_maximum_fusion
  173.5 0.8 slice.94
  174.3 0.0 copy-done.1
  174.4 0.6 bitcast_subtract_fusion
  (32 shorter events, 0.4 us)
Async XLA Ops:
  2.2 10.4 %all-to-all-start = ((bf16[4,128,256]{2,1,0:T(8,128)(2,1)}), bf16[4,128,256]{2,1,0:T(8,128)(2,1)S(1)}, u32[]{:S(2)}, u32[]{:S(2)}) async-start(bf16[4,128,256]{2,1,0:T(8,128)(2,1)} %broadcast_in_dim.16), calls=%async_computation | async-start | bytes 524288 | tf_op jit(solution)/shard_map/all_to_all | solution.py:200
  12.6 0.7 copy-start
  31.8 8.6 %collective-permute-start = (f32[20,128]{1,0:T(8,128)}, f32[20,128]{1,0:T(8,128)S(1)}, u32[]{:S(2)}, u32[]{:S(2)}) collective-permute-start(f32[20,128]{1,0:T(8,128)} %get-tuple-element.17), channel_id=1, source_target_pairs={{0,4},{4,0},{1,5},{5,1},{2,6},{6,2},{3,7},{7,3},{8,12},{12,8},{9,1... | collective-permute-start | bytes 30728 | tf_op jit(solution)/shard_map/ppermute | solution.py:275
  87.9 6.8 %collective-permute-start.1 = (f32[8,216,128]{2,1,0:T(8,128)}, f32[8,216,128]{2,1,0:T(8,128)S(1)}, u32[]{:S(2)}, u32[]{:S(2)}) collective-permute-start(f32[8,216,128]{2,1,0:T(8,128)} %get-tuple-element.27), channel_id=1, source_target_pairs={{0,4},{4,0},{1,5},{5,1},{2,6},{6,2},{3,7},{7,3},{8,12},{12,8},{9,1... | collective-permute-start | bytes 2654216 | tf_op jit(solution)/shard_map/ppermute | solution.py:318
  119.2 14.4 %all-to-all-start.4 = ((bf16[32,24,128]{2,1,0:T(8,128)(2,1)}), bf16[32,24,128]{2,1,0:T(8,128)(2,1)S(1)}, u32[]{:S(2)}, u32[]{:S(2)}) async-start(bf16[32,24,128]{2,1,0:T(8,128)(2,1)} %bitcast.18), calls=%async_computation.4 | async-start | bytes 393216 | tf_op jit(solution)/shard_map/all_to_all | solution.py:337
  134.4 13.6 %all-to-all-start.5 = ((bf16[32,16,128]{2,1,0:T(8,128)(2,1)}), bf16[32,16,128]{2,1,0:T(8,128)(2,1)S(1)}, u32[]{:S(2)}, u32[]{:S(2)}) async-start(bf16[32,16,128]{2,1,0:T(8,128)(2,1)} %broadcast_in_dim.22), calls=%async_computation.5 | async-start | bytes 262144 | tf_op jit(solution)/shard_map/all_to_all | solution.py:200
  162.5 7.9 %collective-permute-start.2 = (bf16[8,216,128]{2,1,0:T(8,128)(2,1)S(1)}, bf16[8,216,128]{2,1,0:T(8,128)(2,1)S(1)}, u32[]{:S(2)}, u32[]{:S(2)}) collective-permute-start(bf16[8,216,128]{2,1,0:T(8,128)(2,1)S(1)} %all_to_all.38), channel_id=1, source_target_pairs={{0,4},{4,0},{1,5},{5,1},{2,6},{6,2},{3,7},{7,3},{8,12},{12,8},{9,1... | collective-permute-start | bytes 1327112 | tf_op jit(solution)/shard_map/ppermute | solution.py:355
  172.6 1.7 copy-start.1

commit v2 on v1

--- a/solution.py
+++ b/solution.py
@@ -1,3 +1,4 @@
+import functools
 import math
 
 import jax
@@ -119,9 +120,11 @@
     first_slope,
     second_slope,
     wide_weight,
+    trunk,
     keep,
     send,
     packed,
+    bias,
     features_t,
     first_act_t,
     covariates_t,
@@ -135,9 +138,8 @@
     slab = tile // 2
     records = presence.shape[0]
     first_cell = place[0]
-    parts = packed.shape[0]
-    head_rows = block_count * slab // parts
-    piece = math.gcd(slab, head_rows)
+    group = block_count // 2
+    core = place[1]
 
     for o in range(blocks):
         features_t[o] = features[o].T
@@ -163,37 +165,81 @@
                 weight_cells[rows, :] = weights.astype(BF16)
 
         slab_grad[...] = dot(features_t[spot // 2], weight_cells[...])
-        for j in range(slab // piece):
-            q = b * (slab // piece) + j
-            source = pl.ds(pl.multiple_of((spot % 2) * slab + j * piece, piece), piece)
-            target = pl.ds(pl.multiple_of(tile + (q % (head_rows // piece)) * piece, piece), piece)
-            packed[q // (head_rows // piece), target, :] = slab_grad[source, :]
+        source = pl.ds(pl.multiple_of((spot % 2) * slab, slab), slab)
+        target = pl.ds(pl.multiple_of((b % group) * slab, slab), slab)
+        packed[b // group, target, :] = slab_grad[source, :]
         group_back[spot // 2] += dot_t(weight_cells[...], wide_weight[b])
         return carry
 
     lax.fori_loop(0, block_count, step, 0)
 
-    bias_row = tile + head_rows
-    packed[:, bias_row:, :] = jnp.zeros((parts, packed.shape[1] - bias_row, tile), F32)
+    bias[...] = jnp.zeros_like(bias)
+    pair = blocks // (trunk.shape[0] // 2)
+
+    def trunk_sums(o, layer, left, dz):
+        part, at = layer * (trunk.shape[0] // 2) + o // pair, o % pair
+        trunk[part, at * tile : (at + 1) * tile, :] = dot(left, dz).astype(LINK)
+        bias[part, at : at + 1, :] = jnp.sum(dz.astype(F32), axis=0, keepdims=True)
+
     for o in range(blocks):
         dz = (group_back[o] * second_slope[o]).astype(BF16)
-        packed[blocks + o, :tile, :] = dot(first_act_t[second_index[o]], dz)
-        packed[blocks + o, bias_row : bias_row + 1, :] = jnp.sum(
-            dz.astype(F32), axis=0, keepdims=True
-        )
+        trunk_sums(o, 1, first_act_t[second_index[o]], dz)
         act_grad[second_index[o]] += dot_t(dz, second_weight[o])
     for o in range(blocks):
         dz = (act_grad[o] * first_slope[o]).astype(BF16)
-        packed[o, :tile, :] = dot(covariates_t[first_index[o]], dz)
-        packed[o, bias_row : bias_row + 1, :] = jnp.sum(dz.astype(F32), axis=0, keepdims=True)
+        trunk_sums(o, 0, covariates_t[first_index[o]], dz)
+    for part in range(trunk.shape[0]):
+        trunk[part, pair * tile :, :] = bias[part].astype(LINK)
+
+    tail = group * slab
+    for half in range(2):
+        packed[half, tail:, :] = jnp.zeros((packed.shape[1] - tail, tile), F32)
+        packed[half, tail : tail + group, :] = hit_sum[half * group : (half + 1) * group, :]
+    keep[...] = packed[core]
+    send[...] = packed[1 - core]
+
+
+def finish_kernel(
+    total_cells,
+    records,
+    place,
+    trunk,
+    own,
+    other,
+    lse,
+    species_loss,
+    head_grad,
+    first_grad,
+    first_bias_grad,
+    second_grad,
+    second_bias_grad,
+    halves,
+):
+    core = place[1]
+    blocks, tile, _ = first_grad.shape
+    block_count, slab, _ = head_grad.shape
+    group = block_count // 2
+    halves[core] = own[...]
+    halves[1 - core] = other[...]
     for b in range(block_count):
-        spot = bias_row + 1 + b % 2
-        packed[b // 2, spot : spot + 1, :] = hit_sum[b : b + 1, :]
-
-    core = place[1]
-    for o in range(blocks):
-        keep[o] = packed[core * blocks + o]
-        send[o] = packed[(1 - core) * blocks + o]
+        rows = slice((b % group) * slab, (b % group + 1) * slab)
+        head_grad[b] = halves[b // group, rows, :].astype(F32)
+    tail = group * slab
+    for half in range(2):
+        rows = slice(half * group, (half + 1) * group)
+        hit_mean = halves[half, tail:, :].astype(F32)[:group] * (1.0 / records)
+        species_loss[rows, :] = lse[rows, :] - math.log(total_cells) - hit_mean
+    half = trunk.shape[0] // 2
+    pair = blocks // half
+    for layer, (grad, bias_grad) in enumerate(
+        ((first_grad, first_bias_grad), (second_grad, second_bias_grad))
+    ):
+        for part in range(half):
+            for at in range(pair):
+                rows = slice(at * tile, (at + 1) * tile)
+                grad[part * pair + at] = trunk[layer * half + part, rows, :].astype(F32)
+            bias = trunk[layer * half + part, pair * tile :, :].astype(F32)
+            bias_grad[part * pair : (part + 1) * pair, :] = bias[:pair]
 
 
 def spread(value, axis, size):
@@ -272,24 +318,27 @@
         )
     )
 
-    lse = join(jnp.stack([local_lse, lax.ppermute(local_lse, "c", swap)]))
-    lse = join(spread(lse, "y", ny))
-    lse = join(spread(lse, "z", nz))
-
-    parts = 2 * ny
-    head_rows = block_count * slab // parts
-    part_rows = -(-(tile + head_rows + 3) // 8) * 8
-    keep, send = pl.pallas_call(
+    lse = join(spread(local_lse, "y", ny))
+    lse = join(spread(lse, ("z", "c"), nz * 2))
+
+    pair = blocks // nx
+    part_rows = pair * tile + 8
+    group = block_count // 2
+    head_rows = group * slab
+    half_rows = head_rows + -(-group // 8) * 8
+    trunk, keep, send = pl.pallas_call(
         backward_kernel,
         name="backward",
         out_shape=(
-            shape((ny, part_rows, tile), F32),
-            shape((ny, part_rows, tile), F32),
+            shape((2 * nx, part_rows, tile), LINK),
+            shape((half_rows, tile), F32),
+            shape((half_rows, tile), F32),
         ),
         in_specs=[SMEM] * 5 + [VMEM] * 12,
-        out_specs=[VMEM] * 2,
+        out_specs=[VMEM] * 3,
         scratch_shapes=[
-            pltpu.VMEM((parts, part_rows, tile), F32),
+            pltpu.VMEM((2, half_rows, tile), F32),
+            pltpu.VMEM((2 * nx, 8, tile), F32),
             pltpu.VMEM((blocks, tile, cells), BF16),
             pltpu.VMEM((blocks, tile, cells), BF16),
             pltpu.VMEM((width // tile, tile, cells), BF16),
@@ -315,58 +364,64 @@
         wide,
     )
 
-    total = keep + lax.ppermute(send, "c", swap)
-    rounded = lax.reduce_precision(total, 8, 7)
-    rest = (total - rounded)[:, tile : tile + head_rows]
-    total = jnp.concatenate([rounded.astype(LINK), rest.astype(LINK)], axis=1)
-    total = jnp.sum(lax.all_to_all(total, "y", 0, 0).astype(F32), axis=0)
-    total_head = (total[tile : tile + head_rows] + total[part_rows:]).astype(LINK)
-    total = total[:part_rows].astype(LINK)
-    trunk_cut, head_cut = tile // (nz * nx), head_rows // nz
-    pieces = [
-        total[:tile].reshape(nz, nx, trunk_cut, tile),
-        jnp.broadcast_to(
-            total_head.reshape(nz, 1, head_cut, tile),
-            (nz, nx, head_cut, tile),
-        ),
-        jnp.broadcast_to(total[tile + head_rows :], (nz, nx, part_rows - tile - head_rows, tile)),
-    ]
-    cut = jnp.concatenate(pieces, axis=2)
-    cut_rows = -(-cut.shape[2] // 8) * 8
-    cut = jnp.pad(cut, ((0, 0), (0, 0), (0, cut_rows - cut.shape[2]), (0, 0)))
-    cut = lax.all_to_all(cut.reshape(nz * nx, cut_rows, tile), ("z", "x"), 0, 0)
-    cut = cut.reshape(nz, nx, cut_rows, tile).astype(F32)
-    over_z = jnp.sum(lax.dynamic_index_in_dim(cut, mine, 1, False), axis=0)
-    over_both = jnp.sum(cut, axis=(0, 1))
-    bias_row = trunk_cut + head_cut
-    bias = over_both[bias_row : bias_row + 1]
-    hit_part = over_z[bias_row + 1 : bias_row + 3]
-
-    done = jnp.concatenate([over_both[:trunk_cut], over_z[trunk_cut:bias_row]])
-    done = jnp.pad(done, ((0, -bias_row % 8), (0, 0))).astype(LINK)
-    done = spread(done, ("z", "x"), nz * nx).reshape(nz, nx, -1, tile)
-    trunk = done[:, :, :trunk_cut].reshape(tile, tile)
-    head = lax.dynamic_index_in_dim(done, mine, 1, False)[:, trunk_cut:bias_row]
-    rows = jnp.concatenate(
-        [trunk, head.reshape(head_rows, tile), bias.astype(LINK), hit_part.astype(LINK)]
-    )
-    rows = jnp.pad(rows, ((0, part_rows - rows.shape[0]), (0, 0)))
-    rows = spread(rows, "y", ny)
-    other = lax.ppermute(rows, "c", swap)
-    low = jnp.where(core == 0, rows, other).astype(F32)
-    upper = jnp.where(core == 0, other, rows).astype(F32)
-    both = jnp.concatenate([low, upper])
-    head_grad = both[:, tile : tile + head_rows].reshape(block_count, slab, species)
-    hit_total = both[:, tile + head_rows + 1 : tile + head_rows + 3].reshape(parts * 2, tile)
-    hit_total = hit_total[:block_count]
-    species_loss = (lse - math.log(total_cells) - hit_total / records).reshape(-1)
+    head = keep + lax.ppermute(send, "c", swap)
+    trunk = jnp.sum(lax.all_to_all(trunk, ("c", "x"), 0, 0).astype(F32), axis=0)
+    peers = ny * nz
+    misc = jnp.concatenate([head[head_rows : head_rows + group], trunk[pair * tile :][:pair]])
+    misc = jnp.pad(misc, ((0, peers - misc.shape[0]), (0, 0)))
+    trunk_cut, head_cut = pair * tile // peers, head_rows // peers
+    cut = jnp.concatenate(
+        [
+            trunk[: pair * tile].reshape(peers, trunk_cut, tile),
+            head[:head_rows].reshape(peers, head_cut, tile),
+            misc[:, None],
+        ],
+        axis=1,
+    )
+    cut = jnp.pad(cut, ((0, 0), (0, -cut.shape[1] % 8), (0, 0))).astype(LINK)
+    cut = jnp.sum(lax.all_to_all(cut, ("y", "z"), 0, 0).astype(F32), axis=0).astype(LINK)
+
+    cut = spread(cut, ("y", "z"), peers)
+    misc = cut[:, trunk_cut + head_cut]
+    head = jnp.concatenate(
+        [
+            cut[:, trunk_cut : trunk_cut + head_cut].reshape(head_rows, tile),
+            jnp.pad(misc[:group], ((0, -group % 8), (0, 0))),
+        ]
+    )
+    other_head = lax.ppermute(head, "c", swap)
+    trunk = jnp.concatenate(
+        [
+            cut[:, :trunk_cut].reshape(pair * tile, tile),
+            jnp.pad(misc[group : group + pair], ((0, -pair % 8), (0, 0))),
+        ]
+    )
+    trunk = spread(trunk, ("c", "x"), 2 * nx)
+    species_loss, head_grad, first_grad, first_bias_grad, second_grad, second_bias_grad = (
+        pl.pallas_call(
+            functools.partial(finish_kernel, total_cells, records),
+            name="finish",
+            out_shape=(
+                shape((block_count, species), F32),
+                shape(head_weight.shape, F32),
+                shape(first_weight.shape, F32),
+                shape((blocks, tile), F32),
+                shape(second_weight.shape, F32),
+                shape((blocks, tile), F32),
+            ),
+            in_specs=[SMEM] + [VMEM] * 4,
+            out_specs=[VMEM] * 6,
+            scratch_shapes=[pltpu.VMEM((2, half_rows, tile), LINK)],
+            compiler_params=PARAMS,
+        )(place, trunk, head, other_head, lse)
+    )
     return (
-        species_loss,
+        species_loss.reshape(-1),
         head_grad,
-        low[:, :tile],
-        low[:, tile + head_rows].reshape(-1),
-        upper[:, :tile],
-        upper[:, tile + head_rows].reshape(-1),
+        first_grad,
+        first_bias_grad.reshape(-1),
+        second_grad,
+        second_bias_grad.reshape(-1),
     )
 
 

time: 176 us -> 161 us (0.915)
  starting transfers between devices: 31.6 us -> 19.7 us
  blocking collectives: 64.2 us -> 74.2 us
  waiting for transfers between devices: 27.2 us -> 18.6 us
  other arithmetic: 8.11 us -> 4 us
    all_to_all x3, blocking collectives: 42.1 us -> 57.2 us  [spread(): lax.all_to_all(jnp.broadcast_to(value[None], (size, *value.shape)), axis,...]
    ppermute x3 -> x2, starting transfers between devices: 18.6 us -> 3.91 us  [the longest x1 2 us: body(): other_head = lax.ppermute(head, 'c', swap)]
    all_to_all x1, blocking collectives: 22.1 us -> 17 us  [body(): lax.all_to_all(cut, ('y', 'z'), 0, 0).astype(F32)]
    ppermute x3 -> x2, waiting for transfers between devices: 4.66 us -> 1.29 us  [the longest x1 1.29 us: body(): other_head = lax.ppermute(head, 'c', swap)]
    all_to_all x2, waiting for transfers between devices: 12.1 us -> 8.89 us  [spread(): lax.all_to_all(jnp.broadcast_to(value[None], (size, *value.shape)), axis,...]
    all_to_all x2, starting transfers between devices: 9.04 us -> 11.8 us  [spread(): lax.all_to_all(jnp.broadcast_to(value[None], (size, *value.shape)), axis,...]
    slice x12 -> x8, local copies, waits for them, and re-layouts: 2.9 us -> 0.14 us  [the longest x1 0.08 us: body(): cut[:, trunk_cut:trunk_cut + head_cut].reshape(head_rows, tile)]
    all_to_all x1, waiting for transfers between devices: 10.5 us -> 8.43 us  [body(): trunk = jnp.sum(lax.all_to_all(trunk, ('c', 'x'), 0, 0).astype(F32), axis=0)]
  transfers between devices with their start and end apart: 6 -> 5, of which waited for: 6 -> 4; matrix products, arithmetic and copies ran while one was open for 2% -> 2% of each run, Pallas kernels for 0% -> 0%
where the time goes in v2:
time: 161 us; the launch traced here: 160 us
  blocking collectives  74.2 us (46%)
  Pallas kernels  36.9 us (23%)
  starting transfers between devices  19.7 us (12%)
  waiting for transfers between devices  18.6 us (12%)
  local copies, waits for them, and re-layouts  5.75 us (4%)
  other arithmetic  4 us (2%)
    all_to_all x3, blocking collectives, spread(): lax.all_to_all(jnp.broadcast_to(value[None], (size, *value.shape)), axis,...  57.2 us
    pallas_call x1, Pallas kernels, body(): pl.pallas_call(forward_kernel, name='forward', out_shape=(shape((block_co...  17.8 us
    all_to_all x1, blocking collectives, body(): lax.all_to_all(cut, ('y', 'z'), 0, 0).astype(F32)  17 us
    pallas_call x1, Pallas kernels, body(): pl.pallas_call(backward_kernel, name='backward', out_shape=(shape((2 * nx...  16.6 us
    all_to_all x2, starting transfers between devices, spread(): lax.all_to_all(jnp.broadcast_to(value[None], (size, *value.shape)), axis,...  11.8 us
    all_to_all x2, waiting for transfers between devices, spread(): lax.all_to_all(jnp.broadcast_to(value[None], (size, *value.shape)), axis,...  8.89 us
    all_to_all x1, waiting for transfers between devices, body(): trunk = jnp.sum(lax.all_to_all(trunk, ('c', 'x'), 0, 0).astype(F32), axis=0)  8.43 us
    all_to_all x1, starting transfers between devices, body(): trunk = jnp.sum(lax.all_to_all(trunk, ('c', 'x'), 0, 0).astype(F32), axis=0)  3.97 us
  transfers between devices with their start and end apart: 5, of which 4 were waited for; matrix products, arithmetic and copies ran while one was open for 2% of the time, Pallas kernels for 0%

profile of v2, /device:TPU:1, one launch (start us, length us, event | category | flops | bytes accessed | tf_op | source)
XLA Modules:
  0.0 159.9 jit_solution(486772417373632752)
XLA Ops:
  0.6 1.6 broadcast_in_dim.13
  2.2 4.8 %all-to-all-start = ((bf16[4,128,256]{2,1,0:T(8,128)(2,1)}), bf16[4,128,256]{2,1,0:T(8,128)(2,1)S(1)}, u32[]{:S(2)}, u32[]{:S(2)}) async-start(bf16[4,128,256]{2,1,0:T(8,128)(2,1)} %broadcast_in_dim.13), calls=%async_computation | async-start | bytes 524288 | tf_op jit(solution)/shard_map/all_to_all | solution.py:246
  7.0 1.0 compare_reduce_fusion.3
  8.1 0.1 bitcast_reduce_fusion.2
  8.2 0.1 bitcast_reduce_fusion
  8.3 0.1 copy.30
  8.4 0.7 reshape.77.busy
  9.1 0.6 pad_add_fusion.place
  9.7 2.9 %all-to-all-done = bf16[4,128,256]{2,1,0:T(8,128)(2,1)S(1)} async-done(((bf16[4,128,256]{2,1,0:T(8,128)(2,1)}), bf16[4,128,256]{2,1,0:T(8,128)(2,1)S(1)}, u32[]{:S(2)}, u32[]{:S(2)}) %all-to-all-start) | async-done | bytes 262176 | tf_op jit(solution)/shard_map/all_to_all | solution.py:246
  12.6 0.0 copy-start
  12.6 0.7 copy-done
  13.3 17.8 %forward.1 = (f32[20,512,128]{2,1,0:T(8,128)}, f32[20,128]{1,0:T(8,128)}, f32[20,128]{1,0:T(8,128)}, f32[20,128]{1,0:T(8,128)}, bf16[8,512,128]{2,1,0:T(8,128)(2...) custom-call(s32[8]{0:T(128)} %first_index.3, ...), custom_call_target="tpu_custom_call" | custom-call | tf_op jit(solution)/shard_map/forward/pallas_call | solution.py:291
  31.0 0.7 broadcast_in_dim.14
  31.8 13.9 %all_to_all.35 = f32[8,20,128]{2,1,0:T(8,128)S(1)} all-to-all(f32[8,20,128]{2,1,0:T(8,128)S(1)} %broadcast_in_dim.14), channel_id=1, replica_groups=mesh['y'=8,'z'=8,'c'=2,'x'=4] {'y'}, dimensions={0} | all-to-all | bytes 163840 | tf_op jit(solution)/shard_map/all_to_all | solution.py:246
  45.7 25.4 %all_to_all.36 = f32[16,20,128]{2,1,0:T(8,128)S(1)} all-to-all(f32[16,20,128]{2,1,0:T(8,128)S(1)} %broadcast_in_dim.15), channel_id=1, replica_groups=mesh['y'=8,'z'=8,'c'=2,'x'=4] {'z','c'}, dimensions={0} | all-to-all | bytes 327680 | tf_op jit(solution)/shard_map/all_to_all | solution.py:246
  71.2 0.6 log_add_fusion.lse
  71.8 16.6 %backward.1 = (bf16[8,264,128]{2,1,0:T(8,128)(2,1)}, f32[656,128]{1,0:T(8,128)}, f32[656,128]{1,0:T(8,128)}) custom-call(s32[8]{0:T(128)} %first_index.3, s32[8]{0:T(128)} %second_index.3, s32[20]{0:T(128)} %clade.3, s32[80]{0:T(128)} %reshape.77.busy, s32[2]{0:T(128)} %pad_add_fusion.place, bf16[512,256]{1,0:T(8,128)(2,1)} %bitcast.36, ...), custom_call_target="tpu_custom_call" | custom-call | tf_op jit(solution)/shard_map/backward/pallas_call | solution.py:329
  88.5 1.9 %collective-permute-start = (f32[656,128]{1,0:T(8,128)}, f32[656,128]{1,0:T(8,128)S(1)}, u32[]{:S(2)}, u32[]{:S(2)}) collective-permute-start(f32[656,128]{1,0:T(8,128)} %get-tuple-element.35), channel_id=1, source_target_pairs={{0,4},{4,0},{1,5},{5,1},{2,6},{6,2},{3,7},{7,3},{8,12},{12,8},{9,1... | collective-permute-start | bytes 1007624 | tf_op jit(solution)/shard_map/ppermute | solution.py:367
  90.4 4.0 %all-to-all-start.3 = ((bf16[8,264,128]{2,1,0:T(8,128)(2,1)}), bf16[8,264,128]{2,1,0:T(8,128)(2,1)S(1)}, u32[]{:S(2)}, u32[]{:S(2)}) async-start(bf16[8,264,128]{2,1,0:T(8,128)(2,1)} %get-tuple-element.33), calls=%async_computation.3 | async-start | bytes 1081344 | tf_op jit(solution)/shard_map/all_to_all | solution.py:368
  94.3 0.0 collective-permute-done
  94.3 1.0 add_convert_fusion
  95.4 0.1 reshape.71
  95.5 8.4 %all-to-all-done.3 = bf16[8,264,128]{2,1,0:T(8,128)(2,1)S(1)} async-done(((bf16[8,264,128]{2,1,0:T(8,128)(2,1)}), bf16[8,264,128]{2,1,0:T(8,128)(2,1)S(1)}, u32[]{:S(2)}, u32[]{:S(2)}) %all-to-all-start.3) | async-done | bytes 540704 | tf_op jit(solution)/shard_map/all_to_all | solution.py:368
  103.9 0.1 reduce.9
  104.0 0.2 fusion.5
  104.2 17.0 %all_to_all.37 = bf16[64,16,128]{2,1,0:T(8,128)(2,1)S(1)} all-to-all(bf16[64,16,128]{2,1,0:T(8,128)(2,1)S(1)} %fusion.5), channel_id=1, replica_groups=mesh['y'=8,'z'=8,'c'=2,'x'=4] {'y','z'}, dimensions={0} | all-to-all | bytes 524288 | tf_op jit(solution)/shard_map/all_to_all | solution.py:382
  121.3 0.1 reduce_sum.42
  121.4 17.9 %all_to_all.38 = bf16[64,16,128]{2,1,0:T(8,128)(2,1)S(1)} all-to-all(bf16[64,16,128]{2,1,0:T(8,128)(2,1)S(1)} %broadcast_in_dim.17), channel_id=1, replica_groups=mesh['y'=8,'z'=8,'c'=2,'x'=4] {'y','z'}, dimensions={0} | all-to-all | bytes 524288 | tf_op jit(solution)/shard_map/all_to_all | solution.py:246
  139.3 0.9 broadcast_in_dim.18
  140.2 7.0 %all-to-all-start.6 = ((bf16[8,264,128]{2,1,0:T(8,128)(2,1)}), bf16[8,264,128]{2,1,0:T(8,128)(2,1)S(1)}, u32[]{:S(2)}, u32[]{:S(2)}) async-start(bf16[8,264,128]{2,1,0:T(8,128)(2,1)} %broadcast_in_dim.18), calls=%async_computation.6 | async-start | bytes 1081344 | tf_op jit(solution)/shard_map/all_to_all | solution.py:246
  147.2 0.1 slice.55
  147.3 0.1 reshape.73
  147.4 0.0 copy-start.2
  147.4 2.0 %collective-permute-start.1 = (bf16[656,128]{1,0:T(8,128)(2,1)S(1)}, bf16[656,128]{1,0:T(8,128)(2,1)S(1)}, u32[]{:S(2)}, u32[]{:S(2)}) collective-permute-start(bf16[656,128]{1,0:T(8,128)(2,1)S(1)} %fusion.6.own), channel_id=1, source_target_pairs={{0,4},{4,0},{1,5},{5,1},{2,6},{6,2},{3,7},{7,3},{8,12},{12,8},{9,1... | collective-permute-start | bytes 503816 | tf_op jit(solution)/shard_map/ppermute | solution.py:392
  149.4 1.3 collective-permute-done.1.other
  150.7 0.0 copy-start.3
  150.7 6.0 %all-to-all-done.6.trunk = bf16[8,264,128]{2,1,0:T(8,128)(2,1)S(1)} async-done(((bf16[8,264,128]{2,1,0:T(8,128)(2,1)}), bf16[8,264,128]{2,1,0:T(8,128)(2,1)S(1)}, u32[]{:S(2)}, u32[]{:S(2)}) %all-to-all-start.6) | async-done | bytes 540704 | tf_op jit(solution)/shard_map/all_to_all | solution.py:246
  156.7 0.0 copy-done.2
  156.7 0.0 copy-done.3
  156.7 0.0 copy-start.1
  156.7 0.8 copy-done.1
  157.5 2.4 %finish.1 = (f32[20,128]{1,0:T(8,128)}, f32[20,64,128]{2,1,0:T(8,128)}, f32[8,128,128]{2,1,0:T(8,128)}, f32[8,128]{1,0:T(8,128)}, f32[8,128,128]{2,1,0:T(8,128)}, /*index=5*/f32[8,128]{1,0:T(8,128)}) custom-call(s32[2]{0:T(128)} %pad_add_fusion.place, bf16[8,264,128]{2,1,0:T(8,128)(2,1)} %copy-done.1, bf16[656,128]{1,0:T(8,128)(2,1)} %copy-done.2, ...), custom_call_target="tpu_custom_call" | custom-call | tf_op jit(solution)/shard_map/finish/pallas_call | solution.py:401
  (21 shorter events, 0.3 us)
Async XLA Ops:
  2.2 10.4 %all-to-all-start = ((bf16[4,128,256]{2,1,0:T(8,128)(2,1)}), bf16[4,128,256]{2,1,0:T(8,128)(2,1)S(1)}, u32[]{:S(2)}, u32[]{:S(2)}) async-start(bf16[4,128,256]{2,1,0:T(8,128)(2,1)} %broadcast_in_dim.13), calls=%async_computation | async-start | bytes 524288 | tf_op jit(solution)/shard_map/all_to_all | solution.py:246
  12.6 0.7 copy-start
  88.5 5.9 %collective-permute-start = (f32[656,128]{1,0:T(8,128)}, f32[656,128]{1,0:T(8,128)S(1)}, u32[]{:S(2)}, u32[]{:S(2)}) collective-permute-start(f32[656,128]{1,0:T(8,128)} %get-tuple-element.35), channel_id=1, source_target_pairs={{0,4},{4,0},{1,5},{5,1},{2,6},{6,2},{3,7},{7,3},{8,12},{12,8},{9,1... | collective-permute-start | bytes 1007624 | tf_op jit(solution)/shard_map/ppermute | solution.py:367
  90.4 13.5 %all-to-all-start.3 = ((bf16[8,264,128]{2,1,0:T(8,128)(2,1)}), bf16[8,264,128]{2,1,0:T(8,128)(2,1)S(1)}, u32[]{:S(2)}, u32[]{:S(2)}) async-start(bf16[8,264,128]{2,1,0:T(8,128)(2,1)} %get-tuple-element.33), calls=%async_computation.3 | async-start | bytes 1081344 | tf_op jit(solution)/shard_map/all_to_all | solution.py:368
  140.2 16.5 %all-to-all-start.6 = ((bf16[8,264,128]{2,1,0:T(8,128)(2,1)}), bf16[8,264,128]{2,1,0:T(8,128)(2,1)S(1)}, u32[]{:S(2)}, u32[]{:S(2)}) async-start(bf16[8,264,128]{2,1,0:T(8,128)(2,1)} %broadcast_in_dim.18), calls=%async_computation.6 | async-start | bytes 1081344 | tf_op jit(solution)/shard_map/all_to_all | solution.py:246
  147.4 9.3 %copy-start.2 = (bf16[656,128]{1,0:T(8,128)(2,1)}, bf16[656,128]{1,0:T(8,128)(2,1)S(1)}, u32[]{:S(2)}) copy-start(bf16[656,128]{1,0:T(8,128)(2,1)S(1)} %fusion.6.own) | copy-start | bytes 503812
  147.4 3.3 %collective-permute-start.1 = (bf16[656,128]{1,0:T(8,128)(2,1)S(1)}, bf16[656,128]{1,0:T(8,128)(2,1)S(1)}, u32[]{:S(2)}, u32[]{:S(2)}) collective-permute-start(bf16[656,128]{1,0:T(8,128)(2,1)S(1)} %fusion.6.own), channel_id=1, source_target_pairs={{0,4},{4,0},{1,5},{5,1},{2,6},{6,2},{3,7},{7,3},{8,12},{12,8},{9,1... | collective-permute-start | bytes 503816 | tf_op jit(solution)/shard_map/ppermute | solution.py:392
  150.7 6.0 %copy-start.3 = (bf16[656,128]{1,0:T(8,128)(2,1)}, bf16[656,128]{1,0:T(8,128)(2,1)S(1)}, u32[]{:S(2)}) copy-start(bf16[656,128]{1,0:T(8,128)(2,1)S(1)} %collective-permute-done.1.other) | copy-start | bytes 503812
  156.7 0.8 copy-start.1

commit v3 on v2

--- a/solution.py
+++ b/solution.py
@@ -11,10 +11,11 @@
 BF16 = jnp.bfloat16
 F32 = jnp.float32
 CHUNK = 128
+GROUP = 10
 LINK = BF16
 VMEM = pl.BlockSpec(memory_space=pltpu.VMEM)
 SMEM = pl.BlockSpec(memory_space=pltpu.SMEM)
-PARAMS = pltpu.CompilerParams(vmem_limit_bytes=56 << 20)
+PARAMS = pltpu.CompilerParams(vmem_limit_bytes=28 << 20)
 
 
 def dot(a, b):
@@ -26,11 +27,28 @@
 
 
 def hits_of(presence_ref, lanes, first_row):
-    rows = first_row + lax.broadcasted_iota(jnp.int32, (CHUNK, lanes.size), 0)
-    hits = jnp.zeros((CHUNK, lanes.size), F32)
+    shape = (CHUNK // 16, 16, lanes.size)
+    rows = 16 * lax.broadcasted_iota(jnp.int32, shape, 0) + lax.broadcasted_iota(jnp.int32, shape, 1)
+    rows = rows.astype(F32).astype(BF16)
+    local = jnp.clip(presence_ref[:, lanes] - first_row, -1, CHUNK).astype(F32)
+    one, zero = jnp.ones(shape, BF16), jnp.zeros(shape, BF16)
+    hits = zero
     for record in range(presence_ref.shape[0]):
-        hits += jnp.where(rows == presence_ref[record : record + 1, lanes], 1.0, 0.0)
-    return hits
+        there = jnp.broadcast_to(local[record : record + 1], shape[1:]).astype(BF16)
+        hits += jnp.where(rows == there[None], one, zero)
+    return hits.reshape(CHUNK, lanes.size)
+
+
+def each_busy(busy, block_count, chunks, act):
+    def step(i, carry):
+        @pl.when(busy[i] > 0)
+        def _():
+            b = i // chunks
+            act(b, pl.multiple_of((i % chunks) * CHUNK, CHUNK))
+
+        return carry
+
+    lax.fori_loop(0, block_count * chunks, step, 0)
 
 
 def forward_kernel(
@@ -46,8 +64,8 @@
     second_bias,
     head_weight,
     presence,
-    shifted,
-    high,
+    logits,
+    hits,
     local_lse,
     hit_sum,
     features,
@@ -55,7 +73,7 @@
     first_slope,
     second_slope,
     wide_weight,
-    logits,
+    tops,
 ):
     blocks, cells, tile = features.shape
     block_count, slab, _ = head_weight.shape
@@ -76,33 +94,38 @@
 
     hit_sum[...] = jnp.zeros_like(hit_sum)
     wide_weight[...] = jnp.zeros_like(wide_weight)
-
-    def step(b, carry):
-        spot = clade[b]
-        half = pl.ds(pl.multiple_of((spot % 2) * slab, slab), slab)
+    for b in range(block_count):
+        half = pl.ds(pl.multiple_of((clade[b] % 2) * slab, slab), slab)
+        wide_weight[b, half, :] = head_weight[b]
+
+    def step(i, carry):
+        for g in range(GROUP):
+            b = i * GROUP + g
+            part = dot(features[clade[b] // 2], wide_weight[b])
+            logits[b] = part
+            tops[g] = jnp.max(part.reshape(cells // 8, 8, -1), axis=0)
+        for g in range(GROUP):
+            b = i * GROUP + g
+            top = jnp.max(tops[g], axis=0, keepdims=True)
+            total = jnp.sum(jnp.exp(logits[b] - top), axis=0, keepdims=True)
+            local_lse[pl.ds(b, 1), :] = top + jnp.log(total)
+        return carry
+
+    lax.fori_loop(0, block_count // GROUP, step, 0)
+
+    def add_hits(b, start):
         lanes = pl.ds(pl.multiple_of(b * tile, tile), tile)
-        row = pl.ds(b, 1)
-        wide_weight[b, half, :] = head_weight[b]
-        logits[...] = dot(features[spot // 2], wide_weight[b])
-        top = jnp.max(logits[...], axis=0, keepdims=True)
-        terms = jnp.exp(logits[...] - top)
-        shifted[b] = terms
-        high[row, :] = top
-        local_lse[row, :] = top + jnp.log(jnp.sum(terms, axis=0, keepdims=True))
-        for k in range(cells // CHUNK):
-
-            @pl.when(busy[b * (cells // CHUNK) + k] > 0)
-            def _():
-                hits = hits_of(presence, lanes, first_cell + k * CHUNK)
-                part = hits * logits[k * CHUNK : (k + 1) * CHUNK, :]
-                hit_sum[row, :] += jnp.sum(part, axis=0, keepdims=True)
-
-        return carry
-
-    lax.fori_loop(0, block_count, step, 0)
+        rows = pl.ds(start, CHUNK)
+        found = hits_of(presence, lanes, first_cell + start)
+        hits[b, rows, :] = found
+        part = found.astype(F32) * logits[b, rows, :]
+        hit_sum[pl.ds(b, 1), :] += jnp.sum(part, axis=0, keepdims=True)
+
+    each_busy(busy, block_count, cells // CHUNK, add_hits)
 
 
 def backward_kernel(
+    records,
     first_index,
     second_index,
     clade,
@@ -110,9 +133,8 @@
     place,
     covariates,
     second_weight,
-    presence,
-    shifted,
-    high,
+    logits,
+    hits,
     lse,
     hit_sum,
     features,
@@ -136,8 +158,6 @@
     blocks, cells, tile = features.shape
     block_count = wide_weight.shape[0]
     slab = tile // 2
-    records = presence.shape[0]
-    first_cell = place[0]
     group = block_count // 2
     core = place[1]
 
@@ -149,29 +169,36 @@
     group_back[...] = jnp.zeros_like(group_back)
     act_grad[...] = jnp.zeros_like(act_grad)
 
-    def step(b, carry):
-        spot = clade[b]
-        lanes = pl.ds(pl.multiple_of(b * tile, tile), tile)
-        row = pl.ds(b, 1)
-        scale = jnp.exp(high[row, :] - lse[row, :])
-        weight_cells[...] = (shifted[b] * scale).astype(BF16)
-        for k in range(cells // CHUNK):
-
-            @pl.when(busy[b * (cells // CHUNK) + k] > 0)
-            def _():
-                hits = hits_of(presence, lanes, first_cell + k * CHUNK)
-                rows = slice(k * CHUNK, (k + 1) * CHUNK)
-                weights = shifted[b, rows, :] * scale - hits * (1.0 / records)
-                weight_cells[rows, :] = weights.astype(BF16)
-
-        slab_grad[...] = dot(features_t[spot // 2], weight_cells[...])
-        source = pl.ds(pl.multiple_of((spot % 2) * slab, slab), slab)
-        target = pl.ds(pl.multiple_of((b % group) * slab, slab), slab)
-        packed[b // group, target, :] = slab_grad[source, :]
-        group_back[spot // 2] += dot_t(weight_cells[...], wide_weight[b])
+    def weigh(i, carry):
+        for g in range(GROUP):
+            b = i * GROUP + g
+            weight_cells[b] = jnp.exp(logits[b] - lse[pl.ds(b, 1), :]).astype(BF16)
         return carry
 
-    lax.fori_loop(0, block_count, step, 0)
+    lax.fori_loop(0, block_count // GROUP, weigh, 0)
+
+    def take_hits(b, start):
+        rows = pl.ds(start, CHUNK)
+        weights = jnp.exp(logits[b, rows, :] - lse[pl.ds(b, 1), :])
+        weights -= hits[b, rows, :].astype(F32) * (1.0 / records)
+        weight_cells[b, rows, :] = weights.astype(BF16)
+
+    each_busy(busy, block_count, cells // CHUNK, take_hits)
+
+    def step(i, carry):
+        for g in range(GROUP):
+            b = i * GROUP + g
+            slab_grad[g] = dot(features_t[clade[b] // 2], weight_cells[b])
+        for g in range(GROUP):
+            b = i * GROUP + g
+            spot = clade[b]
+            source = pl.ds(pl.multiple_of((spot % 2) * slab, slab), slab)
+            target = pl.ds(pl.multiple_of((b % group) * slab, slab), slab)
+            packed[b // group, target, :] = slab_grad[g, source, :]
+            group_back[spot // 2] += dot_t(weight_cells[b], wide_weight[b])
+        return carry
+
+    lax.fori_loop(0, block_count // GROUP, step, 0)
 
     bias[...] = jnp.zeros_like(bias)
     pair = blocks // (trunk.shape[0] // 2)
@@ -251,6 +278,100 @@
     return top + jnp.log(jnp.sum(jnp.exp(parts - top), axis=0))
 
 
+def forward(
+    scalars,
+    covariates,
+    first_weight,
+    first_bias,
+    second_weight,
+    second_bias,
+    head_weight,
+    presence_t,
+):
+    blocks, tile, _ = first_weight.shape
+    block_count, _, species = head_weight.shape
+    cells = covariates.shape[0]
+    by_block = (blocks, cells, tile)
+    shape = jax.ShapeDtypeStruct
+    return pl.pallas_call(
+        forward_kernel,
+        name="forward",
+        out_shape=(
+            shape((block_count, cells, species), F32),
+            shape((block_count, cells, species), BF16),
+            shape((block_count, species), F32),
+            shape((block_count, species), F32),
+            shape(by_block, BF16),
+            shape(by_block, BF16),
+            shape(by_block, F32),
+            shape(by_block, F32),
+            shape((block_count, tile, species), BF16),
+        ),
+        in_specs=[SMEM] * 5 + [VMEM] * 7,
+        out_specs=[VMEM] * 9,
+        scratch_shapes=[pltpu.VMEM((GROUP, 8, species), F32)],
+        compiler_params=PARAMS,
+    )(
+        *scalars,
+        covariates,
+        first_weight,
+        first_bias.reshape(blocks, tile),
+        second_weight,
+        second_bias.reshape(blocks, tile),
+        head_weight,
+        presence_t,
+    )
+
+
+def backward(records, scalars, covariates, second_weight, saved, lse, nx):
+    logits, hits, _, hit_sum, features, first_act, first_slope, second_slope, wide = saved
+    by_block = blocks, cells, tile = features.shape
+    block_count, _, species = logits.shape
+    width, slab = covariates.shape[1], tile // 2
+    shape = jax.ShapeDtypeStruct
+    pair = blocks // nx
+    part_rows = pair * tile + 8
+    group = block_count // 2
+    head_rows = group * slab
+    half_rows = head_rows + -(-group // 8) * 8
+    return pl.pallas_call(
+        functools.partial(backward_kernel, records),
+        name="backward",
+        out_shape=(
+            shape((2 * nx, part_rows, tile), LINK),
+            shape((half_rows, tile), F32),
+            shape((half_rows, tile), F32),
+        ),
+        in_specs=[SMEM] * 5 + [VMEM] * 11,
+        out_specs=[VMEM] * 3,
+        scratch_shapes=[
+            pltpu.VMEM((2, half_rows, tile), F32),
+            pltpu.VMEM((2 * nx, 8, tile), F32),
+            pltpu.VMEM((blocks, tile, cells), BF16),
+            pltpu.VMEM((blocks, tile, cells), BF16),
+            pltpu.VMEM((width // tile, tile, cells), BF16),
+            pltpu.VMEM((block_count, cells, species), BF16),
+            pltpu.VMEM((GROUP, tile, species), F32),
+            pltpu.VMEM(by_block, F32),
+            pltpu.VMEM(by_block, F32),
+        ],
+        compiler_params=PARAMS,
+    )(
+        *scalars,
+        covariates,
+        second_weight,
+        logits,
+        hits,
+        lse,
+        hit_sum,
+        features,
+        first_act,
+        first_slope,
+        second_slope,
+        wide,
+    )
+
+
 def body(
     covariates,
     first_weight,
@@ -285,84 +406,25 @@
     scalars = (first_index, second_index, clade_block, busy, place)
 
     all_covariates = spread(covariates, "x", nx).reshape(cells, width)
-    by_block = (blocks, cells, tile)
-    shape = jax.ShapeDtypeStruct
-    shifted, high, local_lse, hit_sum, features, first_act, first_slope, second_slope, wide = (
-        pl.pallas_call(
-            forward_kernel,
-            name="forward",
-            out_shape=(
-                shape((block_count, cells, species), F32),
-                shape((block_count, species), F32),
-                shape((block_count, species), F32),
-                shape((block_count, species), F32),
-                shape(by_block, BF16),
-                shape(by_block, BF16),
-                shape(by_block, F32),
-                shape(by_block, F32),
-                shape((block_count, tile, species), BF16),
-            ),
-            in_specs=[SMEM] * 5 + [VMEM] * 7,
-            out_specs=[VMEM] * 9,
-            scratch_shapes=[pltpu.VMEM((cells, species), F32)],
-            compiler_params=PARAMS,
-        )(
-            *scalars,
-            all_covariates,
-            first_weight,
-            first_bias.reshape(blocks, tile),
-            second_weight,
-            second_bias.reshape(blocks, tile),
-            head_weight,
-            presence_t,
-        )
-    )
-
-    lse = join(spread(local_lse, "y", ny))
+    saved = forward(
+        scalars,
+        all_covariates,
+        first_weight,
+        first_bias,
+        second_weight,
+        second_bias,
+        head_weight,
+        presence_t,
+    )
+    lse = join(spread(saved[2], "y", ny))
     lse = join(spread(lse, ("z", "c"), nz * 2))
 
-    pair = blocks // nx
-    part_rows = pair * tile + 8
-    group = block_count // 2
+    trunk, keep, send = backward(
+        records, scalars, all_covariates, second_weight, saved, lse, nx
+    )
+    pair, group = blocks // nx, block_count // 2
     head_rows = group * slab
-    half_rows = head_rows + -(-group // 8) * 8
-    trunk, keep, send = pl.pallas_call(
-        backward_kernel,
-        name="backward",
-        out_shape=(
-            shape((2 * nx, part_rows, tile), LINK),
-            shape((half_rows, tile), F32),
-            shape((half_rows, tile), F32),
-        ),
-        in_specs=[SMEM] * 5 + [VMEM] * 12,
-        out_specs=[VMEM] * 3,
-        scratch_shapes=[
-            pltpu.VMEM((2, half_rows, tile), F32),
-            pltpu.VMEM((2 * nx, 8, tile), F32),
-            pltpu.VMEM((blocks, tile, cells), BF16),
-            pltpu.VMEM((blocks, tile, cells), BF16),
-            pltpu.VMEM((width // tile, tile, cells), BF16),
-            pltpu.VMEM((cells, species), BF16),
-            pltpu.VMEM((tile, species), F32),
-            pltpu.VMEM(by_block, F32),
-            pltpu.VMEM(by_block, F32),
-        ],
-        compiler_params=PARAMS,
-    )(
-        *scalars,
-        all_covariates,
-        second_weight,
-        presence_t,
-        shifted,
-        high,
-        lse,
-        hit_sum,
-        features,
-        first_act,
-        first_slope,
-        second_slope,
-        wide,
-    )
+    half_rows = keep.shape[0]
 
     head = keep + lax.ppermute(send, "c", swap)
     trunk = jnp.sum(lax.all_to_all(trunk, ("c", "x"), 0, 0).astype(F32), axis=0)
@@ -397,6 +459,7 @@
         ]
     )
     trunk = spread(trunk, ("c", "x"), 2 * nx)
+    shape = jax.ShapeDtypeStruct
     species_loss, head_grad, first_grad, first_bias_grad, second_grad, second_bias_grad = (
         pl.pallas_call(
             functools.partial(finish_kernel, total_cells, records),

time: 161 us -> 163 us (1.012)
  local copies, waits for them, and re-layouts: 5.75 us -> 28 us
  Pallas kernels: 36.9 us -> 16.7 us
  waiting for transfers between devices: 18.6 us -> 20.7 us
  other arithmetic: 4 us -> 1.93 us
    unnamed x10 -> x54, local copies, waits for them, and re-layouts: 1.51 us -> 25 us
    pallas_call x2, Pallas kernels: 34.4 us -> 14.9 us  [the longest x1 7.61 us: backward(): pl.pallas_call(functools.partial(backward_kernel, records), name='backwar...]
  transfers between devices with their start and end apart: 5 -> 5, of which waited for: 4 -> 4; matrix products, arithmetic and copies ran while one was open for 2% -> 1% of each run, Pallas kernels for 0% -> 0%
where the time goes in v3:
time: 163 us; the launch traced here: 162 us
  blocking collectives  73.7 us (45%)
  local copies, waits for them, and re-layouts  28 us (17%)
  waiting for transfers between devices  20.7 us (13%)
  starting transfers between devices  19.7 us (12%)
  Pallas kernels  16.7 us (10%)
  other arithmetic  1.93 us (1%)
    all_to_all x3, blocking collectives, spread(): lax.all_to_all(jnp.broadcast_to(value[None], (size, *value.shape)), axis,...  56.4 us
    unnamed x54, local copies, waits for them, and re-layouts  25 us
    all_to_all x1, blocking collectives, body(): lax.all_to_all(cut, ('y', 'z'), 0, 0).astype(F32)  17.3 us
    all_to_all x2, starting transfers between devices, spread(): lax.all_to_all(jnp.broadcast_to(value[None], (size, *value.shape)), axis,...  11.8 us
    all_to_all x2, waiting for transfers between devices, spread(): lax.all_to_all(jnp.broadcast_to(value[None], (size, *value.shape)), axis,...  10 us
    all_to_all x1, waiting for transfers between devices, body(): trunk = jnp.sum(lax.all_to_all(trunk, ('c', 'x'), 0, 0).astype(F32), axis=0)  9.39 us
    pallas_call x1, Pallas kernels, backward(): pl.pallas_call(functools.partial(backward_kernel, records), name='backwar...  7.61 us
    pallas_call x1, Pallas kernels, forward(): pl.pallas_call(forward_kernel, name='forward', out_shape=(shape((block_co...  7.33 us
  transfers between devices with their start and end apart: 5, of which 4 were waited for; matrix products, arithmetic and copies ran while one was open for 1% of the time, Pallas kernels for 0%

profile of v3, /device:TPU:1, one launch (start us, length us, event | category | flops | bytes accessed | tf_op | source)
XLA Modules:
  0.0 161.7 jit_solution(8315596520790292957)
XLA Ops:
  0.7 1.6 broadcast_in_dim.13
  2.3 4.8 %all-to-all-start = ((bf16[4,128,256]{2,1,0:T(8,128)(2,1)}), bf16[4,128,256]{2,1,0:T(8,128)(2,1)S(1)}, u32[]{:S(2)}, u32[]{:S(2)}) async-start(bf16[4,128,256]{2,1,0:T(8,128)(2,1)} %broadcast_in_dim.13), calls=%async_computation | async-start | bytes 524288 | tf_op jit(solution)/shard_map/all_to_all | solution.py:273
  7.1 1.0 compare_reduce_fusion.3
  8.2 0.1 bitcast_reduce_fusion.2
  8.3 0.1 bitcast_reduce_fusion
  8.4 0.1 copy.30
  8.5 0.1 reshape.77.busy
  8.6 0.1 pad_add_fusion.place
  8.7 4.0 %all-to-all-done = bf16[4,128,256]{2,1,0:T(8,128)(2,1)S(1)} async-done(((bf16[4,128,256]{2,1,0:T(8,128)(2,1)}), bf16[4,128,256]{2,1,0:T(8,128)(2,1)S(1)}, u32[]{:S(2)}, u32[]{:S(2)}) %all-to-all-start) | async-done | bytes 262176 | tf_op jit(solution)/shard_map/all_to_all | solution.py:273
  12.7 0.9 copy-done.10
  13.6 0.9 copy-done.12
  14.5 1.0 copy-done.16
  15.5 0.9 copy-done.17
  16.4 0.7 copy-done.18
  17.1 0.7 copy-done.19
  17.8 0.7 copy-done.20
  18.5 0.7 copy-done.22
  19.1 0.7 copy-done.24
  19.8 7.3 %forward.1 = (f32[20,512,128]{2,1,0:T(8,128)S(1)}, bf16[20,512,128]{2,1,0:T(8,128)(2,1)S(1)}, f32[20,128]{1,0:T(8,128)S(1)}, f32[20,128]{1,0:T(8,128)S(1)}, bf16...) custom-call(s32[8]{0:T(128)S(1)} %copy-done.20, ...), custom_call_target="tpu_custom_call" | custom-call | tf_op jit(solution)/shard_map/forward/pallas_call | solution.py:296
  27.1 2.3 %copy-done = f32[20,512,128]{2,1,0:T(8,128)} copy-done((f32[20,512,128]{2,1,0:T(8,128)}, f32[20,512,128]{2,1,0:T(8,128)S(1)}, u32[]{:S(2)}) %copy-start) | copy-done | bytes 5242904
  29.4 1.4 copy-done.2
  30.8 1.4 copy-done.4
  32.2 1.0 copy-done.6
  33.2 1.0 copy-done.8
  34.1 0.8 copy-done.13
  35.0 14.3 %all_to_all.35 = f32[8,20,128]{2,1,0:T(8,128)S(1)} all-to-all(f32[8,20,128]{2,1,0:T(8,128)S(1)} %broadcast_in_dim.14), channel_id=1, replica_groups=mesh['y'=8,'z'=8,'c'=2,'x'=4] {'y'}, dimensions={0} | all-to-all | bytes 163840 | tf_op jit(solution)/shard_map/all_to_all | solution.py:273
  49.4 24.6 %all_to_all.36 = f32[16,20,128]{2,1,0:T(8,128)S(1)} all-to-all(f32[16,20,128]{2,1,0:T(8,128)S(1)} %broadcast_in_dim.15), channel_id=1, replica_groups=mesh['y'=8,'z'=8,'c'=2,'x'=4] {'z','c'}, dimensions={0} | all-to-all | bytes 327680 | tf_op jit(solution)/shard_map/all_to_all | solution.py:273
  74.2 2.5 %copy-done.1 = f32[20,512,128]{2,1,0:T(8,128)S(1)} copy-done((f32[20,512,128]{2,1,0:T(8,128)S(1)}, f32[20,512,128]{2,1,0:T(8,128)}, u32[]{:S(2)}) %copy-start.1) | copy-done | bytes 5242904
  76.6 1.6 copy-done.3
  78.2 1.6 copy-done.5
  79.8 1.2 copy-done.7
  81.1 1.2 copy-done.9
  82.3 1.1 copy-done.14
  83.4 7.6 %backward.1 = (bf16[8,264,128]{2,1,0:T(8,128)(2,1)S(1)}, f32[656,128]{1,0:T(8,128)S(1)}, f32[656,128]{1,0:T(8,128)}) custom-call(s32[8]{0:T(128)S(1)} %copy-done.21, s32[8]{0:T(128)S(1)} %copy-done.23, s32[20]{0:T(128)S(1)} %copy-done.25, s32[80]{0:T(128)S(1)} %reshape.77.busy, s32[2]{0:T(128)S(1)} %pad_add_fusion.place, bf16[512,256]{1,0:T(8,128)(2,1)S(1)} %bitcast.36, ...), custom_call_target="tpu_custom_call" | custom-call | tf_op jit(solution)/shard_map/backward/pallas_call | solution.py:337
  91.0 0.8 copy-done.15
  91.8 1.9 %collective-permute-start = (f32[656,128]{1,0:T(8,128)}, f32[656,128]{1,0:T(8,128)S(1)}, u32[]{:S(2)}, u32[]{:S(2)}) collective-permute-start(f32[656,128]{1,0:T(8,128)} %get-tuple-element.35), channel_id=1, source_target_pairs={{0,4},{4,0},{1,5},{5,1},{2,6},{6,2},{3,7},{7,3},{8,12},{12,8},{9,1... | collective-permute-start | bytes 1007624 | tf_op jit(solution)/shard_map/ppermute | solution.py:429
  93.7 4.0 %all-to-all-start.3 = ((bf16[8,264,128]{2,1,0:T(8,128)(2,1)}), bf16[8,264,128]{2,1,0:T(8,128)(2,1)S(1)}, u32[]{:S(2)}, u32[]{:S(2)}) async-start(bf16[8,264,128]{2,1,0:T(8,128)(2,1)} %copy-done.15), calls=%async_computation.3 | async-start | bytes 1081344 | tf_op jit(solution)/shard_map/all_to_all | solution.py:430
  97.8 9.4 %all-to-all-done.3 = bf16[8,264,128]{2,1,0:T(8,128)(2,1)S(1)} async-done(((bf16[8,264,128]{2,1,0:T(8,128)(2,1)}), bf16[8,264,128]{2,1,0:T(8,128)(2,1)S(1)}, u32[]{:S(2)}, u32[]{:S(2)}) %all-to-all-start.3) | async-done | bytes 540704 | tf_op jit(solution)/shard_map/all_to_all | solution.py:430
  107.4 0.2 fusion.5
  107.6 17.3 %all_to_all.37 = bf16[64,16,128]{2,1,0:T(8,128)(2,1)S(1)} all-to-all(bf16[64,16,128]{2,1,0:T(8,128)(2,1)S(1)} %fusion.5), channel_id=1, replica_groups=mesh['y'=8,'z'=8,'c'=2,'x'=4] {'y','z'}, dimensions={0} | all-to-all | bytes 524288 | tf_op jit(solution)/shard_map/all_to_all | solution.py:444
  124.9 17.5 %all_to_all.38 = bf16[64,16,128]{2,1,0:T(8,128)(2,1)S(1)} all-to-all(bf16[64,16,128]{2,1,0:T(8,128)(2,1)S(1)} %broadcast_in_dim.17), channel_id=1, replica_groups=mesh['y'=8,'z'=8,'c'=2,'x'=4] {'y','z'}, dimensions={0} | all-to-all | bytes 524288 | tf_op jit(solution)/shard_map/all_to_all | solution.py:273
  142.4 0.9 broadcast_in_dim.18
  143.3 7.0 %all-to-all-start.6 = ((bf16[8,264,128]{2,1,0:T(8,128)(2,1)}), bf16[8,264,128]{2,1,0:T(8,128)(2,1)S(1)}, u32[]{:S(2)}, u32[]{:S(2)}) async-start(bf16[8,264,128]{2,1,0:T(8,128)(2,1)} %broadcast_in_dim.18), calls=%async_computation.6 | async-start | bytes 1081344 | tf_op jit(solution)/shard_map/all_to_all | solution.py:273
  150.3 0.1 slice.55
  150.5 2.0 %collective-permute-start.1 = (bf16[656,128]{1,0:T(8,128)(2,1)S(1)}, bf16[656,128]{1,0:T(8,128)(2,1)S(1)}, u32[]{:S(2)}, u32[]{:S(2)}) collective-permute-start(bf16[656,128]{1,0:T(8,128)(2,1)S(1)} %fusion.6.own), channel_id=1, source_target_pairs={{0,4},{4,0},{1,5},{5,1},{2,6},{6,2},{3,7},{7,3},{8,12},{12,8},{9,1... | collective-permute-start | bytes 503816 | tf_op jit(solution)/shard_map/ppermute | solution.py:454
  152.5 1.3 collective-permute-done.1.other
  153.8 6.0 %all-to-all-done.6.trunk = bf16[8,264,128]{2,1,0:T(8,128)(2,1)S(1)} async-done(((bf16[8,264,128]{2,1,0:T(8,128)(2,1)}), bf16[8,264,128]{2,1,0:T(8,128)(2,1)S(1)}, u32[]{:S(2)}, u32[]{:S(2)}) %all-to-all-start.6) | async-done | bytes 540704 | tf_op jit(solution)/shard_map/all_to_all | solution.py:273
  159.8 1.8 %finish.1 = (f32[20,128]{1,0:T(8,128)}, f32[20,64,128]{2,1,0:T(8,128)}, f32[8,128,128]{2,1,0:T(8,128)}, f32[8,128]{1,0:T(8,128)}, f32[8,128,128]{2,1,0:T(8,128)}, /*index=5*/f32[8,128]{1,0:T(8,128)}) custom-call(s32[2]{0:T(128)S(1)} %pad_add_fusion.place, bf16[8,264,128]{2,1,0:T(8,128)(2,1)S(1)} %all-to-all-done.6.trunk, bf16[656,128]{1,0:T(8,128)(2,1)S(1)} %fusion.6.own, ...), custom_call_target="tpu_custom_call" | custom-call | tf_op jit(solution)/shard_map/finish/pallas_call | solution.py:464
  (59 shorter events, 0.7 us)
Async XLA Ops:
  0.6 73.5 %copy-start.25 = (s32[20]{0:T(128)S(1)}, s32[20]{0:T(128)}, u32[]{:S(2)}) copy-start(s32[20]{0:T(128)} %clade.3) | copy-start | bytes 244
  0.6 73.5 %copy-start.23 = (s32[8]{0:T(128)S(1)}, s32[8]{0:T(128)}, u32[]{:S(2)}) copy-start(s32[8]{0:T(128)} %second_index.3) | copy-start | bytes 100
  0.7 73.5 %copy-start.11 = (bf16[8,128,128]{2,1,0:T(8,128)(2,1)S(1)}, bf16[8,128,128]{2,1,0:T(8,128)(2,1)}, u32[]{:S(2)}) copy-start(bf16[8,128,128]{2,1,0:T(8,128)(2,1)} %second_weight.3) | copy-start | bytes 786436
  0.7 73.5 %copy-start.21 = (s32[8]{0:T(128)S(1)}, s32[8]{0:T(128)}, u32[]{:S(2)}) copy-start(s32[8]{0:T(128)} %first_index.3) | copy-start | bytes 100
  2.3 10.4 %all-to-all-start = ((bf16[4,128,256]{2,1,0:T(8,128)(2,1)}), bf16[4,128,256]{2,1,0:T(8,128)(2,1)S(1)}, u32[]{:S(2)}, u32[]{:S(2)}) async-start(bf16[4,128,256]{2,1,0:T(8,128)(2,1)} %broadcast_in_dim.13), calls=%async_computation | async-start | bytes 524288 | tf_op jit(solution)/shard_map/all_to_all | solution.py:273
  12.7 1.0 copy-start.10
  13.6 0.9 copy-start.12
  14.5 1.0 copy-start.16
  15.5 0.9 copy-start.17
  16.4 0.7 copy-start.18
  17.1 0.7 copy-start.19
  17.8 0.7 copy-start.20
  18.5 0.7 copy-start.22
  19.1 0.7 copy-start.24
  27.1 2.3 %copy-start = (f32[20,512,128]{2,1,0:T(8,128)}, f32[20,512,128]{2,1,0:T(8,128)S(1)}, u32[]{:S(2)}) copy-start(f32[20,512,128]{2,1,0:T(8,128)S(1)} %get-tuple-element.24.logits) | copy-start | bytes 15728644
  29.4 1.4 copy-start.2
  30.8 1.4 copy-start.4
  32.2 1.0 copy-start.6
  33.2 1.0 copy-start.8
  34.1 0.8 copy-start.13
  74.2 2.5 %copy-start.1 = (f32[20,512,128]{2,1,0:T(8,128)S(1)}, f32[20,512,128]{2,1,0:T(8,128)}, u32[]{:S(2)}) copy-start(f32[20,512,128]{2,1,0:T(8,128)} %copy-done) | copy-start | bytes 15728644
  76.6 1.6 copy-start.3
  78.2 1.6 copy-start.5
  79.8 1.2 copy-start.7
  81.1 1.2 copy-start.9
  82.3 1.1 copy-start.14
  91.0 0.8 copy-start.15
  91.8 5.9 %collective-permute-start = (f32[656,128]{1,0:T(8,128)}, f32[656,128]{1,0:T(8,128)S(1)}, u32[]{:S(2)}, u32[]{:S(2)}) collective-permute-start(f32[656,128]{1,0:T(8,128)} %get-tuple-element.35), channel_id=1, source_target_pairs={{0,4},{4,0},{1,5},{5,1},{2,6},{6,2},{3,7},{7,3},{8,12},{12,8},{9,1... | collective-permute-start | bytes 1007624 | tf_op jit(solution)/shard_map/ppermute | solution.py:429
  93.7 13.5 %all-to-all-start.3 = ((bf16[8,264,128]{2,1,0:T(8,128)(2,1)}), bf16[8,264,128]{2,1,0:T(8,128)(2,1)S(1)}, u32[]{:S(2)}, u32[]{:S(2)}) async-start(bf16[8,264,128]{2,1,0:T(8,128)(2,1)} %copy-done.15), calls=%async_computation.3 | async-start | bytes 1081344 | tf_op jit(solution)/shard_map/all_to_all | solution.py:430
  143.3 16.5 %all-to-all-start.6 = ((bf16[8,264,128]{2,1,0:T(8,128)(2,1)}), bf16[8,264,128]{2,1,0:T(8,128)(2,1)S(1)}, u32[]{:S(2)}, u32[]{:S(2)}) async-start(bf16[8,264,128]{2,1,0:T(8,128)(2,1)} %broadcast_in_dim.18), calls=%async_computation.6 | async-start | bytes 1081344 | tf_op jit(solution)/shard_map/all_to_all | solution.py:273
  150.5 3.3 %collective-permute-start.1 = (bf16[656,128]{1,0:T(8,128)(2,1)S(1)}, bf16[656,128]{1,0:T(8,128)(2,1)S(1)}, u32[]{:S(2)}, u32[]{:S(2)}) collective-permute-start(bf16[656,128]{1,0:T(8,128)(2,1)S(1)} %fusion.6.own), channel_id=1, source_target_pairs={{0,4},{4,0},{1,5},{5,1},{2,6},{6,2},{3,7},{7,3},{8,12},{12,8},{9,1... | collective-permute-start | bytes 503816 | tf_op jit(solution)/shard_map/ppermute | solution.py:454

commit v4 on v3

--- a/solution.py
+++ b/solution.py
@@ -14,8 +14,9 @@
 GROUP = 10
 LINK = BF16
 VMEM = pl.BlockSpec(memory_space=pltpu.VMEM)
+ANY = pl.BlockSpec(memory_space=pl.ANY)
 SMEM = pl.BlockSpec(memory_space=pltpu.SMEM)
-PARAMS = pltpu.CompilerParams(vmem_limit_bytes=28 << 20)
+PARAMS = pltpu.CompilerParams(vmem_limit_bytes=58 << 20)
 
 
 def dot(a, b):
@@ -39,6 +40,34 @@
     return hits.reshape(CHUNK, lanes.size)
 
 
+def fetch(sem, *pairs):
+    copies = [pltpu.make_async_copy(*pair, sem.at[i]) for i, pair in enumerate(pairs)]
+    for copy in copies:
+        copy.start()
+    return copies
+
+
+class Part:
+    def __init__(self, ref, start):
+        self.ref, self.start = ref, start
+
+    def __getitem__(self, i):
+        return self.ref[self.start + i]
+
+
+def scalar_parts(ref, blocks, block_count):
+    starts = (2, 2 + blocks, 2 + 2 * blocks, 2 + 2 * blocks + block_count, 0)
+    return [Part(ref, start) for start in starts]
+
+
+def widen(wide_weight, head_weight, clade):
+    slab = head_weight.shape[1]
+    wide_weight[...] = jnp.zeros_like(wide_weight)
+    for b in range(head_weight.shape[0]):
+        half = pl.ds(pl.multiple_of((clade[b] % 2) * slab, slab), slab)
+        wide_weight[b, half, :] = head_weight[b]
+
+
 def each_busy(busy, block_count, chunks, act):
     def step(i, carry):
         @pl.when(busy[i] > 0)
@@ -52,11 +81,19 @@
 
 
 def forward_kernel(
-    first_index,
-    second_index,
-    clade,
-    busy,
-    place,
+    scalars,
+    covariates_in,
+    first_weight_in,
+    first_bias_in,
+    second_weight_in,
+    second_bias_in,
+    head_weight_in,
+    presence_in,
+    logits_out,
+    hits_out,
+    trunk_out,
+    local_lse,
+    hit_sum,
     covariates,
     first_weight,
     first_bias,
@@ -66,24 +103,37 @@
     presence,
     logits,
     hits,
-    local_lse,
-    hit_sum,
-    features,
-    first_act,
-    first_slope,
-    second_slope,
+    trunk,
     wide_weight,
     tops,
+    fetch_sem,
+    logit_sem,
+    hit_sem,
+    trunk_sem,
 ):
+    fetched = fetch(
+        fetch_sem,
+        (covariates_in, covariates),
+        (first_weight_in, first_weight),
+        (first_bias_in, first_bias),
+        (second_weight_in, second_weight),
+        (second_bias_in, second_bias),
+        (head_weight_in, head_weight),
+        (presence_in, presence),
+    )
+    first_act, features, first_slope, second_slope = (trunk.at[i] for i in range(4))
     blocks, cells, tile = features.shape
     block_count, slab, _ = head_weight.shape
+    first_index, second_index, clade, busy, place = scalar_parts(scalars, blocks, block_count)
     first_cell = place[0]
 
     def layer(pre, act_ref, slope_ref, o):
         sigma = 1.0 / (1.0 + jnp.exp(-pre))
         act_ref[o] = (pre * sigma).astype(BF16)
-        slope_ref[o] = sigma * (1.0 + pre * (1.0 - sigma))
-
+        slope_ref[o] = (sigma * (1.0 + pre * (1.0 - sigma))).astype(BF16)
+
+    for copy in fetched[:5]:
+        copy.wait()
     for o in range(blocks):
         columns = pl.ds(pl.multiple_of(first_index[o] * tile, tile), tile)
         pre = dot(covariates[:, columns], first_weight[o]) + first_bias[o : o + 1, :]
@@ -92,11 +142,12 @@
         pre = dot(first_act[second_index[o]], second_weight[o]) + second_bias[o : o + 1, :]
         layer(pre, features, second_slope, o)
 
+    trunk_copy = pltpu.make_async_copy(trunk, trunk_out, trunk_sem.at[0])
+    trunk_copy.start()
     hit_sum[...] = jnp.zeros_like(hit_sum)
-    wide_weight[...] = jnp.zeros_like(wide_weight)
-    for b in range(block_count):
-        half = pl.ds(pl.multiple_of((clade[b] % 2) * slab, slab), slab)
-        wide_weight[b, half, :] = head_weight[b]
+    fetched[5].wait()
+    fetched[6].wait()
+    widen(wide_weight, head_weight, clade)
 
     def step(i, carry):
         for g in range(GROUP):
@@ -111,7 +162,14 @@
             local_lse[pl.ds(b, 1), :] = top + jnp.log(total)
         return carry
 
-    lax.fori_loop(0, block_count // GROUP, step, 0)
+    logit_copies = []
+    for i in range(block_count // GROUP):
+        step(i, 0)
+        part = pl.ds(i * GROUP, GROUP)
+        logit_copies.append(
+            pltpu.make_async_copy(logits.at[part], logits_out.at[part], logit_sem.at[i])
+        )
+        logit_copies[i].start()
 
     def add_hits(b, start):
         lanes = pl.ds(pl.multiple_of(b * tile, tile), tile)
@@ -122,29 +180,37 @@
         hit_sum[pl.ds(b, 1), :] += jnp.sum(part, axis=0, keepdims=True)
 
     each_busy(busy, block_count, cells // CHUNK, add_hits)
+    hit_copy = pltpu.make_async_copy(hits, hits_out, hit_sem.at[0])
+    hit_copy.start()
+    hit_copy.wait()
+    for copy in logit_copies:
+        copy.wait()
+    trunk_copy.wait()
 
 
 def backward_kernel(
     records,
-    first_index,
-    second_index,
-    clade,
-    busy,
-    place,
-    covariates,
-    second_weight,
-    logits,
-    hits,
-    lse,
-    hit_sum,
-    features,
-    first_act,
-    first_slope,
-    second_slope,
-    wide_weight,
+    scalars,
+    covariates_in,
+    second_weight_in,
+    head_weight_in,
+    logits_in,
+    hits_in,
+    trunk_in,
+    lse_in,
+    hit_sum_in,
     trunk,
     keep,
     send,
+    covariates,
+    second_weight,
+    head_weight,
+    lse,
+    hit_sum,
+    logits,
+    hits,
+    layers,
+    wide_weight,
     packed,
     bias,
     features_t,
@@ -154,18 +220,55 @@
     slab_grad,
     group_back,
     act_grad,
+    fetch_sem,
+    logit_sem,
+    hit_sem,
+    trunk_sem,
 ):
+    first_act, features, first_slope, second_slope = (layers.at[i] for i in range(4))
     blocks, cells, tile = features.shape
-    block_count = wide_weight.shape[0]
-    slab = tile // 2
+    block_count, slab, _ = head_weight.shape
+
+    layer_copies = [
+        pltpu.make_async_copy(trunk_in.at[part], layers.at[part], trunk_sem.at[i])
+        for i, part in enumerate((pl.ds(0, 2), pl.ds(2, 2)))
+    ]
+    logit_copies = [
+        pltpu.make_async_copy(
+            logits_in.at[pl.ds(i * GROUP, GROUP)],
+            logits.at[pl.ds(i * GROUP, GROUP)],
+            logit_sem.at[i],
+        )
+        for i in range(block_count // GROUP)
+    ]
+
+    hit_copy = pltpu.make_async_copy(hits_in, hits, hit_sem.at[0])
+    first_index, second_index, clade, busy, place = scalar_parts(scalars, blocks, block_count)
+    fetched = fetch(
+        fetch_sem,
+        (head_weight_in, head_weight),
+        (covariates_in, covariates),
+        (lse_in, lse),
+        (hit_sum_in, hit_sum),
+        (second_weight_in, second_weight),
+    )
+    layer_copies[0].start()
+    for copy in logit_copies:
+        copy.start()
+    layer_copies[1].start()
+    hit_copy.start()
+    fetched[0].wait()
+    fetched[1].wait()
+    widen(wide_weight, head_weight, clade)
+    for o in range(covariates.shape[1] // tile):
+        covariates_t[o] = covariates[:, o * tile : (o + 1) * tile].T
+    layer_copies[0].wait()
     group = block_count // 2
     core = place[1]
 
     for o in range(blocks):
         features_t[o] = features[o].T
         first_act_t[o] = first_act[o].T
-    for o in range(covariates.shape[1] // tile):
-        covariates_t[o] = covariates[:, o * tile : (o + 1) * tile].T
     group_back[...] = jnp.zeros_like(group_back)
     act_grad[...] = jnp.zeros_like(act_grad)
 
@@ -175,7 +278,10 @@
             weight_cells[b] = jnp.exp(logits[b] - lse[pl.ds(b, 1), :]).astype(BF16)
         return carry
 
-    lax.fori_loop(0, block_count // GROUP, weigh, 0)
+    fetched[2].wait()
+    for i, copy in enumerate(logit_copies):
+        copy.wait()
+        weigh(i, 0)
 
     def take_hits(b, start):
         rows = pl.ds(start, CHUNK)
@@ -183,6 +289,7 @@
         weights -= hits[b, rows, :].astype(F32) * (1.0 / records)
         weight_cells[b, rows, :] = weights.astype(BF16)
 
+    hit_copy.wait()
     each_busy(busy, block_count, cells // CHUNK, take_hits)
 
     def step(i, carry):
@@ -198,8 +305,12 @@
             group_back[spot // 2] += dot_t(weight_cells[b], wide_weight[b])
         return carry
 
-    lax.fori_loop(0, block_count // GROUP, step, 0)
-
+    for i in range(block_count // GROUP):
+        step(i, 0)
+
+    layer_copies[1].wait()
+    fetched[3].wait()
+    fetched[4].wait()
     bias[...] = jnp.zeros_like(bias)
     pair = blocks // (trunk.shape[0] // 2)
 
@@ -209,11 +320,11 @@
         bias[part, at : at + 1, :] = jnp.sum(dz.astype(F32), axis=0, keepdims=True)
 
     for o in range(blocks):
-        dz = (group_back[o] * second_slope[o]).astype(BF16)
+        dz = (group_back[o] * second_slope[o].astype(F32)).astype(BF16)
         trunk_sums(o, 1, first_act_t[second_index[o]], dz)
         act_grad[second_index[o]] += dot_t(dz, second_weight[o])
     for o in range(blocks):
-        dz = (act_grad[o] * first_slope[o]).astype(BF16)
+        dz = (act_grad[o] * first_slope[o].astype(F32)).astype(BF16)
         trunk_sums(o, 0, covariates_t[first_index[o]], dz)
     for part in range(trunk.shape[0]):
         trunk[part, pair * tile :, :] = bias[part].astype(LINK)
@@ -229,7 +340,7 @@
 def finish_kernel(
     total_cells,
     records,
-    place,
+    scalars,
     trunk,
     own,
     other,
@@ -242,7 +353,7 @@
     second_bias_grad,
     halves,
 ):
-    core = place[1]
+    core = scalars[1]
     blocks, tile, _ = first_grad.shape
     block_count, slab, _ = head_grad.shape
     group = block_count // 2
@@ -291,28 +402,42 @@
     blocks, tile, _ = first_weight.shape
     block_count, _, species = head_weight.shape
     cells = covariates.shape[0]
-    by_block = (blocks, cells, tile)
+    by_clade = (block_count, cells, species)
+    by_layer = (4, blocks, cells, tile)
     shape = jax.ShapeDtypeStruct
     return pl.pallas_call(
         forward_kernel,
         name="forward",
         out_shape=(
-            shape((block_count, cells, species), F32),
-            shape((block_count, cells, species), BF16),
+            shape(by_clade, F32),
+            shape(by_clade, BF16),
+            shape(by_layer, BF16),
             shape((block_count, species), F32),
             shape((block_count, species), F32),
-            shape(by_block, BF16),
-            shape(by_block, BF16),
-            shape(by_block, F32),
-            shape(by_block, F32),
-            shape((block_count, tile, species), BF16),
         ),
-        in_specs=[SMEM] * 5 + [VMEM] * 7,
-        out_specs=[VMEM] * 9,
-        scratch_shapes=[pltpu.VMEM((GROUP, 8, species), F32)],
+        in_specs=[SMEM] + [ANY] * 7,
+        out_specs=[ANY] * 3 + [VMEM] * 2,
+        scratch_shapes=[
+            pltpu.VMEM(covariates.shape, BF16),
+            pltpu.VMEM(first_weight.shape, BF16),
+            pltpu.VMEM((blocks, tile), F32),
+            pltpu.VMEM(second_weight.shape, BF16),
+            pltpu.VMEM((blocks, tile), F32),
+            pltpu.VMEM(head_weight.shape, BF16),
+            pltpu.VMEM(presence_t.shape, jnp.int32),
+            pltpu.VMEM(by_clade, F32),
+            pltpu.VMEM(by_clade, BF16),
+            pltpu.VMEM(by_layer, BF16),
+            pltpu.VMEM((block_count, tile, species), BF16),
+            pltpu.VMEM((GROUP, 8, species), F32),
+            pltpu.SemaphoreType.DMA((7,)),
+            pltpu.SemaphoreType.DMA((block_count // GROUP,)),
+            pltpu.SemaphoreType.DMA((1,)),
+            pltpu.SemaphoreType.DMA((1,)),
+        ],
         compiler_params=PARAMS,
     )(
-        *scalars,
+        scalars,
         covariates,
         first_weight,
         first_bias.reshape(blocks, tile),
@@ -323,17 +448,17 @@
     )
 
 
-def backward(records, scalars, covariates, second_weight, saved, lse, nx):
-    logits, hits, _, hit_sum, features, first_act, first_slope, second_slope, wide = saved
-    by_block = blocks, cells, tile = features.shape
-    block_count, _, species = logits.shape
-    width, slab = covariates.shape[1], tile // 2
+def backward(records, scalars, covariates, second_weight, head_weight, saved, lse, nx):
+    logits, hits, layers, _, hit_sum = saved
+    _, *by_block = layers.shape
+    blocks, cells, tile = by_block
+    block_count, slab, species = head_weight.shape
+    width = covariates.shape[1]
     shape = jax.ShapeDtypeStruct
     pair = blocks // nx
     part_rows = pair * tile + 8
     group = block_count // 2
-    head_rows = group * slab
-    half_rows = head_rows + -(-group // 8) * 8
+    half_rows = group * slab + -(-group // 8) * 8
     return pl.pallas_call(
         functools.partial(backward_kernel, records),
         name="backward",
@@ -342,33 +467,43 @@
             shape((half_rows, tile), F32),
             shape((half_rows, tile), F32),
         ),
-        in_specs=[SMEM] * 5 + [VMEM] * 11,
+        in_specs=[SMEM] + [ANY] * 8,
         out_specs=[VMEM] * 3,
         scratch_shapes=[
+            pltpu.VMEM(covariates.shape, BF16),
+            pltpu.VMEM(second_weight.shape, BF16),
+            pltpu.VMEM(head_weight.shape, BF16),
+            pltpu.VMEM(lse.shape, F32),
+            pltpu.VMEM(hit_sum.shape, F32),
+            pltpu.VMEM(logits.shape, F32),
+            pltpu.VMEM(hits.shape, BF16),
+            pltpu.VMEM(layers.shape, BF16),
+            pltpu.VMEM((block_count, tile, species), BF16),
             pltpu.VMEM((2, half_rows, tile), F32),
             pltpu.VMEM((2 * nx, 8, tile), F32),
             pltpu.VMEM((blocks, tile, cells), BF16),
             pltpu.VMEM((blocks, tile, cells), BF16),
             pltpu.VMEM((width // tile, tile, cells), BF16),
-            pltpu.VMEM((block_count, cells, species), BF16),
+            pltpu.VMEM(hits.shape, BF16),
             pltpu.VMEM((GROUP, tile, species), F32),
             pltpu.VMEM(by_block, F32),
             pltpu.VMEM(by_block, F32),
+            pltpu.SemaphoreType.DMA((5,)),
+            pltpu.SemaphoreType.DMA((block_count // GROUP,)),
+            pltpu.SemaphoreType.DMA((1,)),
+            pltpu.SemaphoreType.DMA((2,)),
         ],
         compiler_params=PARAMS,
     )(
-        *scalars,
+        scalars,
         covariates,
         second_weight,
+        head_weight,
         logits,
         hits,
+        layers,
         lse,
         hit_sum,
-        features,
-        first_act,
-        first_slope,
-        second_slope,
-        wide,
     )
 
 
@@ -403,7 +538,7 @@
     )
     busy = busy.astype(jnp.int32).reshape(-1)
     place = jnp.stack([first_cell, core]).astype(jnp.int32)
-    scalars = (first_index, second_index, clade_block, busy, place)
+    scalars = jnp.concatenate([place, first_index, second_index, clade_block, busy])
 
     all_covariates = spread(covariates, "x", nx).reshape(cells, width)
     saved = forward(
@@ -416,11 +551,11 @@
         head_weight,
         presence_t,
     )
-    lse = join(spread(saved[2], "y", ny))
+    lse = join(spread(saved[3], "y", ny))
     lse = join(spread(lse, ("z", "c"), nz * 2))
 
     trunk, keep, send = backward(
-        records, scalars, all_covariates, second_weight, saved, lse, nx
+        records, scalars, all_covariates, second_weight, head_weight, saved, lse, nx
     )
     pair, group = blocks // nx, block_count // 2
     head_rows = group * slab
@@ -476,7 +611,7 @@
             out_specs=[VMEM] * 6,
             scratch_shapes=[pltpu.VMEM((2, half_rows, tile), LINK)],
             compiler_params=PARAMS,
-        )(place, trunk, head, other_head, lse)
+        )(scalars, trunk, head, other_head, lse)
     )
     return (
         species_loss.reshape(-1),

time: 163 us -> 149 us (0.914)
  local copies, waits for them, and re-layouts: 28 us -> 6.46 us
  Pallas kernels: 16.7 us -> 26.2 us
  waiting for transfers between devices: 20.7 us -> 18.5 us
    unnamed x54 -> x10, local copies, waits for them, and re-layouts: 25 us -> 1.51 us
    pallas_call x1, Pallas kernels: 7.33 us -> 12.3 us  [forward(): pl.pallas_call(forward_kernel, name='forward', out_shape=(shape(by_clade,...]
    pallas_call x1, Pallas kernels: 7.61 us -> 11.5 us  [backward(): pl.pallas_call(functools.partial(backward_kernel, records), name='backwar...]
  transfers between devices with their start and end apart: 5 -> 5, of which waited for: 4 -> 4; matrix products, arithmetic and copies ran while one was open for 1% -> 3% of each run, Pallas kernels for 0% -> 0%
where the time goes in v4:
time: 149 us
  blocking collectives  73.5 us (49%)
  Pallas kernels  26.2 us (18%)
  starting transfers between devices  19.7 us (13%)
  waiting for transfers between devices  18.5 us (12%)
  local copies, waits for them, and re-layouts  6.46 us (4%)
  other arithmetic  3.41 us (2%)
    all_to_all x3, blocking collectives, spread(): lax.all_to_all(jnp.broadcast_to(value[None], (size, *value.shape)), axis,...  56.2 us
    all_to_all x1, blocking collectives, body(): lax.all_to_all(cut, ('y', 'z'), 0, 0).astype(F32)  17.3 us
    pallas_call x1, Pallas kernels, forward(): pl.pallas_call(forward_kernel, name='forward', out_shape=(shape(by_clade,...  12.3 us
    all_to_all x2, starting transfers between devices, spread(): lax.all_to_all(jnp.broadcast_to(value[None], (size, *value.shape)), axis,...  11.8 us
    pallas_call x1, Pallas kernels, backward(): pl.pallas_call(functools.partial(backward_kernel, records), name='backwar...  11.5 us
    all_to_all x2, waiting for transfers between devices, spread(): lax.all_to_all(jnp.broadcast_to(value[None], (size, *value.shape)), axis,...  8.79 us
    all_to_all x1, waiting for transfers between devices, body(): trunk = jnp.sum(lax.all_to_all(trunk, ('c', 'x'), 0, 0).astype(F32), axis=0)  8.43 us
    all_to_all x1, starting transfers between devices, body(): trunk = jnp.sum(lax.all_to_all(trunk, ('c', 'x'), 0, 0).astype(F32), axis=0)  3.97 us
  transfers between devices with their start and end apart: 5, of which 4 were waited for; matrix products, arithmetic and copies ran while one was open for 3% of the time, Pallas kernels for 0%

profile of v4, /device:TPU:1, one launch (start us, length us, event | category | flops | bytes accessed | tf_op | source)
XLA Modules:
  0.0 148.6 jit_solution(8744608412470949417)
XLA Ops:
  0.6 1.6 %broadcast_in_dim.13 = bf16[4,128,256]{2,1,0:T(8,128)(2,1)} broadcast(bf16[128,256]{1,0:T(8,128)(2,1)} %param.10), dimensions={1,2} | broadcast | bytes 327680 | tf_op jit(solution)/shard_map/broadcast_in_dim | solution.py:384
  2.2 4.8 %all-to-all-start = ((bf16[4,128,256]{2,1,0:T(8,128)(2,1)}), bf16[4,128,256]{2,1,0:T(8,128)(2,1)S(1)}, u32[]{:S(2)}, u32[]{:S(2)}) async-start(bf16[4,128,256]{2,1,0:T(8,128)(2,1)} %broadcast_in_dim.13), calls=%async_computation | async-start | bytes 524288 | tf_op jit(solution)/shard_map/all_to_all | solution.py:384
  7.0 1.0 compare_reduce_fusion.3
  8.1 0.1 bitcast_reduce_fusion.2
  8.2 0.1 bitcast_reduce_fusion
  8.3 0.1 copy.30
  8.4 0.1 reshape.77
  8.5 1.3 concatenate.17.scalars
  9.8 2.8 %all-to-all-done = bf16[4,128,256]{2,1,0:T(8,128)(2,1)S(1)} async-done(((bf16[4,128,256]{2,1,0:T(8,128)(2,1)}), bf16[4,128,256]{2,1,0:T(8,128)(2,1)S(1)}, u32[]{:S(2)}, u32[]{:S(2)}) %all-to-all-start) | async-done | bytes 262176 | tf_op jit(solution)/shard_map/all_to_all | solution.py:384
  12.6 0.0 copy-start
  12.6 0.7 copy-done
  13.3 12.3 %forward.1 = (f32[20,512,128]{2,1,0:T(8,128)}, bf16[20,512,128]{2,1,0:T(8,128)(2,1)}, bf16[4,8,512,128]{3,2,1,0:T(8,128)(2,1)}, f32[20,128]{1,0:T(8,128)}, f32[20,128]{1,0:T(8,128)}) custom-call(s32[118]{0:T(128)} %concatenate.17.scalars, bf16[512,256]{1,0:T(8,128)(2,1)} %bitcast.35, bf16[8,128,128]{2,1,0:T(8,128)(2,1)} %first_weight_in.1, ...), custom_call_target="tpu_custom_call" | custom-call | tf_op jit(solution)/shard_map/forward/pallas_call | solution.py:408
  25.5 0.7 broadcast_in_dim.14
  26.3 14.2 %all_to_all.35 = f32[8,20,128]{2,1,0:T(8,128)S(1)} all-to-all(f32[8,20,128]{2,1,0:T(8,128)S(1)} %broadcast_in_dim.14), channel_id=1, replica_groups=mesh['y'=8,'z'=8,'c'=2,'x'=4] {'y'}, dimensions={0} | all-to-all | bytes 163840 | tf_op jit(solution)/shard_map/all_to_all | solution.py:384
  40.5 24.6 %all_to_all.36 = f32[16,20,128]{2,1,0:T(8,128)S(1)} all-to-all(f32[16,20,128]{2,1,0:T(8,128)S(1)} %broadcast_in_dim.15), channel_id=1, replica_groups=mesh['y'=8,'z'=8,'c'=2,'x'=4] {'z','c'}, dimensions={0} | all-to-all | bytes 327680 | tf_op jit(solution)/shard_map/all_to_all | solution.py:384
  65.2 0.6 log_add_fusion.lse_in.lse
  65.8 11.5 %backward.1 = (bf16[8,264,128]{2,1,0:T(8,128)(2,1)}, f32[656,128]{1,0:T(8,128)}, f32[656,128]{1,0:T(8,128)}) custom-call(s32[118]{0:T(128)} %concatenate.17.scalars, bf16[512,256]{1,0:T(8,128)(2,1)} %bitcast.36, bf16[8,128,128]{2,1,0:T(8,128)(2,1)} %second_weight_in.3, bf16[20,64,128]{2,1,0:T(8,128)(2,1)} %head_weight_in.3, ...), custom_call_target="tpu_custom_call" | custom-call | tf_op jit(solution)/shard_map/backward/pallas_call | solution.py:462
  77.3 1.9 %collective-permute-start = (f32[656,128]{1,0:T(8,128)}, f32[656,128]{1,0:T(8,128)S(1)}, u32[]{:S(2)}, u32[]{:S(2)}) collective-permute-start(f32[656,128]{1,0:T(8,128)} %get-tuple-element.27), channel_id=1, source_target_pairs={{0,4},{4,0},{1,5},{5,1},{2,6},{6,2},{3,7},{7,3},{8,12},{12,8},{9,1... | collective-permute-start | bytes 1007624 | tf_op jit(solution)/shard_map/ppermute | solution.py:564
  79.2 4.0 %all-to-all-start.3 = ((bf16[8,264,128]{2,1,0:T(8,128)(2,1)}), bf16[8,264,128]{2,1,0:T(8,128)(2,1)S(1)}, u32[]{:S(2)}, u32[]{:S(2)}) async-start(bf16[8,264,128]{2,1,0:T(8,128)(2,1)} %get-tuple-element.25), calls=%async_computation.3 | async-start | bytes 1081344 | tf_op jit(solution)/shard_map/all_to_all | solution.py:565
  83.2 0.0 collective-permute-done
  83.2 1.0 add_convert_fusion
  84.2 0.1 reshape.71
  84.3 8.4 %all-to-all-done.3 = bf16[8,264,128]{2,1,0:T(8,128)(2,1)S(1)} async-done(((bf16[8,264,128]{2,1,0:T(8,128)(2,1)}), bf16[8,264,128]{2,1,0:T(8,128)(2,1)S(1)}, u32[]{:S(2)}, u32[]{:S(2)}) %all-to-all-start.3) | async-done | bytes 540704 | tf_op jit(solution)/shard_map/all_to_all | solution.py:565
  92.7 0.1 reduce.9
  92.9 0.2 fusion.5
  93.1 17.3 %all_to_all.37 = bf16[64,16,128]{2,1,0:T(8,128)(2,1)S(1)} all-to-all(bf16[64,16,128]{2,1,0:T(8,128)(2,1)S(1)} %fusion.5), channel_id=1, replica_groups=mesh['y'=8,'z'=8,'c'=2,'x'=4] {'y','z'}, dimensions={0} | all-to-all | bytes 524288 | tf_op jit(solution)/shard_map/all_to_all | solution.py:579
  110.3 0.1 reduce_sum.42
  110.4 17.5 %all_to_all.38 = bf16[64,16,128]{2,1,0:T(8,128)(2,1)S(1)} all-to-all(bf16[64,16,128]{2,1,0:T(8,128)(2,1)S(1)} %broadcast_in_dim.17), channel_id=1, replica_groups=mesh['y'=8,'z'=8,'c'=2,'x'=4] {'y','z'}, dimensions={0} | all-to-all | bytes 524288 | tf_op jit(solution)/shard_map/all_to_all | solution.py:384
  128.0 0.9 broadcast_in_dim.18
  128.8 7.0 %all-to-all-start.6 = ((bf16[8,264,128]{2,1,0:T(8,128)(2,1)}), bf16[8,264,128]{2,1,0:T(8,128)(2,1)S(1)}, u32[]{:S(2)}, u32[]{:S(2)}) async-start(bf16[8,264,128]{2,1,0:T(8,128)(2,1)} %broadcast_in_dim.18), calls=%async_computation.6 | async-start | bytes 1081344 | tf_op jit(solution)/shard_map/all_to_all | solution.py:384
  135.8 0.1 slice.55
  135.9 0.1 reshape.73
  136.0 0.0 copy-start.2
  136.0 2.0 %collective-permute-start.1 = (bf16[656,128]{1,0:T(8,128)(2,1)S(1)}, bf16[656,128]{1,0:T(8,128)(2,1)S(1)}, u32[]{:S(2)}, u32[]{:S(2)}) collective-permute-start(bf16[656,128]{1,0:T(8,128)(2,1)S(1)} %fusion.6.own), channel_id=1, source_target_pairs={{0,4},{4,0},{1,5},{5,1},{2,6},{6,2},{3,7},{7,3},{8,12},{12,8},{9,1... | collective-permute-start | bytes 503816 | tf_op jit(solution)/shard_map/ppermute | solution.py:589
  138.0 1.3 collective-permute-done.1.other
  139.3 0.0 copy-start.3
  139.3 6.0 %all-to-all-done.6.trunk = bf16[8,264,128]{2,1,0:T(8,128)(2,1)S(1)} async-done(((bf16[8,264,128]{2,1,0:T(8,128)(2,1)}), bf16[8,264,128]{2,1,0:T(8,128)(2,1)S(1)}, u32[]{:S(2)}, u32[]{:S(2)}) %all-to-all-start.6) | async-done | bytes 540704 | tf_op jit(solution)/shard_map/all_to_all | solution.py:384
  145.4 0.0 copy-done.2
  145.4 0.0 copy-done.3
  145.4 0.0 copy-start.1
  145.4 0.8 copy-done.1
  146.2 2.4 %finish.1 = (f32[20,128]{1,0:T(8,128)}, f32[20,64,128]{2,1,0:T(8,128)}, f32[8,128,128]{2,1,0:T(8,128)}, f32[8,128]{1,0:T(8,128)}, f32[8,128,128]{2,1,0:T(8,128)}, /*index=5*/f32[8,128]{1,0:T(8,128)}) custom-call(s32[118]{0:T(128)} %concatenate.17.scalars, bf16[8,264,128]{2,1,0:T(8,128)(2,1)} %copy-done.1, bf16[656,128]{1,0:T(8,128)(2,1)} %copy-done.2, ...), custom_call_target="tpu_custom_call" | custom-call | tf_op jit(solution)/shard_map/finish/pallas_call | solution.py:599
  (21 shorter events, 0.3 us)
Async XLA Ops:
  2.2 10.4 %all-to-all-start = ((bf16[4,128,256]{2,1,0:T(8,128)(2,1)}), bf16[4,128,256]{2,1,0:T(8,128)(2,1)S(1)}, u32[]{:S(2)}, u32[]{:S(2)}) async-start(bf16[4,128,256]{2,1,0:T(8,128)(2,1)} %broadcast_in_dim.13), calls=%async_computation | async-start | bytes 524288 | tf_op jit(solution)/shard_map/all_to_all | solution.py:384
  12.6 0.7 copy-start
  77.3 5.9 %collective-permute-start = (f32[656,128]{1,0:T(8,128)}, f32[656,128]{1,0:T(8,128)S(1)}, u32[]{:S(2)}, u32[]{:S(2)}) collective-permute-start(f32[656,128]{1,0:T(8,128)} %get-tuple-element.27), channel_id=1, source_target_pairs={{0,4},{4,0},{1,5},{5,1},{2,6},{6,2},{3,7},{7,3},{8,12},{12,8},{9,1... | collective-permute-start | bytes 1007624 | tf_op jit(solution)/shard_map/ppermute | solution.py:564
  79.2 13.5 %all-to-all-start.3 = ((bf16[8,264,128]{2,1,0:T(8,128)(2,1)}), bf16[8,264,128]{2,1,0:T(8,128)(2,1)S(1)}, u32[]{:S(2)}, u32[]{:S(2)}) async-start(bf16[8,264,128]{2,1,0:T(8,128)(2,1)} %get-tuple-element.25), calls=%async_computation.3 | async-start | bytes 1081344 | tf_op jit(solution)/shard_map/all_to_all | solution.py:565
  128.8 16.5 %all-to-all-start.6 = ((bf16[8,264,128]{2,1,0:T(8,128)(2,1)}), bf16[8,264,128]{2,1,0:T(8,128)(2,1)S(1)}, u32[]{:S(2)}, u32[]{:S(2)}) async-start(bf16[8,264,128]{2,1,0:T(8,128)(2,1)} %broadcast_in_dim.18), calls=%async_computation.6 | async-start | bytes 1081344 | tf_op jit(solution)/shard_map/all_to_all | solution.py:384
  136.0 9.3 %copy-start.2 = (bf16[656,128]{1,0:T(8,128)(2,1)}, bf16[656,128]{1,0:T(8,128)(2,1)S(1)}, u32[]{:S(2)}) copy-start(bf16[656,128]{1,0:T(8,128)(2,1)S(1)} %fusion.6.own) | copy-start | bytes 503812
  136.0 3.3 %collective-permute-start.1 = (bf16[656,128]{1,0:T(8,128)(2,1)S(1)}, bf16[656,128]{1,0:T(8,128)(2,1)S(1)}, u32[]{:S(2)}, u32[]{:S(2)}) collective-permute-start(bf16[656,128]{1,0:T(8,128)(2,1)S(1)} %fusion.6.own), channel_id=1, source_target_pairs={{0,4},{4,0},{1,5},{5,1},{2,6},{6,2},{3,7},{7,3},{8,12},{12,8},{9,1... | collective-permute-start | bytes 503816 | tf_op jit(solution)/shard_map/ppermute | solution.py:589
  139.3 6.0 %copy-start.3 = (bf16[656,128]{1,0:T(8,128)(2,1)}, bf16[656,128]{1,0:T(8,128)(2,1)S(1)}, u32[]{:S(2)}) copy-start(bf16[656,128]{1,0:T(8,128)(2,1)S(1)} %collective-permute-done.1.other) | copy-start | bytes 503812
  145.4 0.8 copy-start.1

commit v5 on v4

--- a/solution.py
+++ b/solution.py
@@ -159,7 +159,9 @@
             b = i * GROUP + g
             top = jnp.max(tops[g], axis=0, keepdims=True)
             total = jnp.sum(jnp.exp(logits[b] - top), axis=0, keepdims=True)
-            local_lse[pl.ds(b, 1), :] = top + jnp.log(total)
+            spread_lse = top + jnp.log(total)
+            for peer in range(local_lse.shape[0]):
+                local_lse[peer, pl.ds(b, 1), :] = spread_lse
         return carry
 
     logit_copies = []
@@ -186,6 +188,11 @@
     for copy in logit_copies:
         copy.wait()
     trunk_copy.wait()
+
+
+def join(parts):
+    top = functools.reduce(jnp.maximum, [parts[i] for i in range(len(parts))])
+    return top + jnp.log(sum(jnp.exp(parts[i] - top) for i in range(len(parts))))
 
 
 def backward_kernel(
@@ -197,15 +204,15 @@
     logits_in,
     hits_in,
     trunk_in,
-    lse_in,
+    lses_in,
     hit_sum_in,
-    trunk,
     keep,
     send,
+    lse,
     covariates,
     second_weight,
     head_weight,
-    lse,
+    lses,
     hit_sum,
     logits,
     hits,
@@ -220,6 +227,7 @@
     slab_grad,
     group_back,
     act_grad,
+    out_sem,
     fetch_sem,
     logit_sem,
     hit_sem,
@@ -248,7 +256,7 @@
         fetch_sem,
         (head_weight_in, head_weight),
         (covariates_in, covariates),
-        (lse_in, lse),
+        (lses_in, lses),
         (hit_sum_in, hit_sum),
         (second_weight_in, second_weight),
     )
@@ -279,6 +287,7 @@
         return carry
 
     fetched[2].wait()
+    lse[...] = join([lses[i] for i in range(lses.shape[0])])
     for i, copy in enumerate(logit_copies):
         copy.wait()
         weigh(i, 0)
@@ -311,13 +320,22 @@
     layer_copies[1].wait()
     fetched[3].wait()
     fetched[4].wait()
+    head_rows = group * slab
+    trunk_at = head_rows + -(-group // 8) * 8
+    parts = bias.shape[1]
+    pair = blocks // parts
+    part_rows = pair * tile + 8
+    for half in range(2):
+        packed[half, head_rows:trunk_at, :] = jnp.zeros((trunk_at - head_rows, tile), F32)
+        sums = hit_sum[half * group : (half + 1) * group, :]
+        packed[half, head_rows : head_rows + group, :] = sums
     bias[...] = jnp.zeros_like(bias)
-    pair = blocks // (trunk.shape[0] // 2)
 
     def trunk_sums(o, layer, left, dz):
-        part, at = layer * (trunk.shape[0] // 2) + o // pair, o % pair
-        trunk[part, at * tile : (at + 1) * tile, :] = dot(left, dz).astype(LINK)
-        bias[part, at : at + 1, :] = jnp.sum(dz.astype(F32), axis=0, keepdims=True)
+        part, at = o // pair, o % pair
+        start = trunk_at + part * part_rows + at * tile
+        packed[layer, start : start + tile, :] = dot(left, dz)
+        bias[layer, part, at : at + 1, :] = jnp.sum(dz.astype(F32), axis=0, keepdims=True)
 
     for o in range(blocks):
         dz = (group_back[o] * second_slope[o].astype(F32)).astype(BF16)
@@ -326,22 +344,21 @@
     for o in range(blocks):
         dz = (act_grad[o] * first_slope[o].astype(F32)).astype(BF16)
         trunk_sums(o, 0, covariates_t[first_index[o]], dz)
-    for part in range(trunk.shape[0]):
-        trunk[part, pair * tile :, :] = bias[part].astype(LINK)
-
-    tail = group * slab
-    for half in range(2):
-        packed[half, tail:, :] = jnp.zeros((packed.shape[1] - tail, tile), F32)
-        packed[half, tail : tail + group, :] = hit_sum[half * group : (half + 1) * group, :]
-    keep[...] = packed[core]
-    send[...] = packed[1 - core]
+    for layer in range(2):
+        for part in range(parts):
+            start = trunk_at + (part + 1) * part_rows
+            packed[layer, start - 8 : start, :] = bias[layer, part]
+    out = fetch(out_sem, (packed.at[1 - core], send), (packed.at[core], keep))
+    for copy in out:
+        copy.wait()
 
 
 def finish_kernel(
     total_cells,
     records,
     scalars,
-    trunk,
+    own_trunk,
+    other_trunk,
     own,
     other,
     lse,
@@ -352,6 +369,7 @@
     second_grad,
     second_bias_grad,
     halves,
+    trunk,
 ):
     core = scalars[1]
     blocks, tile, _ = first_grad.shape
@@ -359,6 +377,8 @@
     group = block_count // 2
     halves[core] = own[...]
     halves[1 - core] = other[...]
+    trunk[core] = own_trunk[...]
+    trunk[1 - core] = other_trunk[...]
     for b in range(block_count):
         rows = slice((b % group) * slab, (b % group + 1) * slab)
         head_grad[b] = halves[b // group, rows, :].astype(F32)
@@ -367,16 +387,16 @@
         rows = slice(half * group, (half + 1) * group)
         hit_mean = halves[half, tail:, :].astype(F32)[:group] * (1.0 / records)
         species_loss[rows, :] = lse[rows, :] - math.log(total_cells) - hit_mean
-    half = trunk.shape[0] // 2
-    pair = blocks // half
+    parts = trunk.shape[1]
+    pair = blocks // parts
     for layer, (grad, bias_grad) in enumerate(
         ((first_grad, first_bias_grad), (second_grad, second_bias_grad))
     ):
-        for part in range(half):
+        for part in range(parts):
             for at in range(pair):
                 rows = slice(at * tile, (at + 1) * tile)
-                grad[part * pair + at] = trunk[layer * half + part, rows, :].astype(F32)
-            bias = trunk[layer * half + part, pair * tile :, :].astype(F32)
+                grad[part * pair + at] = trunk[layer, part, rows, :].astype(F32)
+            bias = trunk[layer, part, pair * tile :, :].astype(F32)
             bias_grad[part * pair : (part + 1) * pair, :] = bias[:pair]
 
 
@@ -384,12 +404,8 @@
     return lax.all_to_all(jnp.broadcast_to(value[None], (size, *value.shape)), axis, 0, 0)
 
 
-def join(parts):
-    top = jnp.max(parts, axis=0)
-    return top + jnp.log(jnp.sum(jnp.exp(parts - top), axis=0))
-
-
 def forward(
+    peers,
     scalars,
     covariates,
     first_weight,
@@ -412,10 +428,10 @@
             shape(by_clade, F32),
             shape(by_clade, BF16),
             shape(by_layer, BF16),
-            shape((block_count, species), F32),
+            shape((peers, block_count, species), F32),
             shape((block_count, species), F32),
         ),
-        in_specs=[SMEM] + [ANY] * 7,
+        in_specs=[SMEM] + [ANY] + [ANY] * 6,
         out_specs=[ANY] * 3 + [VMEM] * 2,
         scratch_shapes=[
             pltpu.VMEM(covariates.shape, BF16),
@@ -456,19 +472,18 @@
     width = covariates.shape[1]
     shape = jax.ShapeDtypeStruct
     pair = blocks // nx
-    part_rows = pair * tile + 8
     group = block_count // 2
-    half_rows = group * slab + -(-group // 8) * 8
+    rows = group * slab + -(-group // 8) * 8 + nx * (pair * tile + 8)
     return pl.pallas_call(
         functools.partial(backward_kernel, records),
         name="backward",
         out_shape=(
-            shape((2 * nx, part_rows, tile), LINK),
-            shape((half_rows, tile), F32),
-            shape((half_rows, tile), F32),
+            shape((rows, tile), F32),
+            shape((rows, tile), F32),
+            shape((block_count, species), F32),
         ),
-        in_specs=[SMEM] + [ANY] * 8,
-        out_specs=[VMEM] * 3,
+        in_specs=[SMEM, ANY, ANY, ANY, ANY, ANY, ANY, ANY, ANY],
+        out_specs=[ANY, ANY, VMEM],
         scratch_shapes=[
             pltpu.VMEM(covariates.shape, BF16),
             pltpu.VMEM(second_weight.shape, BF16),
@@ -479,8 +494,8 @@
             pltpu.VMEM(hits.shape, BF16),
             pltpu.VMEM(layers.shape, BF16),
             pltpu.VMEM((block_count, tile, species), BF16),
-            pltpu.VMEM((2, half_rows, tile), F32),
-            pltpu.VMEM((2 * nx, 8, tile), F32),
+            pltpu.VMEM((2, rows, tile), F32),
+            pltpu.VMEM((2, nx, 8, tile), F32),
             pltpu.VMEM((blocks, tile, cells), BF16),
             pltpu.VMEM((blocks, tile, cells), BF16),
             pltpu.VMEM((width // tile, tile, cells), BF16),
@@ -488,6 +503,7 @@
             pltpu.VMEM((GROUP, tile, species), F32),
             pltpu.VMEM(by_block, F32),
             pltpu.VMEM(by_block, F32),
+            pltpu.SemaphoreType.DMA((2,)),
             pltpu.SemaphoreType.DMA((5,)),
             pltpu.SemaphoreType.DMA((block_count // GROUP,)),
             pltpu.SemaphoreType.DMA((1,)),
@@ -542,6 +558,7 @@
 
     all_covariates = spread(covariates, "x", nx).reshape(cells, width)
     saved = forward(
+        ny,
         scalars,
         all_covariates,
         first_weight,
@@ -551,18 +568,20 @@
         head_weight,
         presence_t,
     )
-    lse = join(spread(saved[3], "y", ny))
-    lse = join(spread(lse, ("z", "c"), nz * 2))
-
-    trunk, keep, send = backward(
+    lse = join(lax.all_to_all(saved[3], "y", 0, 0))
+    lse = spread(lse, ("z", "c"), nz * 2)
+
+    keep, send, lse = backward(
         records, scalars, all_covariates, second_weight, head_weight, saved, lse, nx
     )
     pair, group = blocks // nx, block_count // 2
     head_rows = group * slab
-    half_rows = keep.shape[0]
-
-    head = keep + lax.ppermute(send, "c", swap)
-    trunk = jnp.sum(lax.all_to_all(trunk, ("c", "x"), 0, 0).astype(F32), axis=0)
+    half_rows = head_rows + -(-group // 8) * 8
+
+    other = lax.ppermute(send, "c", swap)
+    trunk = (keep[half_rows:] + other[half_rows:]).astype(LINK).reshape(nx, -1, tile)
+    trunk = jnp.sum(lax.all_to_all(trunk, "x", 0, 0).astype(F32), axis=0)
+    head = keep[:half_rows] + other[:half_rows]
     peers = ny * nz
     misc = jnp.concatenate([head[head_rows : head_rows + group], trunk[pair * tile :][:pair]])
     misc = jnp.pad(misc, ((0, peers - misc.shape[0]), (0, 0)))
@@ -593,7 +612,8 @@
             jnp.pad(misc[group : group + pair], ((0, -pair % 8), (0, 0))),
         ]
     )
-    trunk = spread(trunk, ("c", "x"), 2 * nx)
+    trunk = spread(trunk, "x", nx)
+    other_trunk = lax.ppermute(trunk, "c", swap)
     shape = jax.ShapeDtypeStruct
     species_loss, head_grad, first_grad, first_bias_grad, second_grad, second_bias_grad = (
         pl.pallas_call(
@@ -607,11 +627,14 @@
                 shape(second_weight.shape, F32),
                 shape((blocks, tile), F32),
             ),
-            in_specs=[SMEM] + [VMEM] * 4,
+            in_specs=[SMEM] + [VMEM] * 5,
             out_specs=[VMEM] * 6,
-            scratch_shapes=[pltpu.VMEM((2, half_rows, tile), LINK)],
-            compiler_params=PARAMS,
-        )(scalars, trunk, head, other_head, lse)
+            scratch_shapes=[
+                pltpu.VMEM((2, half_rows, tile), LINK),
+                pltpu.VMEM((2, *trunk.shape), LINK),
+            ],
+            compiler_params=pltpu.CompilerParams(vmem_limit_bytes=16 << 20),
+        )(scalars, trunk, other_trunk, head, other_head, lse)
     )
     return (
         species_loss.reshape(-1),

time: 149 us -> 151 us (1.013)
  starting transfers between devices: 19.7 us -> 22.1 us
  local copies, waits for them, and re-layouts: 6.46 us -> 4.84 us
    all_to_all x0 -> x1, blocking collectives: none -> 14.4 us  [body(): lse = join(lax.all_to_all(saved[3], 'y', 0, 0))]
    all_to_all x3 -> x2, blocking collectives: 56.2 us -> 42.7 us  [spread(): lax.all_to_all(jnp.broadcast_to(value[None], (size, *value.shape)), axis,...]
    ppermute x1 -> x2, starting transfers between devices: 1.92 us -> 8.42 us  [the longest x1 6.5 us: body(): other_trunk = lax.ppermute(trunk, 'c', swap)]
    all_to_all x2, starting transfers between devices: 11.8 us -> 8.29 us  [spread(): lax.all_to_all(jnp.broadcast_to(value[None], (size, *value.shape)), axis,...]
    all_to_all x1, waiting for transfers between devices: 8.43 us -> 5.6 us  [body(): trunk = jnp.sum(lax.all_to_all(trunk, 'x', 0, 0).astype(F32), axis=0)]
    ppermute x1 -> x2, waiting for transfers between devices: 0.01 us -> 2.59 us  [the longest x1 2.59 us: body(): other = lax.ppermute(send, 'c', swap)]
    convert_element_type x0 -> x1, other arithmetic: none -> 1.87 us  [body(): (keep[half_rows:] + other[half_rows:]).astype(LINK).reshape(nx, -1, tile)]
    broadcast_in_dim x5 -> x4, local copies, waits for them, and re-layouts: 3.2 us -> 2.35 us  [spread(): jnp.broadcast_to(value[None], (size, *value.shape))]
  transfers between devices with their start and end apart: 5 -> 6, of which waited for: 4 -> 5; matrix products, arithmetic and copies ran while one was open for 3% -> 3% of each run, Pallas kernels for 0% -> 0%
where the time goes in v5:
time: 151 us; the launch traced here: 150 us
  blocking collectives  73.7 us (49%)
  Pallas kernels  26.3 us (17%)
  starting transfers between devices  22.1 us (15%)
  waiting for transfers between devices  17.6 us (12%)
  local copies, waits for them, and re-layouts  4.84 us (3%)
  other arithmetic  4.58 us (3%)
    all_to_all x2, blocking collectives, spread(): lax.all_to_all(jnp.broadcast_to(value[None], (size, *value.shape)), axis,...  42.7 us
    all_to_all x1, blocking collectives, body(): lax.all_to_all(cut, ('y', 'z'), 0, 0).astype(F32)  16.6 us
    all_to_all x1, blocking collectives, body(): lse = join(lax.all_to_all(saved[3], 'y', 0, 0))  14.4 us
    pallas_call x1, Pallas kernels, backward(): pl.pallas_call(functools.partial(backward_kernel, records), name='backwar...  12.5 us
    pallas_call x1, Pallas kernels, forward(): pl.pallas_call(forward_kernel, name='forward', out_shape=(shape(by_clade,...  12 us
    all_to_all x2, starting transfers between devices, spread(): lax.all_to_all(jnp.broadcast_to(value[None], (size, *value.shape)), axis,...  8.29 us
    all_to_all x2, waiting for transfers between devices, spread(): lax.all_to_all(jnp.broadcast_to(value[None], (size, *value.shape)), axis,...  8.09 us
    ppermute x1, starting transfers between devices, body(): other_trunk = lax.ppermute(trunk, 'c', swap)  6.5 us
  transfers between devices with their start and end apart: 6, of which 5 were waited for; matrix products, arithmetic and copies ran while one was open for 3% of the time, Pallas kernels for 0%

profile of v5, /device:TPU:1, one launch (start us, length us, event | category | flops | bytes accessed | tf_op | source)
XLA Modules:
  0.0 150.0 jit_solution(1071592508862095070)
XLA Ops:
  0.6 1.6 %broadcast_in_dim.13 = bf16[4,128,256]{2,1,0:T(8,128)(2,1)} broadcast(bf16[128,256]{1,0:T(8,128)(2,1)} %param.10), dimensions={1,2} | broadcast | bytes 327680 | tf_op jit(solution)/shard_map/broadcast_in_dim | solution.py:404
  2.2 4.8 %all-to-all-start = ((bf16[4,128,256]{2,1,0:T(8,128)(2,1)}), bf16[4,128,256]{2,1,0:T(8,128)(2,1)S(1)}, u32[]{:S(2)}, u32[]{:S(2)}) async-start(bf16[4,128,256]{2,1,0:T(8,128)(2,1)} %broadcast_in_dim.13), calls=%async_computation | async-start | bytes 524288 | tf_op jit(solution)/shard_map/all_to_all | solution.py:404
  7.0 1.0 compare_reduce_fusion.3
  8.1 0.1 bitcast_reduce_fusion.2
  8.2 0.1 bitcast_reduce_fusion
  8.3 0.1 copy.26
  8.4 0.1 reshape.72
  8.5 1.3 concatenate.17.scalars
  9.8 2.7 %all-to-all-done = bf16[4,128,256]{2,1,0:T(8,128)(2,1)S(1)} async-done(((bf16[4,128,256]{2,1,0:T(8,128)(2,1)}), bf16[4,128,256]{2,1,0:T(8,128)(2,1)S(1)}, u32[]{:S(2)}, u32[]{:S(2)}) %all-to-all-start) | async-done | bytes 262176 | tf_op jit(solution)/shard_map/all_to_all | solution.py:404
  12.6 0.0 copy-start.2
  12.6 0.7 copy-done.2
  13.3 12.0 %forward.1 = (f32[20,512,128]{2,1,0:T(8,128)}, bf16[20,512,128]{2,1,0:T(8,128)(2,1)}, bf16[4,8,512,128]{3,2,1,0:T(8,128)(2,1)}, f32[8,20,128]{2,1,0:T(8,128)}, f32[20,128]{1,0:T(8,128)}) custom-call(s32[118]{0:T(128)} %concatenate.17.scalars, bf16[512,256]{1,0:T(8,128)(2,1)} %bitcast.38, bf16[8,128,128]{2,1,0:T(8,128)(2,1)} %first_weight_in.1, ...), custom_call_target="tpu_custom_call" | custom-call | tf_op jit(solution)/shard_map/forward/pallas_call | solution.py:424
  25.3 14.4 %all_to_all.35 = f32[8,20,128]{2,1,0:T(8,128)S(1)} all-to-all(f32[8,20,128]{2,1,0:T(8,128)} %get-tuple-element.23), channel_id=1, replica_groups=mesh['y'=8,'z'=8,'c'=2,'x'=4] {'y'}, dimensions={0} | all-to-all | bytes 163840 | tf_op jit(solution)/shard_map/all_to_all | solution.py:571
  39.8 24.8 %all_to_all.36.lses_in = f32[16,20,128]{2,1,0:T(8,128)} all-to-all(f32[16,20,128]{2,1,0:T(8,128)S(1)} %broadcast_in_dim.15), channel_id=1, replica_groups=mesh['y'=8,'z'=8,'c'=2,'x'=4] {'z','c'}, dimensions={0} | all-to-all | bytes 327680 | tf_op jit(solution)/shard_map/all_to_all | solution.py:404
  64.5 12.5 %backward.1 = (f32[1712,128]{1,0:T(8,128)}, f32[1712,128]{1,0:T(8,128)}, f32[20,128]{1,0:T(8,128)}) custom-call(s32[118]{0:T(128)} %concatenate.17.scalars, bf16[512,256]{1,0:T(8,128)(2,1)} %bitcast.39, bf16[8,128,128]{2,1,0:T(8,128)(2,1)} %second_weight_in.3, bf16[20,64,128]{2,1,0:T(8,128)(2,1)} %head_weight_in.3, ...), custom_call_target="tpu_custom_call" | custom-call | tf_op jit(solution)/shard_map/backward/pallas_call | solution.py:477
  77.0 1.9 %collective-permute-start = (f32[1712,128]{1,0:T(8,128)}, f32[1712,128]{1,0:T(8,128)S(1)}, u32[]{:S(2)}, u32[]{:S(2)}) collective-permute-start(f32[1712,128]{1,0:T(8,128)} %get-tuple-element.26), channel_id=1, source_target_pairs={{0,4},{4,0},{1,5},{5,1},{2,6},{6,2},{3,7},{7,3},{8,12},{12,8},{9,1... | collective-permute-start | bytes 2629640 | tf_op jit(solution)/shard_map/ppermute | solution.py:581
  79.0 2.6 %collective-permute-done = f32[1712,128]{1,0:T(8,128)S(1)} collective-permute-done((f32[1712,128]{1,0:T(8,128)}, f32[1712,128]{1,0:T(8,128)S(1)}, u32[]{:S(2)}, u32[]{:S(2)}) %collective-permute-start) | collective-permute-done | bytes 876576 | tf_op jit(solution)/shard_map/ppermute | solution.py:581
  81.6 0.0 copy-start
  81.6 0.0 copy-start.1
  81.6 1.9 %fusion = bf16[1056,128]{1,0:T(8,128)(2,1)} fusion(f32[1712,128]{1,0:T(8,128)S(1)} %collective-permute-done, f32[1712,128]{1,0:T(8,128)} %get-tuple-element.25), kind=kLoop, calls=%fused_computation.1 | loop fusion | flops 270336 | bytes 1351680 | tf_op jit(solution)/shard_map/convert_element_type | solution.py:582
  83.4 3.4 %all-to-all-start.3 = ((bf16[4,264,128]{2,1,0:T(8,128)(2,1)}), bf16[4,264,128]{2,1,0:T(8,128)(2,1)S(1)}, u32[]{:S(2)}, u32[]{:S(2)}) async-start(bf16[4,264,128]{2,1,0:T(8,128)(2,1)} %bitcast.15), calls=%async_computation.3 | async-start | bytes 540672 | tf_op jit(solution)/shard_map/all_to_all | solution.py:583
  86.9 1.0 fusion.4
  88.0 0.1 reshape.66
  88.0 5.6 %all-to-all-done.3 = bf16[4,264,128]{2,1,0:T(8,128)(2,1)S(1)} async-done(((bf16[4,264,128]{2,1,0:T(8,128)(2,1)}), bf16[4,264,128]{2,1,0:T(8,128)(2,1)S(1)}, u32[]{:S(2)}, u32[]{:S(2)}) %all-to-all-start.3) | async-done | bytes 270368 | tf_op jit(solution)/shard_map/all_to_all | solution.py:583
  93.7 0.2 fusion.7
  93.9 16.6 %all_to_all.37 = bf16[64,16,128]{2,1,0:T(8,128)(2,1)S(1)} all-to-all(bf16[64,16,128]{2,1,0:T(8,128)(2,1)S(1)} %fusion.7), channel_id=1, replica_groups=mesh['y'=8,'z'=8,'c'=2,'x'=4] {'y','z'}, dimensions={0} | all-to-all | bytes 524288 | tf_op jit(solution)/shard_map/all_to_all | solution.py:598
  110.5 0.1 reduce_sum.22
  110.6 17.9 %all_to_all.38 = bf16[64,16,128]{2,1,0:T(8,128)(2,1)S(1)} all-to-all(bf16[64,16,128]{2,1,0:T(8,128)(2,1)S(1)} %broadcast_in_dim.34), channel_id=1, replica_groups=mesh['y'=8,'z'=8,'c'=2,'x'=4] {'y','z'}, dimensions={0} | all-to-all | bytes 524288 | tf_op jit(solution)/shard_map/all_to_all | solution.py:404
  128.6 0.7 broadcast_in_dim.35
  129.4 3.4 %all-to-all-start.6 = ((bf16[4,264,128]{2,1,0:T(8,128)(2,1)}), bf16[4,264,128]{2,1,0:T(8,128)(2,1)S(1)}, u32[]{:S(2)}, u32[]{:S(2)}) async-start(bf16[4,264,128]{2,1,0:T(8,128)(2,1)} %broadcast_in_dim.35), calls=%async_computation.6 | async-start | bytes 540672 | tf_op jit(solution)/shard_map/all_to_all | solution.py:404
  132.8 0.1 slice.121
  132.9 0.1 reshape.68
  133.0 5.3 %all-to-all-done.6.own_trunk = bf16[4,264,128]{2,1,0:T(8,128)(2,1)S(1)} async-done(((bf16[4,264,128]{2,1,0:T(8,128)(2,1)}), bf16[4,264,128]{2,1,0:T(8,128)(2,1)S(1)}, u32[]{:S(2)}, u32[]{:S(2)}) %all-to-all-start.6) | async-done | bytes 270368 | tf_op jit(solution)/shard_map/all_to_all | solution.py:404
  138.4 6.5 %collective-permute-start.1 = (bf16[4,264,128]{2,1,0:T(8,128)(2,1)S(1)}, bf16[4,264,128]{2,1,0:T(8,128)(2,1)S(1)}, u32[]{:S(2)}, u32[]{:S(2)}) collective-permute-start(bf16[4,264,128]{2,1,0:T(8,128)(2,1)S(1)} %all-to-all-done.6.own_trunk), channel_id=1, source_target_pairs={{0,4},{4,0},{1,5},{5,1},{2,6},{6,2},{3,7},{7,3},{8,12},{12,8},{9,1... | collective-permute-start | bytes 811016 | tf_op jit(solution)/shard_map/ppermute | solution.py:616
  144.9 1.9 %collective-permute-start.2 = (bf16[656,128]{1,0:T(8,128)(2,1)S(1)}, bf16[656,128]{1,0:T(8,128)(2,1)S(1)}, u32[]{:S(2)}, u32[]{:S(2)}) collective-permute-start(bf16[656,128]{1,0:T(8,128)(2,1)S(1)} %fusion.8.own), channel_id=1, source_target_pairs={{0,4},{4,0},{1,5},{5,1},{2,6},{6,2},{3,7},{7,3},{8,12},{12,8},{9,1... | collective-permute-start | bytes 503816 | tf_op jit(solution)/shard_map/ppermute | solution.py:608
  146.8 1.4 collective-permute-done.2.other
  148.2 0.0 collective-permute-done.1.other_trunk
  148.2 0.0 copy-done
  148.2 0.0 copy-done.1
  148.2 1.8 %finish.1 = (f32[20,128]{1,0:T(8,128)}, f32[20,64,128]{2,1,0:T(8,128)}, f32[8,128,128]{2,1,0:T(8,128)}, f32[8,128]{1,0:T(8,128)}, f32[8,128,128]{2,1,0:T(8,128)}, /*index=5*/f32[8,128]{1,0:T(8,128)}) custom-call(s32[118]{0:T(128)S(1)} %copy-done.1, bf16[4,264,128]{2,1,0:T(8,128)(2,1)S(1)} %all-to-all-done.6.own_trunk, ...), custom_call_target="tpu_custom_call" | custom-call | tf_op jit(solution)/shard_map/finish/pallas_call | solution.py:619
  (18 shorter events, 0.3 us)
Async XLA Ops:
  2.2 10.4 %all-to-all-start = ((bf16[4,128,256]{2,1,0:T(8,128)(2,1)}), bf16[4,128,256]{2,1,0:T(8,128)(2,1)S(1)}, u32[]{:S(2)}, u32[]{:S(2)}) async-start(bf16[4,128,256]{2,1,0:T(8,128)(2,1)} %broadcast_in_dim.13), calls=%async_computation | async-start | bytes 524288 | tf_op jit(solution)/shard_map/all_to_all | solution.py:404
  12.6 0.7 copy-start.2
  77.0 4.5 %collective-permute-start = (f32[1712,128]{1,0:T(8,128)}, f32[1712,128]{1,0:T(8,128)S(1)}, u32[]{:S(2)}, u32[]{:S(2)}) collective-permute-start(f32[1712,128]{1,0:T(8,128)} %get-tuple-element.26), channel_id=1, source_target_pairs={{0,4},{4,0},{1,5},{5,1},{2,6},{6,2},{3,7},{7,3},{8,12},{12,8},{9,1... | collective-permute-start | bytes 2629640 | tf_op jit(solution)/shard_map/ppermute | solution.py:581
  81.6 66.6 %copy-start = (f32[20,128]{1,0:T(8,128)S(1)}, f32[20,128]{1,0:T(8,128)}, u32[]{:S(2)}) copy-start(f32[20,128]{1,0:T(8,128)} %get-tuple-element.27.lse) | copy-start | bytes 30724
  81.6 66.6 %copy-start.1 = (s32[118]{0:T(128)S(1)}, s32[118]{0:T(128)}, u32[]{:S(2)}) copy-start(s32[118]{0:T(128)} %concatenate.17.scalars) | copy-start | bytes 1420
  83.4 10.2 %all-to-all-start.3 = ((bf16[4,264,128]{2,1,0:T(8,128)(2,1)}), bf16[4,264,128]{2,1,0:T(8,128)(2,1)S(1)}, u32[]{:S(2)}, u32[]{:S(2)}) async-start(bf16[4,264,128]{2,1,0:T(8,128)(2,1)} %bitcast.15), calls=%async_computation.3 | async-start | bytes 540672 | tf_op jit(solution)/shard_map/all_to_all | solution.py:583
  129.4 9.0 %all-to-all-start.6 = ((bf16[4,264,128]{2,1,0:T(8,128)(2,1)}), bf16[4,264,128]{2,1,0:T(8,128)(2,1)S(1)}, u32[]{:S(2)}, u32[]{:S(2)}) async-start(bf16[4,264,128]{2,1,0:T(8,128)(2,1)} %broadcast_in_dim.35), calls=%async_computation.6 | async-start | bytes 540672 | tf_op jit(solution)/shard_map/all_to_all | solution.py:404
  138.4 9.8 %collective-permute-start.1 = (bf16[4,264,128]{2,1,0:T(8,128)(2,1)S(1)}, bf16[4,264,128]{2,1,0:T(8,128)(2,1)S(1)}, u32[]{:S(2)}, u32[]{:S(2)}) collective-permute-start(bf16[4,264,128]{2,1,0:T(8,128)(2,1)S(1)} %all-to-all-done.6.own_trunk), channel_id=1, source_target_pairs={{0,4},{4,0},{1,5},{5,1},{2,6},{6,2},{3,7},{7,3},{8,12},{12,8},{9,1... | collective-permute-start | bytes 811016 | tf_op jit(solution)/shard_map/ppermute | solution.py:616
  144.9 3.3 %collective-permute-start.2 = (bf16[656,128]{1,0:T(8,128)(2,1)S(1)}, bf16[656,128]{1,0:T(8,128)(2,1)S(1)}, u32[]{:S(2)}, u32[]{:S(2)}) collective-permute-start(bf16[656,128]{1,0:T(8,128)(2,1)S(1)} %fusion.8.own), channel_id=1, source_target_pairs={{0,4},{4,0},{1,5},{5,1},{2,6},{6,2},{3,7},{7,3},{8,12},{12,8},{9,1... | collective-permute-start | bytes 503816 | tf_op jit(solution)/shard_map/ppermute | solution.py:608

commit v6 on v4

--- a/solution.py
+++ b/solution.py
@@ -88,27 +88,21 @@
     second_weight_in,
     second_bias_in,
     head_weight_in,
-    presence_in,
     logits_out,
-    hits_out,
     trunk_out,
     local_lse,
-    hit_sum,
     covariates,
     first_weight,
     first_bias,
     second_weight,
     second_bias,
     head_weight,
-    presence,
     logits,
-    hits,
     trunk,
     wide_weight,
     tops,
     fetch_sem,
     logit_sem,
-    hit_sem,
     trunk_sem,
 ):
     fetched = fetch(
@@ -119,13 +113,11 @@
         (second_weight_in, second_weight),
         (second_bias_in, second_bias),
         (head_weight_in, head_weight),
-        (presence_in, presence),
     )
     first_act, features, first_slope, second_slope = (trunk.at[i] for i in range(4))
     blocks, cells, tile = features.shape
     block_count, slab, _ = head_weight.shape
-    first_index, second_index, clade, busy, place = scalar_parts(scalars, blocks, block_count)
-    first_cell = place[0]
+    first_index, second_index, clade, _, _ = scalar_parts(scalars, blocks, block_count)
 
     def layer(pre, act_ref, slope_ref, o):
         sigma = 1.0 / (1.0 + jnp.exp(-pre))
@@ -144,9 +136,7 @@
 
     trunk_copy = pltpu.make_async_copy(trunk, trunk_out, trunk_sem.at[0])
     trunk_copy.start()
-    hit_sum[...] = jnp.zeros_like(hit_sum)
     fetched[5].wait()
-    fetched[6].wait()
     widen(wide_weight, head_weight, clade)
 
     def step(i, carry):
@@ -159,7 +149,9 @@
             b = i * GROUP + g
             top = jnp.max(tops[g], axis=0, keepdims=True)
             total = jnp.sum(jnp.exp(logits[b] - top), axis=0, keepdims=True)
-            local_lse[pl.ds(b, 1), :] = top + jnp.log(total)
+            lse = top + jnp.log(total)
+            for peer in range(local_lse.shape[0]):
+                local_lse[peer, pl.ds(b, 1), :] = lse
         return carry
 
     logit_copies = []
@@ -171,6 +163,82 @@
         )
         logit_copies[i].start()
 
+    for copy in logit_copies:
+        copy.wait()
+    trunk_copy.wait()
+
+
+def join(parts):
+    top = functools.reduce(jnp.maximum, [parts[i] for i in range(len(parts))])
+    return top + jnp.log(sum(jnp.exp(parts[i] - top) for i in range(len(parts))))
+
+
+def middle_kernel(
+    scalars,
+    covariates_in,
+    presence_in,
+    local_lse_in,
+    trunk_in,
+    logits_in,
+    hits_out,
+    covariates_t_out,
+    first_act_t_out,
+    soft_grad,
+    hit_grad,
+    hit_sum,
+    covariates,
+    presence,
+    local_lse,
+    trunk,
+    logits,
+    hits,
+    covariates_t,
+    first_act_t,
+    features_t,
+    weight_cells,
+    product,
+    fetch_sem,
+    logit_sem,
+    out_sem,
+):
+    _, blocks, cells, tile = trunk.shape
+    block_count, slab, _ = soft_grad.shape
+    _, _, clade, busy, place = scalar_parts(scalars, blocks, block_count)
+    first_cell = place[0]
+    fetched = fetch(
+        fetch_sem,
+        (trunk_in.at[pl.ds(0, 2)], trunk),
+        (local_lse_in.at[0], local_lse),
+        (covariates_in, covariates),
+        (presence_in, presence),
+    )
+    pieces = [pl.ds(i * GROUP, GROUP) for i in range(block_count // GROUP)]
+    logit_copies = fetch(logit_sem, *[(logits_in.at[p], logits.at[p]) for p in pieces])
+    hit_sum[...] = jnp.zeros_like(hit_sum)
+    hit_grad[...] = jnp.zeros_like(hit_grad)
+    fetched[0].wait()
+    for o in range(blocks):
+        first_act_t[o] = trunk[0, o].T
+        features_t[o] = trunk[1, o].T
+    fetched[1].wait()
+    fetched[2].wait()
+    for o in range(covariates.shape[1] // tile):
+        covariates_t[o] = covariates[:, o * tile : (o + 1) * tile].T
+    out = fetch(out_sem, (covariates_t, covariates_t_out), (first_act_t, first_act_t_out))
+
+    for i, copy in enumerate(logit_copies):
+        copy.wait()
+        for g in range(GROUP):
+            b = i * GROUP + g
+            weight_cells[g] = jnp.exp(logits[b] - local_lse[b : b + 1, :]).astype(BF16)
+        for g in range(GROUP):
+            product[g] = dot(features_t[clade[i * GROUP + g] // 2], weight_cells[g])
+        for g in range(GROUP):
+            b = i * GROUP + g
+            half = pl.ds(pl.multiple_of((clade[b] % 2) * slab, slab), slab)
+            soft_grad[b] = product[g, half, :]
+    fetched[3].wait()
+
     def add_hits(b, start):
         lanes = pl.ds(pl.multiple_of(b * tile, tile), tile)
         rows = pl.ds(start, CHUNK)
@@ -178,61 +246,75 @@
         hits[b, rows, :] = found
         part = found.astype(F32) * logits[b, rows, :]
         hit_sum[pl.ds(b, 1), :] += jnp.sum(part, axis=0, keepdims=True)
+        half = pl.ds(pl.multiple_of((clade[b] % 2) * slab, slab), slab)
+        hit_grad[b] += dot(features_t[clade[b] // 2, half, rows], found)
 
     each_busy(busy, block_count, cells // CHUNK, add_hits)
-    hit_copy = pltpu.make_async_copy(hits, hits_out, hit_sem.at[0])
+    hit_copy = pltpu.make_async_copy(hits, hits_out, out_sem.at[2])
     hit_copy.start()
+    for copy in out:
+        copy.wait()
     hit_copy.wait()
-    for copy in logit_copies:
-        copy.wait()
-    trunk_copy.wait()
 
 
 def backward_kernel(
     records,
     scalars,
-    covariates_in,
     second_weight_in,
     head_weight_in,
     logits_in,
     hits_in,
     trunk_in,
-    lse_in,
+    local_lse_in,
+    lses_in,
     hit_sum_in,
+    covariates_t_in,
+    first_act_t_in,
+    soft_grad_in,
+    hit_grad_in,
     trunk,
     keep,
     send,
-    covariates,
+    lse,
     second_weight,
     head_weight,
-    lse,
+    local_lse,
+    lses,
     hit_sum,
+    covariates_t,
+    first_act_t,
+    soft_grad,
+    hit_grad,
     logits,
     hits,
-    layers,
+    slopes,
     wide_weight,
     packed,
     bias,
-    features_t,
-    first_act_t,
-    covariates_t,
     weight_cells,
-    slab_grad,
     group_back,
     act_grad,
     fetch_sem,
     logit_sem,
-    hit_sem,
-    trunk_sem,
 ):
-    first_act, features, first_slope, second_slope = (layers.at[i] for i in range(4))
-    blocks, cells, tile = features.shape
+    first_slope, second_slope = slopes.at[0], slopes.at[1]
+    blocks, cells, tile = first_slope.shape
     block_count, slab, _ = head_weight.shape
-
-    layer_copies = [
-        pltpu.make_async_copy(trunk_in.at[part], layers.at[part], trunk_sem.at[i])
-        for i, part in enumerate((pl.ds(0, 2), pl.ds(2, 2)))
-    ]
+    first_index, second_index, clade, busy, place = scalar_parts(scalars, blocks, block_count)
+    fetched = fetch(
+        fetch_sem,
+        (head_weight_in, head_weight),
+        (lses_in, lses),
+        (local_lse_in.at[0], local_lse),
+        (hits_in, hits),
+        (soft_grad_in, soft_grad),
+        (hit_grad_in, hit_grad),
+        (hit_sum_in, hit_sum),
+        (second_weight_in, second_weight),
+        (first_act_t_in, first_act_t),
+        (trunk_in.at[pl.ds(2, 2)], slopes),
+        (covariates_t_in, covariates_t),
+    )
     logit_copies = [
         pltpu.make_async_copy(
             logits_in.at[pl.ds(i * GROUP, GROUP)],
@@ -242,33 +324,15 @@
         for i in range(block_count // GROUP)
     ]
 
-    hit_copy = pltpu.make_async_copy(hits_in, hits, hit_sem.at[0])
-    first_index, second_index, clade, busy, place = scalar_parts(scalars, blocks, block_count)
-    fetched = fetch(
-        fetch_sem,
-        (head_weight_in, head_weight),
-        (covariates_in, covariates),
-        (lse_in, lse),
-        (hit_sum_in, hit_sum),
-        (second_weight_in, second_weight),
-    )
-    layer_copies[0].start()
     for copy in logit_copies:
         copy.start()
-    layer_copies[1].start()
-    hit_copy.start()
     fetched[0].wait()
+    widen(wide_weight, head_weight, clade)
     fetched[1].wait()
-    widen(wide_weight, head_weight, clade)
-    for o in range(covariates.shape[1] // tile):
-        covariates_t[o] = covariates[:, o * tile : (o + 1) * tile].T
-    layer_copies[0].wait()
+    lse[...] = join([lses[i] for i in range(lses.shape[0])])
     group = block_count // 2
     core = place[1]
 
-    for o in range(blocks):
-        features_t[o] = features[o].T
-        first_act_t[o] = first_act[o].T
     group_back[...] = jnp.zeros_like(group_back)
     act_grad[...] = jnp.zeros_like(act_grad)
 
@@ -278,10 +342,11 @@
             weight_cells[b] = jnp.exp(logits[b] - lse[pl.ds(b, 1), :]).astype(BF16)
         return carry
 
-    fetched[2].wait()
     for i, copy in enumerate(logit_copies):
         copy.wait()
         weigh(i, 0)
+    for copy in fetched[2:]:
+        copy.wait()
 
     def take_hits(b, start):
         rows = pl.ds(start, CHUNK)
@@ -289,28 +354,23 @@
         weights -= hits[b, rows, :].astype(F32) * (1.0 / records)
         weight_cells[b, rows, :] = weights.astype(BF16)
 
-    hit_copy.wait()
     each_busy(busy, block_count, cells // CHUNK, take_hits)
 
     def step(i, carry):
         for g in range(GROUP):
             b = i * GROUP + g
-            slab_grad[g] = dot(features_t[clade[b] // 2], weight_cells[b])
+            scale = jnp.exp(local_lse[b : b + 1, :] - lse[b : b + 1, :])
+            grad = soft_grad[b] * scale - hit_grad[b] * (1.0 / records)
+            packed[b // group, (b % group) * slab : (b % group + 1) * slab, :] = grad
         for g in range(GROUP):
             b = i * GROUP + g
             spot = clade[b]
-            source = pl.ds(pl.multiple_of((spot % 2) * slab, slab), slab)
-            target = pl.ds(pl.multiple_of((b % group) * slab, slab), slab)
-            packed[b // group, target, :] = slab_grad[g, source, :]
             group_back[spot // 2] += dot_t(weight_cells[b], wide_weight[b])
         return carry
 
     for i in range(block_count // GROUP):
         step(i, 0)
 
-    layer_copies[1].wait()
-    fetched[3].wait()
-    fetched[4].wait()
     bias[...] = jnp.zeros_like(bias)
     pair = blocks // (trunk.shape[0] // 2)
 
@@ -384,12 +444,8 @@
     return lax.all_to_all(jnp.broadcast_to(value[None], (size, *value.shape)), axis, 0, 0)
 
 
-def join(parts):
-    top = jnp.max(parts, axis=0)
-    return top + jnp.log(jnp.sum(jnp.exp(parts - top), axis=0))
-
-
 def forward(
+    peers,
     scalars,
     covariates,
     first_weight,
@@ -397,7 +453,6 @@
     second_weight,
     second_bias,
     head_weight,
-    presence_t,
 ):
     blocks, tile, _ = first_weight.shape
     block_count, _, species = head_weight.shape
@@ -410,13 +465,11 @@
         name="forward",
         out_shape=(
             shape(by_clade, F32),
-            shape(by_clade, BF16),
             shape(by_layer, BF16),
-            shape((block_count, species), F32),
-            shape((block_count, species), F32),
+            shape((peers, block_count, species), F32),
         ),
-        in_specs=[SMEM] + [ANY] * 7,
-        out_specs=[ANY] * 3 + [VMEM] * 2,
+        in_specs=[SMEM] + [ANY] * 6,
+        out_specs=[ANY] * 2 + [VMEM],
         scratch_shapes=[
             pltpu.VMEM(covariates.shape, BF16),
             pltpu.VMEM(first_weight.shape, BF16),
@@ -424,15 +477,12 @@
             pltpu.VMEM(second_weight.shape, BF16),
             pltpu.VMEM((blocks, tile), F32),
             pltpu.VMEM(head_weight.shape, BF16),
-            pltpu.VMEM(presence_t.shape, jnp.int32),
             pltpu.VMEM(by_clade, F32),
-            pltpu.VMEM(by_clade, BF16),
             pltpu.VMEM(by_layer, BF16),
             pltpu.VMEM((block_count, tile, species), BF16),
             pltpu.VMEM((GROUP, 8, species), F32),
-            pltpu.SemaphoreType.DMA((7,)),
+            pltpu.SemaphoreType.DMA((6,)),
             pltpu.SemaphoreType.DMA((block_count // GROUP,)),
-            pltpu.SemaphoreType.DMA((1,)),
             pltpu.SemaphoreType.DMA((1,)),
         ],
         compiler_params=PARAMS,
@@ -444,16 +494,58 @@
         second_weight,
         second_bias.reshape(blocks, tile),
         head_weight,
-        presence_t,
-    )
-
-
-def backward(records, scalars, covariates, second_weight, head_weight, saved, lse, nx):
-    logits, hits, layers, _, hit_sum = saved
+    )
+
+
+def middle(scalars, covariates, presence_t, local_lse, layers, logits, slab):
+    _, blocks, cells, tile = layers.shape
+    block_count, _, species = logits.shape
+    width = covariates.shape[1]
+    shape = jax.ShapeDtypeStruct
+    shapes = (
+        shape(logits.shape, BF16),
+        shape((width // tile, tile, cells), BF16),
+        shape((blocks, tile, cells), BF16),
+        shape((block_count, slab, species), F32),
+        shape((block_count, slab, species), F32),
+        shape((block_count, species), F32),
+    )
+    return pl.pallas_call(
+        middle_kernel,
+        name="middle",
+        out_shape=shapes,
+        in_specs=[SMEM] + [ANY] * 5,
+        out_specs=[ANY] * 3 + [VMEM] * 3,
+        scratch_shapes=[
+            pltpu.VMEM(covariates.shape, BF16),
+            pltpu.VMEM(presence_t.shape, jnp.int32),
+            pltpu.VMEM((block_count, species), F32),
+            pltpu.VMEM((2, blocks, cells, tile), BF16),
+            pltpu.VMEM(logits.shape, F32),
+            pltpu.VMEM(logits.shape, BF16),
+            pltpu.VMEM((width // tile, tile, cells), BF16),
+            pltpu.VMEM((blocks, tile, cells), BF16),
+            pltpu.VMEM((blocks, tile, cells), BF16),
+            pltpu.VMEM((GROUP, cells, species), BF16),
+            pltpu.VMEM((GROUP, tile, species), F32),
+            pltpu.SemaphoreType.DMA((4,)),
+            pltpu.SemaphoreType.DMA((block_count // GROUP,)),
+            pltpu.SemaphoreType.DMA((3,)),
+        ],
+        compiler_params=PARAMS,
+        cost_estimate=pl.CostEstimate(
+            flops=8 * logits.size * tile, bytes_accessed=12 * logits.size, transcendentals=logits.size
+        ),
+    )(scalars, covariates, presence_t, local_lse, layers, logits)
+
+
+def backward(
+    records, scalars, second_weight, head_weight, logits, layers, local_lse, lses, mids, nx
+):
+    hits, covariates_t, first_act_t, soft_grad, hit_grad, hit_sum = mids
     _, *by_block = layers.shape
     blocks, cells, tile = by_block
     block_count, slab, species = head_weight.shape
-    width = covariates.shape[1]
     shape = jax.ShapeDtypeStruct
     pair = blocks // nx
     part_rows = pair * tile + 8
@@ -466,44 +558,47 @@
             shape((2 * nx, part_rows, tile), LINK),
             shape((half_rows, tile), F32),
             shape((half_rows, tile), F32),
+            shape((block_count, species), F32),
         ),
-        in_specs=[SMEM] + [ANY] * 8,
-        out_specs=[VMEM] * 3,
+        in_specs=[SMEM] + [ANY] * 12,
+        out_specs=[VMEM] * 4,
         scratch_shapes=[
-            pltpu.VMEM(covariates.shape, BF16),
             pltpu.VMEM(second_weight.shape, BF16),
             pltpu.VMEM(head_weight.shape, BF16),
-            pltpu.VMEM(lse.shape, F32),
+            pltpu.VMEM((block_count, species), F32),
+            pltpu.VMEM(lses.shape, F32),
             pltpu.VMEM(hit_sum.shape, F32),
+            pltpu.VMEM(covariates_t.shape, BF16),
+            pltpu.VMEM(first_act_t.shape, BF16),
+            pltpu.VMEM(soft_grad.shape, F32),
+            pltpu.VMEM(hit_grad.shape, F32),
             pltpu.VMEM(logits.shape, F32),
             pltpu.VMEM(hits.shape, BF16),
-            pltpu.VMEM(layers.shape, BF16),
+            pltpu.VMEM((2, *by_block), BF16),
             pltpu.VMEM((block_count, tile, species), BF16),
             pltpu.VMEM((2, half_rows, tile), F32),
             pltpu.VMEM((2 * nx, 8, tile), F32),
-            pltpu.VMEM((blocks, tile, cells), BF16),
-            pltpu.VMEM((blocks, tile, cells), BF16),
-            pltpu.VMEM((width // tile, tile, cells), BF16),
             pltpu.VMEM(hits.shape, BF16),
-            pltpu.VMEM((GROUP, tile, species), F32),
             pltpu.VMEM(by_block, F32),
             pltpu.VMEM(by_block, F32),
-            pltpu.SemaphoreType.DMA((5,)),
+            pltpu.SemaphoreType.DMA((11,)),
             pltpu.SemaphoreType.DMA((block_count // GROUP,)),
-            pltpu.SemaphoreType.DMA((1,)),
-            pltpu.SemaphoreType.DMA((2,)),
         ],
         compiler_params=PARAMS,
     )(
         scalars,
-        covariates,
         second_weight,
         head_weight,
         logits,
         hits,
         layers,
-        lse,
+        local_lse,
+        lses,
         hit_sum,
+        covariates_t,
+        first_act_t,
+        soft_grad,
+        hit_grad,
     )
 
 
@@ -541,7 +636,8 @@
     scalars = jnp.concatenate([place, first_index, second_index, clade_block, busy])
 
     all_covariates = spread(covariates, "x", nx).reshape(cells, width)
-    saved = forward(
+    logits, layers, local_lse = forward(
+        ny,
         scalars,
         all_covariates,
         first_weight,
@@ -549,13 +645,12 @@
         second_weight,
         second_bias,
         head_weight,
-        presence_t,
-    )
-    lse = join(spread(saved[3], "y", ny))
-    lse = join(spread(lse, ("z", "c"), nz * 2))
-
-    trunk, keep, send = backward(
-        records, scalars, all_covariates, second_weight, head_weight, saved, lse, nx
+    )
+    lses = lax.all_to_all(local_lse, "y", 0, 0)
+    mids = middle(scalars, all_covariates, presence_t, local_lse, layers, logits, slab)
+    lses = spread(join(lses), ("z", "c"), nz * 2)
+    trunk, keep, send, lse = backward(
+        records, scalars, second_weight, head_weight, logits, layers, local_lse, lses, mids, nx
     )
     pair, group = blocks // nx, block_count // 2
     head_rows = group * slab
@@ -610,7 +705,7 @@
             in_specs=[SMEM] + [VMEM] * 4,
             out_specs=[VMEM] * 6,
             scratch_shapes=[pltpu.VMEM((2, half_rows, tile), LINK)],
-            compiler_params=PARAMS,
+            compiler_params=pltpu.CompilerParams(vmem_limit_bytes=16 << 20),
         )(scalars, trunk, head, other_head, lse)
     )
     return (

time: 149 us -> 153 us (1.027)
  blocking collectives: 73.5 us -> 54 us
  starting transfers between devices: 19.7 us -> 34.8 us
  Pallas kernels: 26.2 us -> 34.9 us
    all_to_all x3 -> x1, blocking collectives: 56.2 us -> 17.9 us  [spread(): lax.all_to_all(jnp.broadcast_to(value[None], (size, *value.shape)), axis,...]
    all_to_all x0 -> x1, blocking collectives: none -> 14.5 us  [body(): lses = lax.all_to_all(local_lse, 'y', 0, 0)]
    all_to_all x2 -> x3, starting transfers between devices: 11.8 us -> 25.5 us  [spread(): lax.all_to_all(jnp.broadcast_to(value[None], (size, *value.shape)), axis,...]
    pallas_call x0 -> x1, Pallas kernels: none -> 12.8 us  [middle(): pl.pallas_call(middle_kernel, name='middle', out_shape=shapes, in_specs=[...]
    all_to_all x1, blocking collectives: 17.3 us -> 21.6 us  [body(): lax.all_to_all(cut, ('y', 'z'), 0, 0).astype(F32)]
    pallas_call x1, Pallas kernels: 12.3 us -> 9.03 us  [forward(): pl.pallas_call(forward_kernel, name='forward', out_shape=(shape(by_clade,...]
    ppermute x1, starting transfers between devices: 1.92 us -> 3.82 us  [body(): head = keep + lax.ppermute(send, 'c', swap)]
    all_to_all x2 -> x3, waiting for transfers between devices: 8.79 us -> 8.73 us  [spread(): lax.all_to_all(jnp.broadcast_to(value[None], (size, *value.shape)), axis,...]
  transfers between devices with their start and end apart: 5 -> 6, of which waited for: 4 -> 4; matrix products, arithmetic and copies ran while one was open for 3% -> 3% of each run, Pallas kernels for 0% -> 8%
where the time goes in v6:
time: 153 us; the launch traced here: 152 us
  blocking collectives  54 us (35%)
  Pallas kernels  34.9 us (23%)
  starting transfers between devices  34.8 us (23%)
  waiting for transfers between devices  18.4 us (12%)
  local copies, waits for them, and re-layouts  6.36 us (4%)
  other arithmetic  2.73 us (2%)
    all_to_all x3, starting transfers between devices, spread(): lax.all_to_all(jnp.broadcast_to(value[None], (size, *value.shape)), axis,...  25.5 us
    all_to_all x1, blocking collectives, body(): lax.all_to_all(cut, ('y', 'z'), 0, 0).astype(F32)  21.6 us
    all_to_all x1, blocking collectives, spread(): lax.all_to_all(jnp.broadcast_to(value[None], (size, *value.shape)), axis,...  17.9 us
    all_to_all x1, blocking collectives, body(): lses = lax.all_to_all(local_lse, 'y', 0, 0)  14.5 us
    pallas_call x1, Pallas kernels, middle(): pl.pallas_call(middle_kernel, name='middle', out_shape=shapes, in_specs=[...  12.8 us
    pallas_call x1, Pallas kernels, backward(): pl.pallas_call(functools.partial(backward_kernel, records), name='backwar...  11.3 us
    pallas_call x1, Pallas kernels, forward(): pl.pallas_call(forward_kernel, name='forward', out_shape=(shape(by_clade,...  9.03 us
    all_to_all x3, waiting for transfers between devices, spread(): lax.all_to_all(jnp.broadcast_to(value[None], (size, *value.shape)), axis,...  8.73 us
  transfers between devices with their start and end apart: 6, of which 4 were waited for; matrix products, arithmetic and copies ran while one was open for 3% of the time, Pallas kernels for 8%

profile of v6, /device:TPU:1, one launch (start us, length us, event | category | flops | bytes accessed | tf_op | source)
XLA Modules:
  0.0 152.2 jit_solution(5622763071539788054)
XLA Ops:
  0.6 1.6 %broadcast_in_dim.13 = bf16[4,128,256]{2,1,0:T(8,128)(2,1)} broadcast(bf16[128,256]{1,0:T(8,128)(2,1)} %param.10), dimensions={1,2} | broadcast | bytes 327680 | tf_op jit(solution)/shard_map/broadcast_in_dim | solution.py:444
  2.2 4.8 %all-to-all-start = ((bf16[4,128,256]{2,1,0:T(8,128)(2,1)}), bf16[4,128,256]{2,1,0:T(8,128)(2,1)S(1)}, u32[]{:S(2)}, u32[]{:S(2)}) async-start(bf16[4,128,256]{2,1,0:T(8,128)(2,1)} %broadcast_in_dim.13), calls=%async_computation | async-start | bytes 524288 | tf_op jit(solution)/shard_map/all_to_all | solution.py:444
  7.0 1.0 compare_reduce_fusion.3
  8.1 0.1 bitcast_reduce_fusion.2
  8.2 0.1 bitcast_reduce_fusion
  8.3 0.1 copy.26
  8.4 0.1 reshape.68
  8.5 1.4 concatenate.17.scalars
  9.9 2.7 %all-to-all-done = bf16[4,128,256]{2,1,0:T(8,128)(2,1)S(1)} async-done(((bf16[4,128,256]{2,1,0:T(8,128)(2,1)}), bf16[4,128,256]{2,1,0:T(8,128)(2,1)S(1)}, u32[]{:S(2)}, u32[]{:S(2)}) %all-to-all-start) | async-done | bytes 262176 | tf_op jit(solution)/shard_map/all_to_all | solution.py:444
  12.6 0.0 copy-start.2
  12.6 0.7 copy-done.2
  13.3 9.0 %forward.1 = (f32[20,512,128]{2,1,0:T(8,128)}, bf16[4,8,512,128]{3,2,1,0:T(8,128)(2,1)}, f32[8,20,128]{2,1,0:T(8,128)}) custom-call(s32[118]{0:T(128)} %concatenate.17.scalars, bf16[512,256]{1,0:T(8,128)(2,1)} %bitcast.37, bf16[8,128,128]{2,1,0:T(8,128)(2,1)} %first_weight_in.1, f32[8,128]{1,0:T(8,128)} %bitcast.43, bf16[8,128,128]{2,1,0:T(8,128)(2,1)} %second_weight_in.3, ...), custom_call_target="tpu_custom_call" | custom-call | tf_op jit(solution)/shard_map/forward/pallas_call | solution.py:463
  22.3 14.5 %all_to_all.35 = f32[8,20,128]{2,1,0:T(8,128)S(1)} all-to-all(f32[8,20,128]{2,1,0:T(8,128)} %get-tuple-element.26.local_lse_in), channel_id=1, replica_groups=mesh['y'=8,'z'=8,'c'=2,'x'=4] {'y'}, dimensions={0} | all-to-all | bytes 163840 | tf_op jit(solution)/shard_map/all_to_all | solution.py:649
  36.9 0.7 broadcast_in_dim.15
  37.6 13.7 %all-to-all-start.2 = ((f32[16,20,128]{2,1,0:T(8,128)}), f32[16,20,128]{2,1,0:T(8,128)S(1)}, u32[]{:S(2)}, u32[]{:S(2)}) async-start(f32[16,20,128]{2,1,0:T(8,128)} %broadcast_in_dim.15), calls=%async_computation.2 | async-start | bytes 393216 | tf_op jit(solution)/shard_map/all_to_all | solution.py:444
  51.3 12.8 %middle.1 = (bf16[20,512,128]{2,1,0:T(8,128)(2,1)}, bf16[2,128,512]{2,1,0:T(8,128)(2,1)}, bf16[8,128,512]{2,1,0:T(8,128)(2,1)}, f32[20,64,128]{2,1,0:T(8,128)}, ...) custom-call(s32[118]{0:T(128)} %concatenate.17.scalars, bf16[512,256]{1,0:T(8,128)(2,1)} %bitcast.38, s32[16,2560]{1,0:T(8,128)} %bitcast.39, ...), custom_call_target="tpu_custom_call" | custom-call | flops 1342177280 | bytes 15728640 | tf_op jit(solution)/shard_map/middle/pallas_call | solution.py:513
  64.1 0.0 all-to-all-done.2.lses_in
  64.1 0.0 copy-start.3
  64.1 0.6 copy-done.3
  64.8 11.3 %backward.1 = (bf16[8,264,128]{2,1,0:T(8,128)(2,1)}, f32[656,128]{1,0:T(8,128)}, f32[656,128]{1,0:T(8,128)}, f32[20,128]{1,0:T(8,128)}) custom-call(s32[118]{0:T(128)} %concatenate.17.scalars, bf16[8,128,128]{2,1,0:T(8,128)(2,1)} %second_weight_in.3, bf16[20,64,128]{2,1,0:T(8,128)(2,1)} %head_weight_in.3, f32[20,512,128]{2,1,0:T(8,128)} %get-tuple-element.25.logits_in, ...), custom_call_target="tpu_custom_call" | custom-call | tf_op jit(solution)/shard_map/backward/pallas_call | solution.py:554
  76.1 3.8 %collective-permute-start = (f32[656,128]{1,0:T(8,128)}, f32[656,128]{1,0:T(8,128)S(1)}, u32[]{:S(2)}, u32[]{:S(2)}) collective-permute-start(f32[656,128]{1,0:T(8,128)} %get-tuple-element.36), channel_id=1, source_target_pairs={{0,4},{4,0},{1,5},{5,1},{2,6},{6,2},{3,7},{7,3},{8,12},{12,8},{9,1... | collective-permute-start | bytes 1007624 | tf_op jit(solution)/shard_map/ppermute | solution.py:659
  79.9 3.5 %all-to-all-start.3 = ((bf16[8,264,128]{2,1,0:T(8,128)(2,1)}), bf16[8,264,128]{2,1,0:T(8,128)(2,1)S(1)}, u32[]{:S(2)}, u32[]{:S(2)}) async-start(bf16[8,264,128]{2,1,0:T(8,128)(2,1)} %get-tuple-element.34), calls=%async_computation.3 | async-start | bytes 1081344 | tf_op jit(solution)/shard_map/all_to_all | solution.py:660
  83.4 0.0 copy-start
  83.4 0.0 copy-start.1
  83.4 0.0 collective-permute-done
  83.5 1.0 add_convert_fusion
  84.5 0.1 reshape.62
  84.6 8.4 %all-to-all-done.3 = bf16[8,264,128]{2,1,0:T(8,128)(2,1)S(1)} async-done(((bf16[8,264,128]{2,1,0:T(8,128)(2,1)}), bf16[8,264,128]{2,1,0:T(8,128)(2,1)S(1)}, u32[]{:S(2)}, u32[]{:S(2)}) %all-to-all-start.3) | async-done | bytes 540704 | tf_op jit(solution)/shard_map/all_to_all | solution.py:660
  92.9 0.1 reduce.9
  93.1 0.2 fusion.5
  93.3 21.6 %all_to_all.36 = bf16[64,16,128]{2,1,0:T(8,128)(2,1)S(1)} all-to-all(bf16[64,16,128]{2,1,0:T(8,128)(2,1)S(1)} %fusion.5), channel_id=1, replica_groups=mesh['y'=8,'z'=8,'c'=2,'x'=4] {'y','z'}, dimensions={0} | all-to-all | bytes 524288 | tf_op jit(solution)/shard_map/all_to_all | solution.py:674
  114.9 0.1 reduce_sum.22
  115.0 17.9 %all_to_all.37 = bf16[64,16,128]{2,1,0:T(8,128)(2,1)S(1)} all-to-all(bf16[64,16,128]{2,1,0:T(8,128)(2,1)S(1)} %broadcast_in_dim.34), channel_id=1, replica_groups=mesh['y'=8,'z'=8,'c'=2,'x'=4] {'y','z'}, dimensions={0} | all-to-all | bytes 524288 | tf_op jit(solution)/shard_map/all_to_all | solution.py:444
  133.0 0.9 broadcast_in_dim.35
  133.9 7.0 %all-to-all-start.6 = ((bf16[8,264,128]{2,1,0:T(8,128)(2,1)}), bf16[8,264,128]{2,1,0:T(8,128)(2,1)S(1)}, u32[]{:S(2)}, u32[]{:S(2)}) async-start(bf16[8,264,128]{2,1,0:T(8,128)(2,1)} %broadcast_in_dim.35), calls=%async_computation.6 | async-start | bytes 1081344 | tf_op jit(solution)/shard_map/all_to_all | solution.py:444
  140.8 0.1 slice.103
  140.9 0.1 reshape.64
  141.0 2.0 %collective-permute-start.1 = (bf16[656,128]{1,0:T(8,128)(2,1)S(1)}, bf16[656,128]{1,0:T(8,128)(2,1)S(1)}, u32[]{:S(2)}, u32[]{:S(2)}) collective-permute-start(bf16[656,128]{1,0:T(8,128)(2,1)S(1)} %fusion.6.own), channel_id=1, source_target_pairs={{0,4},{4,0},{1,5},{5,1},{2,6},{6,2},{3,7},{7,3},{8,12},{12,8},{9,1... | collective-permute-start | bytes 503816 | tf_op jit(solution)/shard_map/ppermute | solution.py:684
  143.0 1.3 collective-permute-done.1.other
  144.3 6.0 %all-to-all-done.6.trunk = bf16[8,264,128]{2,1,0:T(8,128)(2,1)S(1)} async-done(((bf16[8,264,128]{2,1,0:T(8,128)(2,1)}), bf16[8,264,128]{2,1,0:T(8,128)(2,1)S(1)}, u32[]{:S(2)}, u32[]{:S(2)}) %all-to-all-start.6) | async-done | bytes 540704 | tf_op jit(solution)/shard_map/all_to_all | solution.py:444
  150.4 0.0 copy-done
  150.4 0.0 copy-done.1
  150.4 1.8 %finish.1 = (f32[20,128]{1,0:T(8,128)}, f32[20,64,128]{2,1,0:T(8,128)}, f32[8,128,128]{2,1,0:T(8,128)}, f32[8,128]{1,0:T(8,128)}, f32[8,128,128]{2,1,0:T(8,128)}, /*index=5*/f32[8,128]{1,0:T(8,128)}) custom-call(s32[118]{0:T(128)S(1)} %copy-done, bf16[8,264,128]{2,1,0:T(8,128)(2,1)S(1)} %all-to-all-done.6.trunk, bf16[656,128]{1,0:T(8,128)(2,1)S(1)} %fusion.6.own, ...), custom_call_target="tpu_custom_call" | custom-call | tf_op jit(solution)/shard_map/finish/pallas_call | solution.py:694
  (16 shorter events, 0.2 us)
Async XLA Ops:
  2.2 10.4 %all-to-all-start = ((bf16[4,128,256]{2,1,0:T(8,128)(2,1)}), bf16[4,128,256]{2,1,0:T(8,128)(2,1)S(1)}, u32[]{:S(2)}, u32[]{:S(2)}) async-start(bf16[4,128,256]{2,1,0:T(8,128)(2,1)} %broadcast_in_dim.13), calls=%async_computation | async-start | bytes 524288 | tf_op jit(solution)/shard_map/all_to_all | solution.py:444
  12.6 0.7 copy-start.2
  37.6 26.5 %all-to-all-start.2 = ((f32[16,20,128]{2,1,0:T(8,128)}), f32[16,20,128]{2,1,0:T(8,128)S(1)}, u32[]{:S(2)}, u32[]{:S(2)}) async-start(f32[16,20,128]{2,1,0:T(8,128)} %broadcast_in_dim.15), calls=%async_computation.2 | async-start | bytes 393216 | tf_op jit(solution)/shard_map/all_to_all | solution.py:444
  64.1 0.7 copy-start.3
  76.1 7.4 %collective-permute-start = (f32[656,128]{1,0:T(8,128)}, f32[656,128]{1,0:T(8,128)S(1)}, u32[]{:S(2)}, u32[]{:S(2)}) collective-permute-start(f32[656,128]{1,0:T(8,128)} %get-tuple-element.36), channel_id=1, source_target_pairs={{0,4},{4,0},{1,5},{5,1},{2,6},{6,2},{3,7},{7,3},{8,12},{12,8},{9,1... | collective-permute-start | bytes 1007624 | tf_op jit(solution)/shard_map/ppermute | solution.py:659
  79.9 13.0 %all-to-all-start.3 = ((bf16[8,264,128]{2,1,0:T(8,128)(2,1)}), bf16[8,264,128]{2,1,0:T(8,128)(2,1)S(1)}, u32[]{:S(2)}, u32[]{:S(2)}) async-start(bf16[8,264,128]{2,1,0:T(8,128)(2,1)} %get-tuple-element.34), calls=%async_computation.3 | async-start | bytes 1081344 | tf_op jit(solution)/shard_map/all_to_all | solution.py:660
  83.4 66.9 %copy-start = (s32[118]{0:T(128)S(1)}, s32[118]{0:T(128)}, u32[]{:S(2)}) copy-start(s32[118]{0:T(128)} %concatenate.17.scalars) | copy-start | bytes 1420
  83.4 66.9 %copy-start.1 = (f32[20,128]{1,0:T(8,128)S(1)}, f32[20,128]{1,0:T(8,128)}, u32[]{:S(2)}) copy-start(f32[20,128]{1,0:T(8,128)} %get-tuple-element.37.lse) | copy-start | bytes 30724
  133.9 16.5 %all-to-all-start.6 = ((bf16[8,264,128]{2,1,0:T(8,128)(2,1)}), bf16[8,264,128]{2,1,0:T(8,128)(2,1)S(1)}, u32[]{:S(2)}, u32[]{:S(2)}) async-start(bf16[8,264,128]{2,1,0:T(8,128)(2,1)} %broadcast_in_dim.35), calls=%async_computation.6 | async-start | bytes 1081344 | tf_op jit(solution)/shard_map/all_to_all | solution.py:444
  141.0 3.3 %collective-permute-start.1 = (bf16[656,128]{1,0:T(8,128)(2,1)S(1)}, bf16[656,128]{1,0:T(8,128)(2,1)S(1)}, u32[]{:S(2)}, u32[]{:S(2)}) collective-permute-start(bf16[656,128]{1,0:T(8,128)(2,1)S(1)} %fusion.6.own), channel_id=1, source_target_pairs={{0,4},{4,0},{1,5},{5,1},{2,6},{6,2},{3,7},{7,3},{8,12},{12,8},{9,1... | collective-permute-start | bytes 503816 | tf_op jit(solution)/shard_map/ppermute | solution.py:684

commit v7 on v4

--- a/solution.py
+++ b/solution.py
@@ -12,6 +12,8 @@
 F32 = jnp.float32
 CHUNK = 128
 GROUP = 10
+AT_ONCE = 4
+NOWHERE = -(1 << 30)
 LINK = BF16
 VMEM = pl.BlockSpec(memory_space=pltpu.VMEM)
 ANY = pl.BlockSpec(memory_space=pl.ANY)
@@ -32,7 +34,7 @@
     rows = 16 * lax.broadcasted_iota(jnp.int32, shape, 0) + lax.broadcasted_iota(jnp.int32, shape, 1)
     rows = rows.astype(F32).astype(BF16)
     local = jnp.clip(presence_ref[:, lanes] - first_row, -1, CHUNK).astype(F32)
-    one, zero = jnp.ones(shape, BF16), jnp.zeros(shape, BF16)
+    one, zero = jnp.full(shape, 1.0 / presence_ref.shape[0], BF16), jnp.zeros(shape, BF16)
     hits = zero
     for record in range(presence_ref.shape[0]):
         there = jnp.broadcast_to(local[record : record + 1], shape[1:]).astype(BF16)
@@ -68,16 +70,19 @@
         wide_weight[b, half, :] = head_weight[b]
 
 
-def each_busy(busy, block_count, chunks, act):
-    def step(i, carry):
-        @pl.when(busy[i] > 0)
-        def _():
-            b = i // chunks
-            act(b, pl.multiple_of((i % chunks) * CHUNK, CHUNK))
-
+def each_busy(busy, found, count, act):
+    def note(i, n):
+        found[n] = i
+        return n + jnp.where(busy[i] > 0, 1, 0)
+
+    total = lax.fori_loop(0, count, note, 0)
+
+    def step(j, carry):
+        spots = [j * AT_ONCE + u for u in range(AT_ONCE)]
+        act([(jnp.where(spot < total, found[spot], 0), spot < total) for spot in spots])
         return carry
 
-    lax.fori_loop(0, block_count * chunks, step, 0)
+    lax.fori_loop(0, (total + AT_ONCE - 1) // AT_ONCE, step, 0)
 
 
 def forward_kernel(
@@ -88,27 +93,23 @@
     second_weight_in,
     second_bias_in,
     head_weight_in,
-    presence_in,
-    logits_out,
-    hits_out,
+    terms_out,
     trunk_out,
     local_lse,
-    hit_sum,
+    high,
     covariates,
     first_weight,
     first_bias,
     second_weight,
     second_bias,
     head_weight,
-    presence,
-    logits,
-    hits,
+    terms,
     trunk,
     wide_weight,
+    logits,
     tops,
     fetch_sem,
-    logit_sem,
-    hit_sem,
+    term_sem,
     trunk_sem,
 ):
     fetched = fetch(
@@ -119,13 +120,11 @@
         (second_weight_in, second_weight),
         (second_bias_in, second_bias),
         (head_weight_in, head_weight),
-        (presence_in, presence),
     )
     first_act, features, first_slope, second_slope = (trunk.at[i] for i in range(4))
     blocks, cells, tile = features.shape
     block_count, slab, _ = head_weight.shape
-    first_index, second_index, clade, busy, place = scalar_parts(scalars, blocks, block_count)
-    first_cell = place[0]
+    first_index, second_index, clade, _, _ = scalar_parts(scalars, blocks, block_count)
 
     def layer(pre, act_ref, slope_ref, o):
         sigma = 1.0 / (1.0 + jnp.exp(-pre))
@@ -144,72 +143,127 @@
 
     trunk_copy = pltpu.make_async_copy(trunk, trunk_out, trunk_sem.at[0])
     trunk_copy.start()
-    hit_sum[...] = jnp.zeros_like(hit_sum)
     fetched[5].wait()
-    fetched[6].wait()
     widen(wide_weight, head_weight, clade)
 
-    def step(i, carry):
+    def step(i):
         for g in range(GROUP):
             b = i * GROUP + g
             part = dot(features[clade[b] // 2], wide_weight[b])
-            logits[b] = part
+            logits[g] = part
             tops[g] = jnp.max(part.reshape(cells // 8, 8, -1), axis=0)
         for g in range(GROUP):
             b = i * GROUP + g
             top = jnp.max(tops[g], axis=0, keepdims=True)
-            total = jnp.sum(jnp.exp(logits[b] - top), axis=0, keepdims=True)
-            local_lse[pl.ds(b, 1), :] = top + jnp.log(total)
-        return carry
-
-    logit_copies = []
+            part = jnp.exp(logits[g] - top)
+            terms[b] = part.astype(BF16)
+            lse = top + jnp.log(jnp.sum(part, axis=0, keepdims=True))
+            high[b : b + 1, :] = top
+            for peer in range(local_lse.shape[0]):
+                local_lse[peer, b : b + 1, :] = lse
+
+    term_copies = []
     for i in range(block_count // GROUP):
-        step(i, 0)
+        step(i)
         part = pl.ds(i * GROUP, GROUP)
-        logit_copies.append(
-            pltpu.make_async_copy(logits.at[part], logits_out.at[part], logit_sem.at[i])
-        )
-        logit_copies[i].start()
-
-    def add_hits(b, start):
-        lanes = pl.ds(pl.multiple_of(b * tile, tile), tile)
-        rows = pl.ds(start, CHUNK)
-        found = hits_of(presence, lanes, first_cell + start)
-        hits[b, rows, :] = found
-        part = found.astype(F32) * logits[b, rows, :]
-        hit_sum[pl.ds(b, 1), :] += jnp.sum(part, axis=0, keepdims=True)
-
-    each_busy(busy, block_count, cells // CHUNK, add_hits)
-    hit_copy = pltpu.make_async_copy(hits, hits_out, hit_sem.at[0])
-    hit_copy.start()
-    hit_copy.wait()
-    for copy in logit_copies:
+        copy = pltpu.make_async_copy(terms.at[part], terms_out.at[part], term_sem.at[i])
+        copy.start()
+        term_copies.append(copy)
+    for copy in term_copies:
         copy.wait()
     trunk_copy.wait()
 
 
+def join(parts):
+    top = functools.reduce(jnp.maximum, [parts[i] for i in range(len(parts))])
+    return top + jnp.log(sum(jnp.exp(parts[i] - top) for i in range(len(parts))))
+
+
+def middle_kernel(
+    scalars,
+    presence_in,
+    head_weight_in,
+    trunk_in,
+    hit_back,
+    hit_grad,
+    hit_sum,
+    presence,
+    head_weight,
+    features,
+    wide_weight,
+    back,
+    found,
+    fetch_sem,
+):
+    blocks, cells, tile = features.shape
+    block_count, slab, _ = head_weight.shape
+    _, _, clade, busy, place = scalar_parts(scalars, blocks, block_count)
+    first_cell = place[0]
+    fetched = fetch(
+        fetch_sem,
+        (head_weight_in, head_weight),
+        (presence_in, presence),
+        (trunk_in.at[1], features),
+    )
+    hit_grad[...] = jnp.zeros_like(hit_grad)
+    back[...] = jnp.zeros_like(back)
+    fetched[0].wait()
+    widen(wide_weight, head_weight, clade)
+    for copy in fetched[1:]:
+        copy.wait()
+
+    def add_hits(chosen):
+        products = []
+        for i, valid in chosen:
+            b, start = i // (cells // CHUNK), pl.multiple_of((i % (cells // CHUNK)) * CHUNK, CHUNK)
+            lanes = pl.ds(pl.multiple_of(b * tile, tile), tile)
+            rows = pl.ds(start, CHUNK)
+            hits = hits_of(presence, lanes, jnp.where(valid, first_cell + start, NOWHERE))
+            grad = lax.dot_general(
+                features[clade[b] // 2, rows, :],
+                hits,
+                (((0,), (0,)), ((), ())),
+                preferred_element_type=F32,
+            )
+            products.append((b, rows, grad, dot_t(hits, wide_weight[b])))
+        for b, rows, grad, part in products:
+            hit_grad[b] += grad
+            back[clade[b] // 2, rows, :] += part
+
+    each_busy(busy, found, block_count * (cells // CHUNK), add_hits)
+    for b in range(block_count):
+        terms = hit_grad[b] * wide_weight[b].astype(F32)
+        hit_sum[b : b + 1, :] = jnp.sum(terms, axis=0, keepdims=True)
+    for o in range(blocks):
+        hit_back[o] = back[o].astype(BF16)
+
+
 def backward_kernel(
-    records,
     scalars,
     covariates_in,
     second_weight_in,
     head_weight_in,
-    logits_in,
-    hits_in,
+    terms_in,
     trunk_in,
-    lse_in,
+    high_in,
+    lses_in,
+    hit_back_in,
+    hit_grad_in,
     hit_sum_in,
     trunk,
     keep,
     send,
+    lse,
     covariates,
     second_weight,
     head_weight,
-    lse,
+    terms,
+    layers,
+    high,
+    lses,
+    hit_back,
+    hit_grad,
     hit_sum,
-    logits,
-    hits,
-    layers,
     wide_weight,
     packed,
     bias,
@@ -221,96 +275,68 @@
     group_back,
     act_grad,
     fetch_sem,
-    logit_sem,
-    hit_sem,
-    trunk_sem,
+    term_sem,
 ):
     first_act, features, first_slope, second_slope = (layers.at[i] for i in range(4))
     blocks, cells, tile = features.shape
     block_count, slab, _ = head_weight.shape
-
-    layer_copies = [
-        pltpu.make_async_copy(trunk_in.at[part], layers.at[part], trunk_sem.at[i])
-        for i, part in enumerate((pl.ds(0, 2), pl.ds(2, 2)))
-    ]
-    logit_copies = [
-        pltpu.make_async_copy(
-            logits_in.at[pl.ds(i * GROUP, GROUP)],
-            logits.at[pl.ds(i * GROUP, GROUP)],
-            logit_sem.at[i],
-        )
-        for i in range(block_count // GROUP)
-    ]
-
-    hit_copy = pltpu.make_async_copy(hits_in, hits, hit_sem.at[0])
-    first_index, second_index, clade, busy, place = scalar_parts(scalars, blocks, block_count)
-    fetched = fetch(
+    first_index, second_index, clade, _, place = scalar_parts(scalars, blocks, block_count)
+    early = fetch(
         fetch_sem,
+        (lses_in, lses),
+        (high_in, high),
         (head_weight_in, head_weight),
+        (trunk_in.at[pl.ds(0, 2)], layers.at[pl.ds(0, 2)]),
         (covariates_in, covariates),
-        (lse_in, lse),
+    )
+    pieces = [pl.ds(i * GROUP, GROUP) for i in range(block_count // GROUP)]
+    term_copies = fetch(term_sem, *[(terms_in.at[p], terms.at[p]) for p in pieces])
+    late = fetch(
+        fetch_sem.at[pl.ds(len(early), 5)],
+        (hit_back_in, hit_back),
+        (hit_grad_in, hit_grad),
         (hit_sum_in, hit_sum),
+        (trunk_in.at[pl.ds(2, 2)], layers.at[pl.ds(2, 2)]),
         (second_weight_in, second_weight),
     )
-    layer_copies[0].start()
-    for copy in logit_copies:
-        copy.start()
-    layer_copies[1].start()
-    hit_copy.start()
-    fetched[0].wait()
-    fetched[1].wait()
+    early[0].wait()
+    early[1].wait()
+    lse[...] = join([lses[i] for i in range(lses.shape[0])])
+    high[...] = jnp.exp(high[...] - lse[...])
+    early[2].wait()
     widen(wide_weight, head_weight, clade)
-    for o in range(covariates.shape[1] // tile):
-        covariates_t[o] = covariates[:, o * tile : (o + 1) * tile].T
-    layer_copies[0].wait()
-    group = block_count // 2
-    core = place[1]
-
+    early[3].wait()
     for o in range(blocks):
         features_t[o] = features[o].T
         first_act_t[o] = first_act[o].T
-    group_back[...] = jnp.zeros_like(group_back)
+    early[4].wait()
+    for o in range(covariates.shape[1] // tile):
+        covariates_t[o] = covariates[:, o * tile : (o + 1) * tile].T
+    group = block_count // 2
+    core = place[1]
+
     act_grad[...] = jnp.zeros_like(act_grad)
-
-    def weigh(i, carry):
-        for g in range(GROUP):
-            b = i * GROUP + g
-            weight_cells[b] = jnp.exp(logits[b] - lse[pl.ds(b, 1), :]).astype(BF16)
-        return carry
-
-    fetched[2].wait()
-    for i, copy in enumerate(logit_copies):
+    for i, copy in enumerate(term_copies):
         copy.wait()
-        weigh(i, 0)
-
-    def take_hits(b, start):
-        rows = pl.ds(start, CHUNK)
-        weights = jnp.exp(logits[b, rows, :] - lse[pl.ds(b, 1), :])
-        weights -= hits[b, rows, :].astype(F32) * (1.0 / records)
-        weight_cells[b, rows, :] = weights.astype(BF16)
-
-    hit_copy.wait()
-    each_busy(busy, block_count, cells // CHUNK, take_hits)
-
-    def step(i, carry):
+        for b in range(i * GROUP, (i + 1) * GROUP):
+            weights = terms[b].astype(F32) * high[b : b + 1, :]
+            weight_cells[b] = weights.astype(BF16)
+    for copy in late:
+        copy.wait()
+    for o in range(blocks):
+        group_back[o] = -hit_back[o].astype(F32)
+    for i in range(block_count // GROUP):
         for g in range(GROUP):
             b = i * GROUP + g
             slab_grad[g] = dot(features_t[clade[b] // 2], weight_cells[b])
         for g in range(GROUP):
             b = i * GROUP + g
-            spot = clade[b]
-            source = pl.ds(pl.multiple_of((spot % 2) * slab, slab), slab)
-            target = pl.ds(pl.multiple_of((b % group) * slab, slab), slab)
-            packed[b // group, target, :] = slab_grad[g, source, :]
-            group_back[spot // 2] += dot_t(weight_cells[b], wide_weight[b])
-        return carry
-
-    for i in range(block_count // GROUP):
-        step(i, 0)
-
-    layer_copies[1].wait()
-    fetched[3].wait()
-    fetched[4].wait()
+            half = pl.ds(pl.multiple_of((clade[b] % 2) * slab, slab), slab)
+            rows = slice((b % group) * slab, (b % group + 1) * slab)
+            grad = slab_grad[g, half, :] - hit_grad[b, half, :]
+            packed[b // group, rows, :] = grad
+            group_back[clade[b] // 2] += dot_t(weight_cells[b], wide_weight[b])
+
     bias[...] = jnp.zeros_like(bias)
     pair = blocks // (trunk.shape[0] // 2)
 
@@ -339,7 +365,6 @@
 
 def finish_kernel(
     total_cells,
-    records,
     scalars,
     trunk,
     own,
@@ -365,7 +390,7 @@
     tail = group * slab
     for half in range(2):
         rows = slice(half * group, (half + 1) * group)
-        hit_mean = halves[half, tail:, :].astype(F32)[:group] * (1.0 / records)
+        hit_mean = halves[half, tail:, :].astype(F32)[:group]
         species_loss[rows, :] = lse[rows, :] - math.log(total_cells) - hit_mean
     half = trunk.shape[0] // 2
     pair = blocks // half
@@ -384,12 +409,8 @@
     return lax.all_to_all(jnp.broadcast_to(value[None], (size, *value.shape)), axis, 0, 0)
 
 
-def join(parts):
-    top = jnp.max(parts, axis=0)
-    return top + jnp.log(jnp.sum(jnp.exp(parts - top), axis=0))
-
-
 def forward(
+    peers,
     scalars,
     covariates,
     first_weight,
@@ -397,7 +418,6 @@
     second_weight,
     second_bias,
     head_weight,
-    presence_t,
 ):
     blocks, tile, _ = first_weight.shape
     block_count, _, species = head_weight.shape
@@ -409,14 +429,13 @@
         forward_kernel,
         name="forward",
         out_shape=(
-            shape(by_clade, F32),
             shape(by_clade, BF16),
             shape(by_layer, BF16),
-            shape((block_count, species), F32),
+            shape((peers, block_count, species), F32),
             shape((block_count, species), F32),
         ),
-        in_specs=[SMEM] + [ANY] * 7,
-        out_specs=[ANY] * 3 + [VMEM] * 2,
+        in_specs=[SMEM] + [ANY] * 6,
+        out_specs=[ANY] * 2 + [VMEM] * 2,
         scratch_shapes=[
             pltpu.VMEM(covariates.shape, BF16),
             pltpu.VMEM(first_weight.shape, BF16),
@@ -424,15 +443,13 @@
             pltpu.VMEM(second_weight.shape, BF16),
             pltpu.VMEM((blocks, tile), F32),
             pltpu.VMEM(head_weight.shape, BF16),
-            pltpu.VMEM(presence_t.shape, jnp.int32),
-            pltpu.VMEM(by_clade, F32),
             pltpu.VMEM(by_clade, BF16),
             pltpu.VMEM(by_layer, BF16),
             pltpu.VMEM((block_count, tile, species), BF16),
+            pltpu.VMEM((GROUP, cells, species), F32),
             pltpu.VMEM((GROUP, 8, species), F32),
-            pltpu.SemaphoreType.DMA((7,)),
+            pltpu.SemaphoreType.DMA((6,)),
             pltpu.SemaphoreType.DMA((block_count // GROUP,)),
-            pltpu.SemaphoreType.DMA((1,)),
             pltpu.SemaphoreType.DMA((1,)),
         ],
         compiler_params=PARAMS,
@@ -444,12 +461,46 @@
         second_weight,
         second_bias.reshape(blocks, tile),
         head_weight,
-        presence_t,
-    )
-
-
-def backward(records, scalars, covariates, second_weight, head_weight, saved, lse, nx):
-    logits, hits, layers, _, hit_sum = saved
+    )
+
+
+def middle(scalars, presence_t, head_weight, layers):
+    _, *by_block = layers.shape
+    blocks, cells, tile = by_block
+    block_count, _, species = head_weight.shape
+    shape = jax.ShapeDtypeStruct
+    return pl.pallas_call(
+        middle_kernel,
+        name="middle",
+        out_shape=(
+            shape(by_block, BF16),
+            shape((block_count, tile, species), F32),
+            shape((block_count, species), F32),
+        ),
+        in_specs=[SMEM] + [ANY] * 3,
+        out_specs=[VMEM] * 3,
+        scratch_shapes=[
+            pltpu.VMEM(presence_t.shape, jnp.int32),
+            pltpu.VMEM(head_weight.shape, BF16),
+            pltpu.VMEM(by_block, BF16),
+            pltpu.VMEM((block_count, tile, species), BF16),
+            pltpu.VMEM(by_block, F32),
+            pltpu.SMEM((block_count * (cells // CHUNK) + AT_ONCE,), jnp.int32),
+            pltpu.SemaphoreType.DMA((3,)),
+        ],
+        compiler_params=PARAMS,
+        cost_estimate=pl.CostEstimate(
+            flops=8 * block_count * cells * species * tile,
+            bytes_accessed=8 * blocks * cells * tile,
+            transcendentals=0,
+        ),
+    )(scalars, presence_t, head_weight, layers)
+
+
+def backward(
+    scalars, covariates, second_weight, head_weight, terms, layers, high, lses, hits, nx
+):
+    hit_back, hit_grad, hit_sum = hits
     _, *by_block = layers.shape
     blocks, cells, tile = by_block
     block_count, slab, species = head_weight.shape
@@ -460,38 +511,39 @@
     group = block_count // 2
     half_rows = group * slab + -(-group // 8) * 8
     return pl.pallas_call(
-        functools.partial(backward_kernel, records),
+        backward_kernel,
         name="backward",
         out_shape=(
             shape((2 * nx, part_rows, tile), LINK),
             shape((half_rows, tile), F32),
             shape((half_rows, tile), F32),
+            shape((block_count, species), F32),
         ),
-        in_specs=[SMEM] + [ANY] * 8,
-        out_specs=[VMEM] * 3,
+        in_specs=[SMEM] + [ANY] * 10,
+        out_specs=[VMEM] * 4,
         scratch_shapes=[
             pltpu.VMEM(covariates.shape, BF16),
             pltpu.VMEM(second_weight.shape, BF16),
             pltpu.VMEM(head_weight.shape, BF16),
-            pltpu.VMEM(lse.shape, F32),
+            pltpu.VMEM(terms.shape, BF16),
+            pltpu.VMEM(layers.shape, BF16),
+            pltpu.VMEM(high.shape, F32),
+            pltpu.VMEM(lses.shape, F32),
+            pltpu.VMEM(by_block, BF16),
+            pltpu.VMEM(hit_grad.shape, F32),
             pltpu.VMEM(hit_sum.shape, F32),
-            pltpu.VMEM(logits.shape, F32),
-            pltpu.VMEM(hits.shape, BF16),
-            pltpu.VMEM(layers.shape, BF16),
             pltpu.VMEM((block_count, tile, species), BF16),
             pltpu.VMEM((2, half_rows, tile), F32),
             pltpu.VMEM((2 * nx, 8, tile), F32),
             pltpu.VMEM((blocks, tile, cells), BF16),
             pltpu.VMEM((blocks, tile, cells), BF16),
             pltpu.VMEM((width // tile, tile, cells), BF16),
-            pltpu.VMEM(hits.shape, BF16),
+            pltpu.VMEM(terms.shape, BF16),
             pltpu.VMEM((GROUP, tile, species), F32),
             pltpu.VMEM(by_block, F32),
             pltpu.VMEM(by_block, F32),
-            pltpu.SemaphoreType.DMA((5,)),
+            pltpu.SemaphoreType.DMA((10,)),
             pltpu.SemaphoreType.DMA((block_count // GROUP,)),
-            pltpu.SemaphoreType.DMA((1,)),
-            pltpu.SemaphoreType.DMA((2,)),
         ],
         compiler_params=PARAMS,
     )(
@@ -499,10 +551,12 @@
         covariates,
         second_weight,
         head_weight,
-        logits,
-        hits,
+        terms,
         layers,
-        lse,
+        high,
+        lses,
+        hit_back,
+        hit_grad,
         hit_sum,
     )
 
@@ -541,7 +595,8 @@
     scalars = jnp.concatenate([place, first_index, second_index, clade_block, busy])
 
     all_covariates = spread(covariates, "x", nx).reshape(cells, width)
-    saved = forward(
+    terms, layers, local_lse, high = forward(
+        ny,
         scalars,
         all_covariates,
         first_weight,
@@ -549,13 +604,21 @@
         second_weight,
         second_bias,
         head_weight,
-        presence_t,
-    )
-    lse = join(spread(saved[3], "y", ny))
-    lse = join(spread(lse, ("z", "c"), nz * 2))
-
-    trunk, keep, send = backward(
-        records, scalars, all_covariates, second_weight, head_weight, saved, lse, nx
+    )
+    lses = lax.all_to_all(local_lse, "y", 0, 0)
+    hits = middle(scalars, presence_t, head_weight, layers)
+    lses = spread(join(lses), ("z", "c"), nz * 2)
+    trunk, keep, send, lse = backward(
+        scalars,
+        all_covariates,
+        second_weight,
+        head_weight,
+        terms,
+        layers,
+        high,
+        lses,
+        hits,
+        nx,
     )
     pair, group = blocks // nx, block_count // 2
     head_rows = group * slab
@@ -597,7 +660,7 @@
     shape = jax.ShapeDtypeStruct
     species_loss, head_grad, first_grad, first_bias_grad, second_grad, second_bias_grad = (
         pl.pallas_call(
-            functools.partial(finish_kernel, total_cells, records),
+            functools.partial(finish_kernel, total_cells),
             name="finish",
             out_shape=(
                 shape((block_count, species), F32),
@@ -610,7 +673,7 @@
             in_specs=[SMEM] + [VMEM] * 4,
             out_specs=[VMEM] * 6,
             scratch_shapes=[pltpu.VMEM((2, half_rows, tile), LINK)],
-            compiler_params=PARAMS,
+            compiler_params=pltpu.CompilerParams(vmem_limit_bytes=16 << 20),
         )(scalars, trunk, head, other_head, lse)
     )
     return (

time: 149 us -> 143 us (0.960)
  blocking collectives: 73.5 us -> 50.7 us
  starting transfers between devices: 19.7 us -> 33.4 us
  waiting for transfers between devices: 18.5 us -> 22.2 us
    all_to_all x3 -> x1, blocking collectives: 56.2 us -> 17.9 us  [spread(): lax.all_to_all(jnp.broadcast_to(value[None], (size, *value.shape)), axis,...]
    all_to_all x0 -> x1, blocking collectives: none -> 14.5 us  [body(): lses = lax.all_to_all(local_lse, 'y', 0, 0)]
    all_to_all x2 -> x3, starting transfers between devices: 11.8 us -> 25.5 us  [spread(): lax.all_to_all(jnp.broadcast_to(value[None], (size, *value.shape)), axis,...]
    pallas_call x1, Pallas kernels: 12.3 us -> 8.34 us  [forward(): pl.pallas_call(forward_kernel, name='forward', out_shape=(shape(by_clade,...]
    all_to_all x2 -> x3, waiting for transfers between devices: 8.79 us -> 12.5 us  [spread(): lax.all_to_all(jnp.broadcast_to(value[None], (size, *value.shape)), axis,...]
    pallas_call x2 -> x3, Pallas kernels: 13.9 us -> 17.4 us  [the longest x1 9.03 us: backward(): pl.pallas_call(backward_kernel, name='backward', out_shape=(shape((2 * nx...]
    broadcast_in_dim x5 -> x4, local copies, waits for them, and re-layouts: 3.2 us -> 3.16 us  [spread(): jnp.broadcast_to(value[None], (size, *value.shape))]
  transfers between devices with their start and end apart: 5 -> 6, of which waited for: 4 -> 5; matrix products, arithmetic and copies ran while one was open for 3% -> 3% of each run, Pallas kernels for 0% -> 5%
where the time goes in v7:
time: 143 us; the launch traced here: 142 us
  blocking collectives  50.7 us (35%)
  starting transfers between devices  33.4 us (23%)
  Pallas kernels  25.8 us (18%)
  waiting for transfers between devices  22.2 us (16%)
  local copies, waits for them, and re-layouts  6.4 us (4%)
  other arithmetic  2.72 us (2%)
    all_to_all x3, starting transfers between devices, spread(): lax.all_to_all(jnp.broadcast_to(value[None], (size, *value.shape)), axis,...  25.5 us
    all_to_all x1, blocking collectives, body(): lax.all_to_all(cut, ('y', 'z'), 0, 0).astype(F32)  18.3 us
    all_to_all x1, blocking collectives, spread(): lax.all_to_all(jnp.broadcast_to(value[None], (size, *value.shape)), axis,...  17.9 us
    all_to_all x1, blocking collectives, body(): lses = lax.all_to_all(local_lse, 'y', 0, 0)  14.5 us
    all_to_all x3, waiting for transfers between devices, spread(): lax.all_to_all(jnp.broadcast_to(value[None], (size, *value.shape)), axis,...  12.5 us
    pallas_call x1, Pallas kernels, backward(): pl.pallas_call(backward_kernel, name='backward', out_shape=(shape((2 * nx...  9.03 us
    all_to_all x1, waiting for transfers between devices, body(): trunk = jnp.sum(lax.all_to_all(trunk, ('c', 'x'), 0, 0).astype(F32), axis=0)  8.43 us
    pallas_call x1, Pallas kernels, forward(): pl.pallas_call(forward_kernel, name='forward', out_shape=(shape(by_clade,...  8.34 us
  transfers between devices with their start and end apart: 6, of which 5 were waited for; matrix products, arithmetic and copies ran while one was open for 3% of the time, Pallas kernels for 5%

profile of v7, /device:TPU:1, one launch (start us, length us, event | category | flops | bytes accessed | tf_op | source)
XLA Modules:
  0.0 142.1 jit_solution(6569663189418023014)
XLA Ops:
  0.6 1.6 %broadcast_in_dim.13 = bf16[4,128,256]{2,1,0:T(8,128)(2,1)} broadcast(bf16[128,256]{1,0:T(8,128)(2,1)} %param.10), dimensions={1,2} | broadcast | bytes 327680 | tf_op jit(solution)/shard_map/broadcast_in_dim | solution.py:409
  2.2 4.8 %all-to-all-start = ((bf16[4,128,256]{2,1,0:T(8,128)(2,1)}), bf16[4,128,256]{2,1,0:T(8,128)(2,1)S(1)}, u32[]{:S(2)}, u32[]{:S(2)}) async-start(bf16[4,128,256]{2,1,0:T(8,128)(2,1)} %broadcast_in_dim.13), calls=%async_computation | async-start | bytes 524288 | tf_op jit(solution)/shard_map/all_to_all | solution.py:409
  7.0 1.0 compare_reduce_fusion.3
  8.1 0.1 bitcast_reduce_fusion.2
  8.2 0.1 bitcast_reduce_fusion
  8.3 0.1 copy.26
  8.4 0.1 reshape.68
  8.5 1.3 concatenate.17.scalars
  9.9 2.7 %all-to-all-done = bf16[4,128,256]{2,1,0:T(8,128)(2,1)S(1)} async-done(((bf16[4,128,256]{2,1,0:T(8,128)(2,1)}), bf16[4,128,256]{2,1,0:T(8,128)(2,1)S(1)}, u32[]{:S(2)}, u32[]{:S(2)}) %all-to-all-start) | async-done | bytes 262176 | tf_op jit(solution)/shard_map/all_to_all | solution.py:409
  12.6 0.0 copy-start.2
  12.6 0.7 copy-done.2
  13.3 8.3 %forward.1 = (bf16[20,512,128]{2,1,0:T(8,128)(2,1)}, bf16[4,8,512,128]{3,2,1,0:T(8,128)(2,1)}, f32[8,20,128]{2,1,0:T(8,128)}, f32[20,128]{1,0:T(8,128)}) custom-call(s32[118]{0:T(128)} %concatenate.17.scalars, bf16[512,256]{1,0:T(8,128)(2,1)} %bitcast.37, bf16[8,128,128]{2,1,0:T(8,128)(2,1)} %first_weight_in.1, f32[8,128]{1,0:T(8,128)} %bitcast.43, ...), custom_call_target="tpu_custom_call" | custom-call | tf_op jit(solution)/shard_map/forward/pallas_call | solution.py:428
  21.6 14.5 %all_to_all.35 = f32[8,20,128]{2,1,0:T(8,128)S(1)} all-to-all(f32[8,20,128]{2,1,0:T(8,128)} %get-tuple-element.26), channel_id=1, replica_groups=mesh['y'=8,'z'=8,'c'=2,'x'=4] {'y'}, dimensions={0} | all-to-all | bytes 163840 | tf_op jit(solution)/shard_map/all_to_all | solution.py:608
  36.2 0.7 broadcast_in_dim.15
  36.9 13.7 %all-to-all-start.2 = ((f32[16,20,128]{2,1,0:T(8,128)}), f32[16,20,128]{2,1,0:T(8,128)S(1)}, u32[]{:S(2)}, u32[]{:S(2)}) async-start(f32[16,20,128]{2,1,0:T(8,128)} %broadcast_in_dim.15), calls=%async_computation.2 | async-start | bytes 393216 | tf_op jit(solution)/shard_map/all_to_all | solution.py:409
  50.6 6.6 %middle.1 = (bf16[8,512,128]{2,1,0:T(8,128)(2,1)}, f32[20,128,128]{2,1,0:T(8,128)}, f32[20,128]{1,0:T(8,128)}) custom-call(s32[118]{0:T(128)} %concatenate.17.scalars, s32[16,2560]{1,0:T(8,128)} %bitcast.41, bf16[20,64,128]{2,1,0:T(8,128)(2,1)} %head_weight_in.5, bf16[4,8,512,128]{3,2,1,0:T(8,128)(2,1)} %get-tuple-element.24.trunk_in), custom_call_target="tpu_custom_call" | custom-call | flops 1342177280 | bytes 4194304 | tf_op jit(solution)/shard_map/middle/pallas_call | solution.py:472
  57.2 3.7 %all-to-all-done.2.lses_in = f32[16,20,128]{2,1,0:T(8,128)S(1)} async-done(((f32[16,20,128]{2,1,0:T(8,128)}), f32[16,20,128]{2,1,0:T(8,128)S(1)}, u32[]{:S(2)}, u32[]{:S(2)}) %all-to-all-start.2) | async-done | bytes 163872 | tf_op jit(solution)/shard_map/all_to_all | solution.py:409
  61.0 0.0 copy-start.3
  61.0 0.7 copy-done.3
  61.7 9.0 %backward.1 = (bf16[8,264,128]{2,1,0:T(8,128)(2,1)}, f32[656,128]{1,0:T(8,128)}, f32[656,128]{1,0:T(8,128)}, f32[20,128]{1,0:T(8,128)}) custom-call(s32[118]{0:T(128)} %concatenate.17.scalars, bf16[512,256]{1,0:T(8,128)(2,1)} %bitcast.38, bf16[8,128,128]{2,1,0:T(8,128)(2,1)} %second_weight_in.3, bf16[20,64,128]{2,1,0:T(8,128)(2,1)} %head_weight_in.5, ...), custom_call_target="tpu_custom_call" | custom-call | tf_op jit(solution)/shard_map/backward/pallas_call | solution.py:513
  70.7 1.9 %collective-permute-start = (f32[656,128]{1,0:T(8,128)}, f32[656,128]{1,0:T(8,128)S(1)}, u32[]{:S(2)}, u32[]{:S(2)}) collective-permute-start(f32[656,128]{1,0:T(8,128)} %get-tuple-element.32), channel_id=1, source_target_pairs={{0,4},{4,0},{1,5},{5,1},{2,6},{6,2},{3,7},{7,3},{8,12},{12,8},{9,1... | collective-permute-start | bytes 1007624 | tf_op jit(solution)/shard_map/ppermute | solution.py:627
  72.6 4.0 %all-to-all-start.3 = ((bf16[8,264,128]{2,1,0:T(8,128)(2,1)}), bf16[8,264,128]{2,1,0:T(8,128)(2,1)S(1)}, u32[]{:S(2)}, u32[]{:S(2)}) async-start(bf16[8,264,128]{2,1,0:T(8,128)(2,1)} %get-tuple-element.30), calls=%async_computation.3 | async-start | bytes 1081344 | tf_op jit(solution)/shard_map/all_to_all | solution.py:628
  76.6 0.0 collective-permute-done
  76.6 1.0 add_convert_fusion
  77.6 0.1 reshape.62
  77.7 8.4 %all-to-all-done.3 = bf16[8,264,128]{2,1,0:T(8,128)(2,1)S(1)} async-done(((bf16[8,264,128]{2,1,0:T(8,128)(2,1)}), bf16[8,264,128]{2,1,0:T(8,128)(2,1)S(1)}, u32[]{:S(2)}, u32[]{:S(2)}) %all-to-all-start.3) | async-done | bytes 540704 | tf_op jit(solution)/shard_map/all_to_all | solution.py:628
  86.1 0.1 reduce.9
  86.3 0.0 copy-start
  86.3 0.0 copy-start.1
  86.3 0.2 fusion.5
  86.5 18.3 %all_to_all.36 = bf16[64,16,128]{2,1,0:T(8,128)(2,1)S(1)} all-to-all(bf16[64,16,128]{2,1,0:T(8,128)(2,1)S(1)} %fusion.5), channel_id=1, replica_groups=mesh['y'=8,'z'=8,'c'=2,'x'=4] {'y','z'}, dimensions={0} | all-to-all | bytes 524288 | tf_op jit(solution)/shard_map/all_to_all | solution.py:642
  104.8 0.1 reduce_sum.22
  105.0 17.9 %all_to_all.37 = bf16[64,16,128]{2,1,0:T(8,128)(2,1)S(1)} all-to-all(bf16[64,16,128]{2,1,0:T(8,128)(2,1)S(1)} %broadcast_in_dim.34), channel_id=1, replica_groups=mesh['y'=8,'z'=8,'c'=2,'x'=4] {'y','z'}, dimensions={0} | all-to-all | bytes 524288 | tf_op jit(solution)/shard_map/all_to_all | solution.py:409
  122.9 0.9 broadcast_in_dim.35
  123.8 7.0 %all-to-all-start.6 = ((bf16[8,264,128]{2,1,0:T(8,128)(2,1)}), bf16[8,264,128]{2,1,0:T(8,128)(2,1)S(1)}, u32[]{:S(2)}, u32[]{:S(2)}) async-start(bf16[8,264,128]{2,1,0:T(8,128)(2,1)} %broadcast_in_dim.35), calls=%async_computation.6 | async-start | bytes 1081344 | tf_op jit(solution)/shard_map/all_to_all | solution.py:409
  130.7 0.1 slice.103
  130.8 0.1 reshape.64
  130.9 2.0 %collective-permute-start.1 = (bf16[656,128]{1,0:T(8,128)(2,1)S(1)}, bf16[656,128]{1,0:T(8,128)(2,1)S(1)}, u32[]{:S(2)}, u32[]{:S(2)}) collective-permute-start(bf16[656,128]{1,0:T(8,128)(2,1)S(1)} %fusion.6.own), channel_id=1, source_target_pairs={{0,4},{4,0},{1,5},{5,1},{2,6},{6,2},{3,7},{7,3},{8,12},{12,8},{9,1... | collective-permute-start | bytes 503816 | tf_op jit(solution)/shard_map/ppermute | solution.py:652
  132.9 1.3 collective-permute-done.1.other
  134.2 6.0 %all-to-all-done.6.trunk = bf16[8,264,128]{2,1,0:T(8,128)(2,1)S(1)} async-done(((bf16[8,264,128]{2,1,0:T(8,128)(2,1)}), bf16[8,264,128]{2,1,0:T(8,128)(2,1)S(1)}, u32[]{:S(2)}, u32[]{:S(2)}) %all-to-all-start.6) | async-done | bytes 540704 | tf_op jit(solution)/shard_map/all_to_all | solution.py:409
  140.3 0.0 copy-done
  140.3 0.0 copy-done.1
  140.3 1.8 %finish.1 = (f32[20,128]{1,0:T(8,128)}, f32[20,64,128]{2,1,0:T(8,128)}, f32[8,128,128]{2,1,0:T(8,128)}, f32[8,128]{1,0:T(8,128)}, f32[8,128,128]{2,1,0:T(8,128)}, /*index=5*/f32[8,128]{1,0:T(8,128)}) custom-call(s32[118]{0:T(128)S(1)} %copy-done.1, bf16[8,264,128]{2,1,0:T(8,128)(2,1)S(1)} %all-to-all-done.6.trunk, bf16[656,128]{1,0:T(8,128)(2,1)S(1)} %fusion.6.own, ...), custom_call_target="tpu_custom_call" | custom-call | tf_op jit(solution)/shard_map/finish/pallas_call | solution.py:662
  (16 shorter events, 0.2 us)
Async XLA Ops:
  2.2 10.4 %all-to-all-start = ((bf16[4,128,256]{2,1,0:T(8,128)(2,1)}), bf16[4,128,256]{2,1,0:T(8,128)(2,1)S(1)}, u32[]{:S(2)}, u32[]{:S(2)}) async-start(bf16[4,128,256]{2,1,0:T(8,128)(2,1)} %broadcast_in_dim.13), calls=%async_computation | async-start | bytes 524288 | tf_op jit(solution)/shard_map/all_to_all | solution.py:409
  12.6 0.7 copy-start.2
  36.9 24.1 %all-to-all-start.2 = ((f32[16,20,128]{2,1,0:T(8,128)}), f32[16,20,128]{2,1,0:T(8,128)S(1)}, u32[]{:S(2)}, u32[]{:S(2)}) async-start(f32[16,20,128]{2,1,0:T(8,128)} %broadcast_in_dim.15), calls=%async_computation.2 | async-start | bytes 393216 | tf_op jit(solution)/shard_map/all_to_all | solution.py:409
  61.0 0.7 copy-start.3
  70.7 5.9 %collective-permute-start = (f32[656,128]{1,0:T(8,128)}, f32[656,128]{1,0:T(8,128)S(1)}, u32[]{:S(2)}, u32[]{:S(2)}) collective-permute-start(f32[656,128]{1,0:T(8,128)} %get-tuple-element.32), channel_id=1, source_target_pairs={{0,4},{4,0},{1,5},{5,1},{2,6},{6,2},{3,7},{7,3},{8,12},{12,8},{9,1... | collective-permute-start | bytes 1007624 | tf_op jit(solution)/shard_map/ppermute | solution.py:627
  72.6 13.5 %all-to-all-start.3 = ((bf16[8,264,128]{2,1,0:T(8,128)(2,1)}), bf16[8,264,128]{2,1,0:T(8,128)(2,1)S(1)}, u32[]{:S(2)}, u32[]{:S(2)}) async-start(bf16[8,264,128]{2,1,0:T(8,128)(2,1)} %get-tuple-element.30), calls=%async_computation.3 | async-start | bytes 1081344 | tf_op jit(solution)/shard_map/all_to_all | solution.py:628
  86.3 54.0 %copy-start = (f32[20,128]{1,0:T(8,128)S(1)}, f32[20,128]{1,0:T(8,128)}, u32[]{:S(2)}) copy-start(f32[20,128]{1,0:T(8,128)} %get-tuple-element.33.lse) | copy-start | bytes 30724
  86.3 54.0 %copy-start.1 = (s32[118]{0:T(128)S(1)}, s32[118]{0:T(128)}, u32[]{:S(2)}) copy-start(s32[118]{0:T(128)} %concatenate.17.scalars) | copy-start | bytes 1420
  123.8 16.5 %all-to-all-start.6 = ((bf16[8,264,128]{2,1,0:T(8,128)(2,1)}), bf16[8,264,128]{2,1,0:T(8,128)(2,1)S(1)}, u32[]{:S(2)}, u32[]{:S(2)}) async-start(bf16[8,264,128]{2,1,0:T(8,128)(2,1)} %broadcast_in_dim.35), calls=%async_computation.6 | async-start | bytes 1081344 | tf_op jit(solution)/shard_map/all_to_all | solution.py:409
  130.9 3.3 %collective-permute-start.1 = (bf16[656,128]{1,0:T(8,128)(2,1)S(1)}, bf16[656,128]{1,0:T(8,128)(2,1)S(1)}, u32[]{:S(2)}, u32[]{:S(2)}) collective-permute-start(bf16[656,128]{1,0:T(8,128)(2,1)S(1)} %fusion.6.own), channel_id=1, source_target_pairs={{0,4},{4,0},{1,5},{5,1},{2,6},{6,2},{3,7},{7,3},{8,12},{12,8},{9,1... | collective-permute-start | bytes 503816 | tf_op jit(solution)/shard_map/ppermute | solution.py:652

commit v8 on v7

--- a/solution.py
+++ b/solution.py
@@ -179,6 +179,53 @@
     return top + jnp.log(sum(jnp.exp(parts[i] - top) for i in range(len(parts))))
 
 
+def early_kernel(
+    scalars,
+    covariates_in,
+    trunk_in,
+    terms_in,
+    covariates_t,
+    first_act_t,
+    soft_grad,
+    covariates,
+    layers,
+    terms,
+    features_t,
+    product,
+    fetch_sem,
+    term_sem,
+):
+    _, blocks, cells, tile = layers.shape
+    block_count, slab, _ = soft_grad.shape
+    _, _, clade, _, _ = scalar_parts(scalars, blocks, block_count)
+    fetched = fetch(
+        fetch_sem,
+        (trunk_in.at[1], layers.at[1]),
+        (trunk_in.at[0], layers.at[0]),
+        (covariates_in, covariates),
+    )
+    pieces = [pl.ds(i * GROUP, GROUP) for i in range(block_count // GROUP)]
+    term_copies = fetch(term_sem, *[(terms_in.at[p], terms.at[p]) for p in pieces])
+    fetched[0].wait()
+    for o in range(blocks):
+        features_t[o] = layers[1, o].T
+    fetched[1].wait()
+    for o in range(blocks):
+        first_act_t[o] = layers[0, o].T
+    fetched[2].wait()
+    for o in range(covariates.shape[1] // tile):
+        covariates_t[o] = covariates[:, o * tile : (o + 1) * tile].T
+    for i, copy in enumerate(term_copies):
+        copy.wait()
+        for g in range(GROUP):
+            b = i * GROUP + g
+            product[g] = dot(features_t[clade[b] // 2], terms[b])
+        for g in range(GROUP):
+            b = i * GROUP + g
+            half = pl.ds(pl.multiple_of((clade[b] % 2) * slab, slab), slab)
+            soft_grad[b] = product[g, half, :]
+
+
 def middle_kernel(
     scalars,
     presence_in,
@@ -240,13 +287,15 @@
 
 def backward_kernel(
     scalars,
-    covariates_in,
     second_weight_in,
     head_weight_in,
     terms_in,
     trunk_in,
     high_in,
     lses_in,
+    covariates_t_in,
+    first_act_t_in,
+    soft_grad_in,
     hit_back_in,
     hit_grad_in,
     hit_sum_in,
@@ -254,31 +303,29 @@
     keep,
     send,
     lse,
-    covariates,
     second_weight,
     head_weight,
     terms,
-    layers,
+    slopes,
     high,
     lses,
+    covariates_t,
+    first_act_t,
+    soft_grad,
     hit_back,
     hit_grad,
     hit_sum,
     wide_weight,
     packed,
     bias,
-    features_t,
-    first_act_t,
-    covariates_t,
     weight_cells,
-    slab_grad,
     group_back,
     act_grad,
     fetch_sem,
     term_sem,
 ):
-    first_act, features, first_slope, second_slope = (layers.at[i] for i in range(4))
-    blocks, cells, tile = features.shape
+    first_slope, second_slope = slopes.at[0], slopes.at[1]
+    blocks, cells, tile = first_slope.shape
     block_count, slab, _ = head_weight.shape
     first_index, second_index, clade, _, place = scalar_parts(scalars, blocks, block_count)
     early = fetch(
@@ -286,18 +333,19 @@
         (lses_in, lses),
         (high_in, high),
         (head_weight_in, head_weight),
-        (trunk_in.at[pl.ds(0, 2)], layers.at[pl.ds(0, 2)]),
-        (covariates_in, covariates),
     )
     pieces = [pl.ds(i * GROUP, GROUP) for i in range(block_count // GROUP)]
     term_copies = fetch(term_sem, *[(terms_in.at[p], terms.at[p]) for p in pieces])
     late = fetch(
-        fetch_sem.at[pl.ds(len(early), 5)],
+        fetch_sem.at[pl.ds(len(early), 8)],
         (hit_back_in, hit_back),
         (hit_grad_in, hit_grad),
+        (soft_grad_in, soft_grad),
+        (trunk_in.at[pl.ds(2, 2)], slopes),
+        (first_act_t_in, first_act_t),
+        (second_weight_in, second_weight),
+        (covariates_t_in, covariates_t),
         (hit_sum_in, hit_sum),
-        (trunk_in.at[pl.ds(2, 2)], layers.at[pl.ds(2, 2)]),
-        (second_weight_in, second_weight),
     )
     early[0].wait()
     early[1].wait()
@@ -305,13 +353,6 @@
     high[...] = jnp.exp(high[...] - lse[...])
     early[2].wait()
     widen(wide_weight, head_weight, clade)
-    early[3].wait()
-    for o in range(blocks):
-        features_t[o] = features[o].T
-        first_act_t[o] = first_act[o].T
-    early[4].wait()
-    for o in range(covariates.shape[1] // tile):
-        covariates_t[o] = covariates[:, o * tile : (o + 1) * tile].T
     group = block_count // 2
     core = place[1]
 
@@ -321,22 +362,21 @@
         for b in range(i * GROUP, (i + 1) * GROUP):
             weights = terms[b].astype(F32) * high[b : b + 1, :]
             weight_cells[b] = weights.astype(BF16)
-    for copy in late:
+    for copy in late[:3]:
         copy.wait()
     for o in range(blocks):
         group_back[o] = -hit_back[o].astype(F32)
     for i in range(block_count // GROUP):
         for g in range(GROUP):
             b = i * GROUP + g
-            slab_grad[g] = dot(features_t[clade[b] // 2], weight_cells[b])
-        for g in range(GROUP):
-            b = i * GROUP + g
             half = pl.ds(pl.multiple_of((clade[b] % 2) * slab, slab), slab)
             rows = slice((b % group) * slab, (b % group + 1) * slab)
-            grad = slab_grad[g, half, :] - hit_grad[b, half, :]
+            grad = soft_grad[b] * high[b : b + 1, :] - hit_grad[b, half, :]
             packed[b // group, rows, :] = grad
             group_back[clade[b] // 2] += dot_t(weight_cells[b], wide_weight[b])
 
+    for copy in late[3:]:
+        copy.wait()
     bias[...] = jnp.zeros_like(bias)
     pair = blocks // (trunk.shape[0] // 2)
 
@@ -464,6 +504,37 @@
     )
 
 
+def early(scalars, covariates, layers, terms, slab):
+    _, blocks, cells, tile = layers.shape
+    block_count, _, species = terms.shape
+    width = covariates.shape[1]
+    shape = jax.ShapeDtypeStruct
+    return pl.pallas_call(
+        early_kernel,
+        name="early",
+        out_shape=(
+            shape((width // tile, tile, cells), BF16),
+            shape((blocks, tile, cells), BF16),
+            shape((block_count, slab, species), F32),
+        ),
+        in_specs=[SMEM] + [ANY] * 3,
+        out_specs=[VMEM] * 3,
+        scratch_shapes=[
+            pltpu.VMEM(covariates.shape, BF16),
+            pltpu.VMEM((2, blocks, cells, tile), BF16),
+            pltpu.VMEM(terms.shape, BF16),
+            pltpu.VMEM((blocks, tile, cells), BF16),
+            pltpu.VMEM((GROUP, tile, species), F32),
+            pltpu.SemaphoreType.DMA((3,)),
+            pltpu.SemaphoreType.DMA((block_count // GROUP,)),
+        ],
+        compiler_params=PARAMS,
+        cost_estimate=pl.CostEstimate(
+            flops=2 * terms.size * tile, bytes_accessed=6 * terms.size, transcendentals=0
+        ),
+    )(scalars, covariates, layers, terms)
+
+
 def middle(scalars, presence_t, head_weight, layers):
     _, *by_block = layers.shape
     blocks, cells, tile = by_block
@@ -498,13 +569,13 @@
 
 
 def backward(
-    scalars, covariates, second_weight, head_weight, terms, layers, high, lses, hits, nx
+    scalars, second_weight, head_weight, terms, layers, high, lses, ready, hits, nx
 ):
+    covariates_t, first_act_t, soft_grad = ready
     hit_back, hit_grad, hit_sum = hits
     _, *by_block = layers.shape
     blocks, cells, tile = by_block
     block_count, slab, species = head_weight.shape
-    width = covariates.shape[1]
     shape = jax.ShapeDtypeStruct
     pair = blocks // nx
     part_rows = pair * tile + 8
@@ -519,42 +590,42 @@
             shape((half_rows, tile), F32),
             shape((block_count, species), F32),
         ),
-        in_specs=[SMEM] + [ANY] * 10,
+        in_specs=[SMEM] + [ANY] * 12,
         out_specs=[VMEM] * 4,
         scratch_shapes=[
-            pltpu.VMEM(covariates.shape, BF16),
             pltpu.VMEM(second_weight.shape, BF16),
             pltpu.VMEM(head_weight.shape, BF16),
             pltpu.VMEM(terms.shape, BF16),
-            pltpu.VMEM(layers.shape, BF16),
+            pltpu.VMEM((2, *by_block), BF16),
             pltpu.VMEM(high.shape, F32),
             pltpu.VMEM(lses.shape, F32),
+            pltpu.VMEM(covariates_t.shape, BF16),
+            pltpu.VMEM(first_act_t.shape, BF16),
+            pltpu.VMEM(soft_grad.shape, F32),
             pltpu.VMEM(by_block, BF16),
             pltpu.VMEM(hit_grad.shape, F32),
             pltpu.VMEM(hit_sum.shape, F32),
             pltpu.VMEM((block_count, tile, species), BF16),
             pltpu.VMEM((2, half_rows, tile), F32),
             pltpu.VMEM((2 * nx, 8, tile), F32),
-            pltpu.VMEM((blocks, tile, cells), BF16),
-            pltpu.VMEM((blocks, tile, cells), BF16),
-            pltpu.VMEM((width // tile, tile, cells), BF16),
             pltpu.VMEM(terms.shape, BF16),
-            pltpu.VMEM((GROUP, tile, species), F32),
             pltpu.VMEM(by_block, F32),
             pltpu.VMEM(by_block, F32),
-            pltpu.SemaphoreType.DMA((10,)),
+            pltpu.SemaphoreType.DMA((11,)),
             pltpu.SemaphoreType.DMA((block_count // GROUP,)),
         ],
         compiler_params=PARAMS,
     )(
         scalars,
-        covariates,
         second_weight,
         head_weight,
         terms,
         layers,
         high,
         lses,
+        covariates_t,
+        first_act_t,
+        soft_grad,
         hit_back,
         hit_grad,
         hit_sum,
@@ -606,17 +677,19 @@
         head_weight,
     )
     lses = lax.all_to_all(local_lse, "y", 0, 0)
-    hits = middle(scalars, presence_t, head_weight, layers)
-    lses = spread(join(lses), ("z", "c"), nz * 2)
+    ready = early(scalars, all_covariates, layers, terms, slab)
+    lses, ready, later = lax.optimization_barrier((join(lses), ready, scalars))
+    hits = middle(later, presence_t, head_weight, layers)
+    lses = spread(lses, ("z", "c"), nz * 2)
     trunk, keep, send, lse = backward(
         scalars,
-        all_covariates,
         second_weight,
         head_weight,
         terms,
         layers,
         high,
         lses,
+        ready,
         hits,
         nx,
     )

time: 143 us -> 144 us (level)
  blocking collectives: 50.7 us -> 37.6 us
  starting transfers between devices: 33.4 us -> 40.3 us
  Pallas kernels: 25.8 us -> 31.3 us
  waiting for transfers between devices: 22.2 us -> 23.7 us
    all_to_all x1 -> x0, blocking collectives: 14.5 us -> none  [body(): lses = lax.all_to_all(local_lse, 'y', 0, 0)]
    all_to_all x0 -> x1, starting transfers between devices: none -> 6.86 us  [body(): lses = lax.all_to_all(local_lse, 'y', 0, 0)]
    pallas_call x0 -> x1, Pallas kernels: none -> 4.9 us  [early(): pl.pallas_call(early_kernel, name='early', out_shape=(shape((width // til...]
    all_to_all x0 -> x1, waiting for transfers between devices: none -> 2.78 us  [body(): lses = lax.all_to_all(local_lse, 'y', 0, 0)]
  transfers between devices with their start and end apart: 6 -> 7, of which waited for: 5 -> 6; matrix products, arithmetic and copies ran while one was open for 3% -> 3% of each run, Pallas kernels for 5% -> 9%
where the time goes in v8:
time: 144 us; the launch traced here: 143 us
  starting transfers between devices  40.3 us (28%)
  blocking collectives  37.6 us (26%)
  Pallas kernels  31.3 us (22%)
  waiting for transfers between devices  23.7 us (16%)
  local copies, waits for them, and re-layouts  6.4 us (4%)
  other arithmetic  2.72 us (2%)
    all_to_all x3, starting transfers between devices, spread(): lax.all_to_all(jnp.broadcast_to(value[None], (size, *value.shape)), axis,...  25.5 us
    all_to_all x1, blocking collectives, body(): lax.all_to_all(cut, ('y', 'z'), 0, 0).astype(F32)  19.8 us
    all_to_all x1, blocking collectives, spread(): lax.all_to_all(jnp.broadcast_to(value[None], (size, *value.shape)), axis,...  17.9 us
    all_to_all x3, waiting for transfers between devices, spread(): lax.all_to_all(jnp.broadcast_to(value[None], (size, *value.shape)), axis,...  11.2 us
    all_to_all x1, waiting for transfers between devices, body(): trunk = jnp.sum(lax.all_to_all(trunk, ('c', 'x'), 0, 0).astype(F32), axis=0)  8.43 us
    pallas_call x1, Pallas kernels, backward(): pl.pallas_call(backward_kernel, name='backward', out_shape=(shape((2 * nx...  8.43 us
    pallas_call x1, Pallas kernels, forward(): pl.pallas_call(forward_kernel, name='forward', out_shape=(shape(by_clade,...  8.33 us
    pallas_call x1, Pallas kernels, middle(): pl.pallas_call(middle_kernel, name='middle', out_shape=(shape(by_block, B...  7.82 us
  transfers between devices with their start and end apart: 7, of which 6 were waited for; matrix products, arithmetic and copies ran while one was open for 3% of the time, Pallas kernels for 9%

profile of v8, /device:TPU:1, one launch (start us, length us, event | category | flops | bytes accessed | tf_op | source)
XLA Modules:
  0.0 142.9 jit_solution(6915481068111515782)
XLA Ops:
  0.6 1.6 %broadcast_in_dim.11 = bf16[4,128,256]{2,1,0:T(8,128)(2,1)} broadcast(bf16[128,256]{1,0:T(8,128)(2,1)} %param.10), dimensions={1,2} | broadcast | bytes 327680 | tf_op jit(solution)/shard_map/broadcast_in_dim | solution.py:449
  2.2 4.8 %all-to-all-start = ((bf16[4,128,256]{2,1,0:T(8,128)(2,1)}), bf16[4,128,256]{2,1,0:T(8,128)(2,1)S(1)}, u32[]{:S(2)}, u32[]{:S(2)}) async-start(bf16[4,128,256]{2,1,0:T(8,128)(2,1)} %broadcast_in_dim.11), calls=%async_computation | async-start | bytes 524288 | tf_op jit(solution)/shard_map/all_to_all | solution.py:449
  7.0 1.0 compare_reduce_fusion.3
  8.1 0.1 bitcast_reduce_fusion.2
  8.2 0.1 bitcast_reduce_fusion
  8.3 0.1 copy.26
  8.4 0.1 reshape.69
  8.5 1.4 concatenate.17.scalars
  9.9 2.7 %all-to-all-done = bf16[4,128,256]{2,1,0:T(8,128)(2,1)S(1)} async-done(((bf16[4,128,256]{2,1,0:T(8,128)(2,1)}), bf16[4,128,256]{2,1,0:T(8,128)(2,1)S(1)}, u32[]{:S(2)}, u32[]{:S(2)}) %all-to-all-start) | async-done | bytes 262176 | tf_op jit(solution)/shard_map/all_to_all | solution.py:449
  12.6 0.0 copy-start.2
  12.6 0.7 copy-done.2
  13.3 8.3 %forward.1 = (bf16[20,512,128]{2,1,0:T(8,128)(2,1)}, bf16[4,8,512,128]{3,2,1,0:T(8,128)(2,1)}, f32[8,20,128]{2,1,0:T(8,128)}, f32[20,128]{1,0:T(8,128)}) custom-call(s32[118]{0:T(128)} %concatenate.17.scalars, bf16[512,256]{1,0:T(8,128)(2,1)} %bitcast.67, bf16[8,128,128]{2,1,0:T(8,128)(2,1)} %first_weight_in.1, f32[8,128]{1,0:T(8,128)} %bitcast.73, ...), custom_call_target="tpu_custom_call" | custom-call | tf_op jit(solution)/shard_map/forward/pallas_call | solution.py:468
  21.6 6.9 %all-to-all-start.1 = ((f32[8,20,128]{2,1,0:T(8,128)}), f32[8,20,128]{2,1,0:T(8,128)S(1)}, u32[]{:S(2)}, u32[]{:S(2)}) async-start(f32[8,20,128]{2,1,0:T(8,128)} %get-tuple-element.34), calls=%async_computation.1 | async-start | bytes 196608 | tf_op jit(solution)/shard_map/all_to_all | solution.py:679
  28.5 4.9 %early.1 = (bf16[2,128,512]{2,1,0:T(8,128)(2,1)}, bf16[8,128,512]{2,1,0:T(8,128)(2,1)}, f32[20,64,128]{2,1,0:T(8,128)}) custom-call(s32[118]{0:T(128)} %concatenate.17.scalars, bf16[512,256]{1,0:T(8,128)(2,1)} %bitcast.68, bf16[4,8,512,128]{3,2,1,0:T(8,128)(2,1)} %get-tuple-element.32.trunk_in, bf16[20,512,128]{2,1,0:T(8,128)(2,1)} %get-tuple-element.31.terms_in), custom_call_target="tpu_custom_call" | custom-call | flops 335544320 | bytes 7864320 | tf_op jit(solution)/shard_map/early/pallas_call | solution.py:512
  33.4 2.8 %all-to-all-done.1 = f32[8,20,128]{2,1,0:T(8,128)S(1)} async-done(((f32[8,20,128]{2,1,0:T(8,128)}), f32[8,20,128]{2,1,0:T(8,128)S(1)}, u32[]{:S(2)}, u32[]{:S(2)}) %all-to-all-start.1) | async-done | bytes 81952 | tf_op jit(solution)/shard_map/all_to_all | solution.py:679
  36.2 0.7 broadcast_in_dim.12
  36.9 13.7 %all-to-all-start.2 = ((f32[16,20,128]{2,1,0:T(8,128)}), f32[16,20,128]{2,1,0:T(8,128)S(1)}, u32[]{:S(2)}, u32[]{:S(2)}) async-start(f32[16,20,128]{2,1,0:T(8,128)} %broadcast_in_dim.12), calls=%async_computation.2 | async-start | bytes 393216 | tf_op jit(solution)/shard_map/all_to_all | solution.py:449
  50.6 7.8 %middle.1 = (bf16[8,512,128]{2,1,0:T(8,128)(2,1)}, f32[20,128,128]{2,1,0:T(8,128)}, f32[20,128]{1,0:T(8,128)}) custom-call(s32[118]{0:T(128)} %concatenate.17.scalars, s32[16,2560]{1,0:T(8,128)} %bitcast.71, bf16[20,64,128]{2,1,0:T(8,128)(2,1)} %head_weight_in.5, bf16[4,8,512,128]{3,2,1,0:T(8,128)(2,1)} %get-tuple-element.32.trunk_in), custom_call_target="tpu_custom_call" | custom-call | flops 1342177280 | bytes 4194304 | tf_op jit(solution)/shard_map/middle/pallas_call | solution.py:543
  58.4 2.5 %all-to-all-done.2.lses_in = f32[16,20,128]{2,1,0:T(8,128)S(1)} async-done(((f32[16,20,128]{2,1,0:T(8,128)}), f32[16,20,128]{2,1,0:T(8,128)S(1)}, u32[]{:S(2)}, u32[]{:S(2)}) %all-to-all-start.2) | async-done | bytes 163872 | tf_op jit(solution)/shard_map/all_to_all | solution.py:449
  60.9 0.0 copy-start.3
  60.9 0.7 copy-done.3
  61.6 8.4 %backward.1 = (bf16[8,264,128]{2,1,0:T(8,128)(2,1)}, f32[656,128]{1,0:T(8,128)}, f32[656,128]{1,0:T(8,128)}, f32[20,128]{1,0:T(8,128)}) custom-call(s32[118]{0:T(128)} %concatenate.17.scalars, bf16[8,128,128]{2,1,0:T(8,128)(2,1)} %second_weight_in.3, bf16[20,64,128]{2,1,0:T(8,128)(2,1)} %head_weight_in.5, bf16[20,512,128]{2,1,0:T(8,128)(2,1)} %get-tuple-element.31.terms_in, ...), custom_call_target="tpu_custom_call" | custom-call | tf_op jit(solution)/shard_map/backward/pallas_call | solution.py:584
  70.1 1.9 %collective-permute-start = (f32[656,128]{1,0:T(8,128)}, f32[656,128]{1,0:T(8,128)S(1)}, u32[]{:S(2)}, u32[]{:S(2)}) collective-permute-start(f32[656,128]{1,0:T(8,128)} %get-tuple-element.48), channel_id=1, source_target_pairs={{0,4},{4,0},{1,5},{5,1},{2,6},{6,2},{3,7},{7,3},{8,12},{12,8},{9,1... | collective-permute-start | bytes 1007624 | tf_op jit(solution)/shard_map/ppermute | solution.py:700
  72.0 4.0 %all-to-all-start.3 = ((bf16[8,264,128]{2,1,0:T(8,128)(2,1)}), bf16[8,264,128]{2,1,0:T(8,128)(2,1)S(1)}, u32[]{:S(2)}, u32[]{:S(2)}) async-start(bf16[8,264,128]{2,1,0:T(8,128)(2,1)} %get-tuple-element.46), calls=%async_computation.3 | async-start | bytes 1081344 | tf_op jit(solution)/shard_map/all_to_all | solution.py:701
  76.0 0.0 collective-permute-done
  76.0 1.0 add_convert_fusion
  77.0 0.1 reshape.63
  77.1 8.4 %all-to-all-done.3 = bf16[8,264,128]{2,1,0:T(8,128)(2,1)S(1)} async-done(((bf16[8,264,128]{2,1,0:T(8,128)(2,1)}), bf16[8,264,128]{2,1,0:T(8,128)(2,1)S(1)}, u32[]{:S(2)}, u32[]{:S(2)}) %all-to-all-start.3) | async-done | bytes 540704 | tf_op jit(solution)/shard_map/all_to_all | solution.py:701
  85.5 0.1 reduce.9
  85.7 0.0 copy-start
  85.7 0.0 copy-start.1
  85.7 0.2 fusion.5
  85.9 19.8 %all_to_all.35 = bf16[64,16,128]{2,1,0:T(8,128)(2,1)S(1)} all-to-all(bf16[64,16,128]{2,1,0:T(8,128)(2,1)S(1)} %fusion.5), channel_id=1, replica_groups=mesh['y'=8,'z'=8,'c'=2,'x'=4] {'y','z'}, dimensions={0} | all-to-all | bytes 524288 | tf_op jit(solution)/shard_map/all_to_all | solution.py:715
  105.7 0.1 reduce_sum.22
  105.8 17.9 %all_to_all.36 = bf16[64,16,128]{2,1,0:T(8,128)(2,1)S(1)} all-to-all(bf16[64,16,128]{2,1,0:T(8,128)(2,1)S(1)} %broadcast_in_dim.14), channel_id=1, replica_groups=mesh['y'=8,'z'=8,'c'=2,'x'=4] {'y','z'}, dimensions={0} | all-to-all | bytes 524288 | tf_op jit(solution)/shard_map/all_to_all | solution.py:449
  123.7 0.9 broadcast_in_dim.15
  124.6 7.0 %all-to-all-start.6 = ((bf16[8,264,128]{2,1,0:T(8,128)(2,1)}), bf16[8,264,128]{2,1,0:T(8,128)(2,1)S(1)}, u32[]{:S(2)}, u32[]{:S(2)}) async-start(bf16[8,264,128]{2,1,0:T(8,128)(2,1)} %broadcast_in_dim.15), calls=%async_computation.6 | async-start | bytes 1081344 | tf_op jit(solution)/shard_map/all_to_all | solution.py:449
  131.6 0.1 slice.103
  131.7 0.1 reshape.65
  131.8 2.0 %collective-permute-start.1 = (bf16[656,128]{1,0:T(8,128)(2,1)S(1)}, bf16[656,128]{1,0:T(8,128)(2,1)S(1)}, u32[]{:S(2)}, u32[]{:S(2)}) collective-permute-start(bf16[656,128]{1,0:T(8,128)(2,1)S(1)} %fusion.6.own), channel_id=1, source_target_pairs={{0,4},{4,0},{1,5},{5,1},{2,6},{6,2},{3,7},{7,3},{8,12},{12,8},{9,1... | collective-permute-start | bytes 503816 | tf_op jit(solution)/shard_map/ppermute | solution.py:725
  133.8 1.3 collective-permute-done.1.other
  135.0 6.0 %all-to-all-done.6.trunk = bf16[8,264,128]{2,1,0:T(8,128)(2,1)S(1)} async-done(((bf16[8,264,128]{2,1,0:T(8,128)(2,1)}), bf16[8,264,128]{2,1,0:T(8,128)(2,1)S(1)}, u32[]{:S(2)}, u32[]{:S(2)}) %all-to-all-start.6) | async-done | bytes 540704 | tf_op jit(solution)/shard_map/all_to_all | solution.py:449
  141.1 0.0 copy-done
  141.1 0.0 copy-done.1
  141.1 1.8 %finish.1 = (f32[20,128]{1,0:T(8,128)}, f32[20,64,128]{2,1,0:T(8,128)}, f32[8,128,128]{2,1,0:T(8,128)}, f32[8,128]{1,0:T(8,128)}, f32[8,128,128]{2,1,0:T(8,128)}, /*index=5*/f32[8,128]{1,0:T(8,128)}) custom-call(s32[118]{0:T(128)S(1)} %copy-done, bf16[8,264,128]{2,1,0:T(8,128)(2,1)S(1)} %all-to-all-done.6.trunk, bf16[656,128]{1,0:T(8,128)(2,1)S(1)} %fusion.6.own, ...), custom_call_target="tpu_custom_call" | custom-call | tf_op jit(solution)/shard_map/finish/pallas_call | solution.py:735
  (16 shorter events, 0.2 us)
Async XLA Ops:
  2.2 10.4 %all-to-all-start = ((bf16[4,128,256]{2,1,0:T(8,128)(2,1)}), bf16[4,128,256]{2,1,0:T(8,128)(2,1)S(1)}, u32[]{:S(2)}, u32[]{:S(2)}) async-start(bf16[4,128,256]{2,1,0:T(8,128)(2,1)} %broadcast_in_dim.11), calls=%async_computation | async-start | bytes 524288 | tf_op jit(solution)/shard_map/all_to_all | solution.py:449
  12.6 0.7 copy-start.2
  21.6 14.5 %all-to-all-start.1 = ((f32[8,20,128]{2,1,0:T(8,128)}), f32[8,20,128]{2,1,0:T(8,128)S(1)}, u32[]{:S(2)}, u32[]{:S(2)}) async-start(f32[8,20,128]{2,1,0:T(8,128)} %get-tuple-element.34), calls=%async_computation.1 | async-start | bytes 196608 | tf_op jit(solution)/shard_map/all_to_all | solution.py:679
  36.9 24.1 %all-to-all-start.2 = ((f32[16,20,128]{2,1,0:T(8,128)}), f32[16,20,128]{2,1,0:T(8,128)S(1)}, u32[]{:S(2)}, u32[]{:S(2)}) async-start(f32[16,20,128]{2,1,0:T(8,128)} %broadcast_in_dim.12), calls=%async_computation.2 | async-start | bytes 393216 | tf_op jit(solution)/shard_map/all_to_all | solution.py:449
  60.9 0.7 copy-start.3
  70.1 5.9 %collective-permute-start = (f32[656,128]{1,0:T(8,128)}, f32[656,128]{1,0:T(8,128)S(1)}, u32[]{:S(2)}, u32[]{:S(2)}) collective-permute-start(f32[656,128]{1,0:T(8,128)} %get-tuple-element.48), channel_id=1, source_target_pairs={{0,4},{4,0},{1,5},{5,1},{2,6},{6,2},{3,7},{7,3},{8,12},{12,8},{9,1... | collective-permute-start | bytes 1007624 | tf_op jit(solution)/shard_map/ppermute | solution.py:700
  72.0 13.5 %all-to-all-start.3 = ((bf16[8,264,128]{2,1,0:T(8,128)(2,1)}), bf16[8,264,128]{2,1,0:T(8,128)(2,1)S(1)}, u32[]{:S(2)}, u32[]{:S(2)}) async-start(bf16[8,264,128]{2,1,0:T(8,128)(2,1)} %get-tuple-element.46), calls=%async_computation.3 | async-start | bytes 1081344 | tf_op jit(solution)/shard_map/all_to_all | solution.py:701
  85.7 55.4 %copy-start = (s32[118]{0:T(128)S(1)}, s32[118]{0:T(128)}, u32[]{:S(2)}) copy-start(s32[118]{0:T(128)} %concatenate.17.scalars) | copy-start | bytes 1420
  85.7 55.4 %copy-start.1 = (f32[20,128]{1,0:T(8,128)S(1)}, f32[20,128]{1,0:T(8,128)}, u32[]{:S(2)}) copy-start(f32[20,128]{1,0:T(8,128)} %get-tuple-element.49.lse) | copy-start | bytes 30724
  124.6 16.5 %all-to-all-start.6 = ((bf16[8,264,128]{2,1,0:T(8,128)(2,1)}), bf16[8,264,128]{2,1,0:T(8,128)(2,1)S(1)}, u32[]{:S(2)}, u32[]{:S(2)}) async-start(bf16[8,264,128]{2,1,0:T(8,128)(2,1)} %broadcast_in_dim.15), calls=%async_computation.6 | async-start | bytes 1081344 | tf_op jit(solution)/shard_map/all_to_all | solution.py:449
  131.8 3.3 %collective-permute-start.1 = (bf16[656,128]{1,0:T(8,128)(2,1)S(1)}, bf16[656,128]{1,0:T(8,128)(2,1)S(1)}, u32[]{:S(2)}, u32[]{:S(2)}) collective-permute-start(bf16[656,128]{1,0:T(8,128)(2,1)S(1)} %fusion.6.own), channel_id=1, source_target_pairs={{0,4},{4,0},{1,5},{5,1},{2,6},{6,2},{3,7},{7,3},{8,12},{12,8},{9,1... | collective-permute-start | bytes 503816 | tf_op jit(solution)/shard_map/ppermute | solution.py:725

commit v9 on v8

--- a/solution.py
+++ b/solution.py
@@ -68,6 +68,15 @@
     for b in range(head_weight.shape[0]):
         half = pl.ds(pl.multiple_of((clade[b] % 2) * slab, slab), slab)
         wide_weight[b, half, :] = head_weight[b]
+
+
+def widen_pairs(pairs, head_weight, clade):
+    _, slab, species = head_weight.shape
+    pairs[...] = jnp.zeros_like(pairs)
+    for b in range(head_weight.shape[0]):
+        start = pl.multiple_of((b % 2) * 2 * slab + (clade[b] % 2) * slab, slab)
+        lanes = slice((b % 2) * species, (b % 2 + 1) * species)
+        pairs[b // 2, pl.ds(start, slab), lanes] = head_weight[b]
 
 
 def each_busy(busy, found, count, act):
@@ -105,7 +114,7 @@
     head_weight,
     terms,
     trunk,
-    wide_weight,
+    pairs,
     logits,
     tops,
     fetch_sem,
@@ -144,14 +153,17 @@
     trunk_copy = pltpu.make_async_copy(trunk, trunk_out, trunk_sem.at[0])
     trunk_copy.start()
     fetched[5].wait()
-    widen(wide_weight, head_weight, clade)
+    widen_pairs(pairs, head_weight, clade)
 
     def step(i):
-        for g in range(GROUP):
+        for g in range(0, GROUP, 2):
             b = i * GROUP + g
-            part = dot(features[clade[b] // 2], wide_weight[b])
-            logits[g] = part
-            tops[g] = jnp.max(part.reshape(cells // 8, 8, -1), axis=0)
+            left = [features[clade[b + j] // 2] for j in range(2)]
+            both = dot(jnp.concatenate(left, axis=1), pairs[b // 2])
+            for j in range(2):
+                part = both[:, j * tile : (j + 1) * tile]
+                logits[g + j] = part
+                tops[g + j] = jnp.max(part.reshape(cells // 8, 8, -1), axis=0)
         for g in range(GROUP):
             b = i * GROUP + g
             top = jnp.max(tops[g], axis=0, keepdims=True)
@@ -315,7 +327,7 @@
     hit_back,
     hit_grad,
     hit_sum,
-    wide_weight,
+    pairs,
     packed,
     bias,
     weight_cells,
@@ -352,7 +364,7 @@
     lse[...] = join([lses[i] for i in range(lses.shape[0])])
     high[...] = jnp.exp(high[...] - lse[...])
     early[2].wait()
-    widen(wide_weight, head_weight, clade)
+    widen_pairs(pairs, head_weight, clade)
     group = block_count // 2
     core = place[1]
 
@@ -373,7 +385,12 @@
             rows = slice((b % group) * slab, (b % group + 1) * slab)
             grad = soft_grad[b] * high[b : b + 1, :] - hit_grad[b, half, :]
             packed[b // group, rows, :] = grad
-            group_back[clade[b] // 2] += dot_t(weight_cells[b], wide_weight[b])
+        for g in range(0, GROUP, 2):
+            b = i * GROUP + g
+            left = [weight_cells[b + j] for j in range(2)]
+            both = dot_t(jnp.concatenate(left, axis=1), pairs[b // 2])
+            for j in range(2):
+                group_back[clade[b + j] // 2] += both[:, j * tile : (j + 1) * tile]
 
     for copy in late[3:]:
         copy.wait()
@@ -485,7 +502,7 @@
             pltpu.VMEM(head_weight.shape, BF16),
             pltpu.VMEM(by_clade, BF16),
             pltpu.VMEM(by_layer, BF16),
-            pltpu.VMEM((block_count, tile, species), BF16),
+            pltpu.VMEM((block_count // 2, 2 * tile, 2 * species), BF16),
             pltpu.VMEM((GROUP, cells, species), F32),
             pltpu.VMEM((GROUP, 8, species), F32),
             pltpu.SemaphoreType.DMA((6,)),
@@ -605,7 +622,7 @@
             pltpu.VMEM(by_block, BF16),
             pltpu.VMEM(hit_grad.shape, F32),
             pltpu.VMEM(hit_sum.shape, F32),
-            pltpu.VMEM((block_count, tile, species), BF16),
+            pltpu.VMEM((block_count // 2, 2 * tile, 2 * species), BF16),
             pltpu.VMEM((2, half_rows, tile), F32),
             pltpu.VMEM((2 * nx, 8, tile), F32),
             pltpu.VMEM(terms.shape, BF16),

time: 144 us -> 144 us (level)
  transfers between devices with their start and end apart: 7 -> 7, of which waited for: 6 -> 6; matrix products, arithmetic and copies ran while one was open for 3% -> 3% of each run, Pallas kernels for 9% -> 8%
where the time goes in v9:
time: 144 us; the launch traced here: 143 us
  starting transfers between devices  40.3 us (28%)
  blocking collectives  37.5 us (26%)
  Pallas kernels  30.7 us (21%)
  waiting for transfers between devices  24.6 us (17%)
  local copies, waits for them, and re-layouts  6.4 us (4%)
  other arithmetic  2.72 us (2%)
    all_to_all x3, starting transfers between devices, spread(): lax.all_to_all(jnp.broadcast_to(value[None], (size, *value.shape)), axis,...  25.5 us
    all_to_all x1, blocking collectives, body(): lax.all_to_all(cut, ('y', 'z'), 0, 0).astype(F32)  19.7 us
    all_to_all x1, blocking collectives, spread(): lax.all_to_all(jnp.broadcast_to(value[None], (size, *value.shape)), axis,...  17.9 us
    all_to_all x3, waiting for transfers between devices, spread(): lax.all_to_all(jnp.broadcast_to(value[None], (size, *value.shape)), axis,...  12.1 us
    pallas_call x1, Pallas kernels, backward(): pl.pallas_call(backward_kernel, name='backward', out_shape=(shape((2 * nx...  8.67 us
    all_to_all x1, waiting for transfers between devices, body(): trunk = jnp.sum(lax.all_to_all(trunk, ('c', 'x'), 0, 0).astype(F32), axis=0)  8.43 us
    pallas_call x1, Pallas kernels, forward(): pl.pallas_call(forward_kernel, name='forward', out_shape=(shape(by_clade,...  8.33 us
    pallas_call x1, Pallas kernels, middle(): pl.pallas_call(middle_kernel, name='middle', out_shape=(shape(by_block, B...  6.93 us
  transfers between devices with their start and end apart: 7, of which 6 were waited for; matrix products, arithmetic and copies ran while one was open for 3% of the time, Pallas kernels for 8%

profile of v9, /device:TPU:1, one launch (start us, length us, event | category | flops | bytes accessed | tf_op | source)
XLA Modules:
  0.0 143.0 jit_solution(3456418441385715901)
XLA Ops:
  0.6 1.6 %broadcast_in_dim.11 = bf16[4,128,256]{2,1,0:T(8,128)(2,1)} broadcast(bf16[128,256]{1,0:T(8,128)(2,1)} %param.10), dimensions={1,2} | broadcast | bytes 327680 | tf_op jit(solution)/shard_map/broadcast_in_dim | solution.py:466
  2.2 4.8 %all-to-all-start = ((bf16[4,128,256]{2,1,0:T(8,128)(2,1)}), bf16[4,128,256]{2,1,0:T(8,128)(2,1)S(1)}, u32[]{:S(2)}, u32[]{:S(2)}) async-start(bf16[4,128,256]{2,1,0:T(8,128)(2,1)} %broadcast_in_dim.11), calls=%async_computation | async-start | bytes 524288 | tf_op jit(solution)/shard_map/all_to_all | solution.py:466
  7.0 1.0 compare_reduce_fusion.3
  8.1 0.1 bitcast_reduce_fusion.2
  8.2 0.1 bitcast_reduce_fusion
  8.3 0.1 copy.26
  8.4 0.1 reshape.69
  8.5 1.4 concatenate.17.scalars
  9.9 2.7 %all-to-all-done = bf16[4,128,256]{2,1,0:T(8,128)(2,1)S(1)} async-done(((bf16[4,128,256]{2,1,0:T(8,128)(2,1)}), bf16[4,128,256]{2,1,0:T(8,128)(2,1)S(1)}, u32[]{:S(2)}, u32[]{:S(2)}) %all-to-all-start) | async-done | bytes 262176 | tf_op jit(solution)/shard_map/all_to_all | solution.py:466
  12.6 0.0 copy-start.2
  12.6 0.7 copy-done.2
  13.3 8.3 %forward.1 = (bf16[20,512,128]{2,1,0:T(8,128)(2,1)}, bf16[4,8,512,128]{3,2,1,0:T(8,128)(2,1)}, f32[8,20,128]{2,1,0:T(8,128)}, f32[20,128]{1,0:T(8,128)}) custom-call(s32[118]{0:T(128)} %concatenate.17.scalars, bf16[512,256]{1,0:T(8,128)(2,1)} %bitcast.67, bf16[8,128,128]{2,1,0:T(8,128)(2,1)} %first_weight_in.1, f32[8,128]{1,0:T(8,128)} %bitcast.73, ...), custom_call_target="tpu_custom_call" | custom-call | tf_op jit(solution)/shard_map/forward/pallas_call | solution.py:485
  21.6 6.9 %all-to-all-start.1 = ((f32[8,20,128]{2,1,0:T(8,128)}), f32[8,20,128]{2,1,0:T(8,128)S(1)}, u32[]{:S(2)}, u32[]{:S(2)}) async-start(f32[8,20,128]{2,1,0:T(8,128)} %get-tuple-element.34), calls=%async_computation.1 | async-start | bytes 196608 | tf_op jit(solution)/shard_map/all_to_all | solution.py:696
  28.5 4.9 %early.1 = (bf16[2,128,512]{2,1,0:T(8,128)(2,1)}, bf16[8,128,512]{2,1,0:T(8,128)(2,1)}, f32[20,64,128]{2,1,0:T(8,128)}) custom-call(s32[118]{0:T(128)} %concatenate.17.scalars, bf16[512,256]{1,0:T(8,128)(2,1)} %bitcast.68, bf16[4,8,512,128]{3,2,1,0:T(8,128)(2,1)} %get-tuple-element.32.trunk_in, bf16[20,512,128]{2,1,0:T(8,128)(2,1)} %get-tuple-element.31.terms_in), custom_call_target="tpu_custom_call" | custom-call | flops 335544320 | bytes 7864320 | tf_op jit(solution)/shard_map/early/pallas_call | solution.py:529
  33.4 2.8 %all-to-all-done.1 = f32[8,20,128]{2,1,0:T(8,128)S(1)} async-done(((f32[8,20,128]{2,1,0:T(8,128)}), f32[8,20,128]{2,1,0:T(8,128)S(1)}, u32[]{:S(2)}, u32[]{:S(2)}) %all-to-all-start.1) | async-done | bytes 81952 | tf_op jit(solution)/shard_map/all_to_all | solution.py:696
  36.2 0.7 broadcast_in_dim.12
  36.9 13.7 %all-to-all-start.2 = ((f32[16,20,128]{2,1,0:T(8,128)}), f32[16,20,128]{2,1,0:T(8,128)S(1)}, u32[]{:S(2)}, u32[]{:S(2)}) async-start(f32[16,20,128]{2,1,0:T(8,128)} %broadcast_in_dim.12), calls=%async_computation.2 | async-start | bytes 393216 | tf_op jit(solution)/shard_map/all_to_all | solution.py:466
  50.6 6.9 %middle.1 = (bf16[8,512,128]{2,1,0:T(8,128)(2,1)}, f32[20,128,128]{2,1,0:T(8,128)}, f32[20,128]{1,0:T(8,128)}) custom-call(s32[118]{0:T(128)} %concatenate.17.scalars, s32[16,2560]{1,0:T(8,128)} %bitcast.71, bf16[20,64,128]{2,1,0:T(8,128)(2,1)} %head_weight_in.5, bf16[4,8,512,128]{3,2,1,0:T(8,128)(2,1)} %get-tuple-element.32.trunk_in), custom_call_target="tpu_custom_call" | custom-call | flops 1342177280 | bytes 4194304 | tf_op jit(solution)/shard_map/middle/pallas_call | solution.py:560
  57.6 3.4 %all-to-all-done.2.lses_in = f32[16,20,128]{2,1,0:T(8,128)S(1)} async-done(((f32[16,20,128]{2,1,0:T(8,128)}), f32[16,20,128]{2,1,0:T(8,128)S(1)}, u32[]{:S(2)}, u32[]{:S(2)}) %all-to-all-start.2) | async-done | bytes 163872 | tf_op jit(solution)/shard_map/all_to_all | solution.py:466
  60.9 0.0 copy-start.3
  60.9 0.7 copy-done.3
  61.6 8.7 %backward.1 = (bf16[8,264,128]{2,1,0:T(8,128)(2,1)}, f32[656,128]{1,0:T(8,128)}, f32[656,128]{1,0:T(8,128)}, f32[20,128]{1,0:T(8,128)}) custom-call(s32[118]{0:T(128)} %concatenate.17.scalars, bf16[8,128,128]{2,1,0:T(8,128)(2,1)} %second_weight_in.3, bf16[20,64,128]{2,1,0:T(8,128)(2,1)} %head_weight_in.5, bf16[20,512,128]{2,1,0:T(8,128)(2,1)} %get-tuple-element.31.terms_in, ...), custom_call_target="tpu_custom_call" | custom-call | tf_op jit(solution)/shard_map/backward/pallas_call | solution.py:601
  70.3 1.9 %collective-permute-start = (f32[656,128]{1,0:T(8,128)}, f32[656,128]{1,0:T(8,128)S(1)}, u32[]{:S(2)}, u32[]{:S(2)}) collective-permute-start(f32[656,128]{1,0:T(8,128)} %get-tuple-element.48), channel_id=1, source_target_pairs={{0,4},{4,0},{1,5},{5,1},{2,6},{6,2},{3,7},{7,3},{8,12},{12,8},{9,1... | collective-permute-start | bytes 1007624 | tf_op jit(solution)/shard_map/ppermute | solution.py:717
  72.2 4.0 %all-to-all-start.3 = ((bf16[8,264,128]{2,1,0:T(8,128)(2,1)}), bf16[8,264,128]{2,1,0:T(8,128)(2,1)S(1)}, u32[]{:S(2)}, u32[]{:S(2)}) async-start(bf16[8,264,128]{2,1,0:T(8,128)(2,1)} %get-tuple-element.46), calls=%async_computation.3 | async-start | bytes 1081344 | tf_op jit(solution)/shard_map/all_to_all | solution.py:718
  76.2 0.0 collective-permute-done
  76.2 1.0 add_convert_fusion
  77.3 0.1 reshape.63
  77.3 8.4 %all-to-all-done.3 = bf16[8,264,128]{2,1,0:T(8,128)(2,1)S(1)} async-done(((bf16[8,264,128]{2,1,0:T(8,128)(2,1)}), bf16[8,264,128]{2,1,0:T(8,128)(2,1)S(1)}, u32[]{:S(2)}, u32[]{:S(2)}) %all-to-all-start.3) | async-done | bytes 540704 | tf_op jit(solution)/shard_map/all_to_all | solution.py:718
  85.8 0.1 reduce.9
  85.9 0.0 copy-start
  85.9 0.0 copy-start.1
  85.9 0.2 fusion.5
  86.1 19.7 %all_to_all.35 = bf16[64,16,128]{2,1,0:T(8,128)(2,1)S(1)} all-to-all(bf16[64,16,128]{2,1,0:T(8,128)(2,1)S(1)} %fusion.5), channel_id=1, replica_groups=mesh['y'=8,'z'=8,'c'=2,'x'=4] {'y','z'}, dimensions={0} | all-to-all | bytes 524288 | tf_op jit(solution)/shard_map/all_to_all | solution.py:732
  105.8 0.1 reduce_sum.22
  105.9 17.9 %all_to_all.36 = bf16[64,16,128]{2,1,0:T(8,128)(2,1)S(1)} all-to-all(bf16[64,16,128]{2,1,0:T(8,128)(2,1)S(1)} %broadcast_in_dim.14), channel_id=1, replica_groups=mesh['y'=8,'z'=8,'c'=2,'x'=4] {'y','z'}, dimensions={0} | all-to-all | bytes 524288 | tf_op jit(solution)/shard_map/all_to_all | solution.py:466
  123.8 0.9 broadcast_in_dim.15
  124.7 7.0 %all-to-all-start.6 = ((bf16[8,264,128]{2,1,0:T(8,128)(2,1)}), bf16[8,264,128]{2,1,0:T(8,128)(2,1)S(1)}, u32[]{:S(2)}, u32[]{:S(2)}) async-start(bf16[8,264,128]{2,1,0:T(8,128)(2,1)} %broadcast_in_dim.15), calls=%async_computation.6 | async-start | bytes 1081344 | tf_op jit(solution)/shard_map/all_to_all | solution.py:466
  131.7 0.1 slice.103
  131.8 0.1 reshape.65
  131.9 2.0 %collective-permute-start.1 = (bf16[656,128]{1,0:T(8,128)(2,1)S(1)}, bf16[656,128]{1,0:T(8,128)(2,1)S(1)}, u32[]{:S(2)}, u32[]{:S(2)}) collective-permute-start(bf16[656,128]{1,0:T(8,128)(2,1)S(1)} %fusion.6.own), channel_id=1, source_target_pairs={{0,4},{4,0},{1,5},{5,1},{2,6},{6,2},{3,7},{7,3},{8,12},{12,8},{9,1... | collective-permute-start | bytes 503816 | tf_op jit(solution)/shard_map/ppermute | solution.py:742
  133.9 1.3 collective-permute-done.1.other
  135.2 6.0 %all-to-all-done.6.trunk = bf16[8,264,128]{2,1,0:T(8,128)(2,1)S(1)} async-done(((bf16[8,264,128]{2,1,0:T(8,128)(2,1)}), bf16[8,264,128]{2,1,0:T(8,128)(2,1)S(1)}, u32[]{:S(2)}, u32[]{:S(2)}) %all-to-all-start.6) | async-done | bytes 540704 | tf_op jit(solution)/shard_map/all_to_all | solution.py:466
  141.2 0.0 copy-done
  141.2 0.0 copy-done.1
  141.2 1.8 %finish.1 = (f32[20,128]{1,0:T(8,128)}, f32[20,64,128]{2,1,0:T(8,128)}, f32[8,128,128]{2,1,0:T(8,128)}, f32[8,128]{1,0:T(8,128)}, f32[8,128,128]{2,1,0:T(8,128)}, /*index=5*/f32[8,128]{1,0:T(8,128)}) custom-call(s32[118]{0:T(128)S(1)} %copy-done, bf16[8,264,128]{2,1,0:T(8,128)(2,1)S(1)} %all-to-all-done.6.trunk, bf16[656,128]{1,0:T(8,128)(2,1)S(1)} %fusion.6.own, ...), custom_call_target="tpu_custom_call" | custom-call | tf_op jit(solution)/shard_map/finish/pallas_call | solution.py:752
  (16 shorter events, 0.2 us)
Async XLA Ops:
  2.2 10.4 %all-to-all-start = ((bf16[4,128,256]{2,1,0:T(8,128)(2,1)}), bf16[4,128,256]{2,1,0:T(8,128)(2,1)S(1)}, u32[]{:S(2)}, u32[]{:S(2)}) async-start(bf16[4,128,256]{2,1,0:T(8,128)(2,1)} %broadcast_in_dim.11), calls=%async_computation | async-start | bytes 524288 | tf_op jit(solution)/shard_map/all_to_all | solution.py:466
  12.6 0.7 copy-start.2
  21.6 14.5 %all-to-all-start.1 = ((f32[8,20,128]{2,1,0:T(8,128)}), f32[8,20,128]{2,1,0:T(8,128)S(1)}, u32[]{:S(2)}, u32[]{:S(2)}) async-start(f32[8,20,128]{2,1,0:T(8,128)} %get-tuple-element.34), calls=%async_computation.1 | async-start | bytes 196608 | tf_op jit(solution)/shard_map/all_to_all | solution.py:696
  36.9 24.1 %all-to-all-start.2 = ((f32[16,20,128]{2,1,0:T(8,128)}), f32[16,20,128]{2,1,0:T(8,128)S(1)}, u32[]{:S(2)}, u32[]{:S(2)}) async-start(f32[16,20,128]{2,1,0:T(8,128)} %broadcast_in_dim.12), calls=%async_computation.2 | async-start | bytes 393216 | tf_op jit(solution)/shard_map/all_to_all | solution.py:466
  60.9 0.7 copy-start.3
  70.3 5.9 %collective-permute-start = (f32[656,128]{1,0:T(8,128)}, f32[656,128]{1,0:T(8,128)S(1)}, u32[]{:S(2)}, u32[]{:S(2)}) collective-permute-start(f32[656,128]{1,0:T(8,128)} %get-tuple-element.48), channel_id=1, source_target_pairs={{0,4},{4,0},{1,5},{5,1},{2,6},{6,2},{3,7},{7,3},{8,12},{12,8},{9,1... | collective-permute-start | bytes 1007624 | tf_op jit(solution)/shard_map/ppermute | solution.py:717
  72.2 13.5 %all-to-all-start.3 = ((bf16[8,264,128]{2,1,0:T(8,128)(2,1)}), bf16[8,264,128]{2,1,0:T(8,128)(2,1)S(1)}, u32[]{:S(2)}, u32[]{:S(2)}) async-start(bf16[8,264,128]{2,1,0:T(8,128)(2,1)} %get-tuple-element.46), calls=%async_computation.3 | async-start | bytes 1081344 | tf_op jit(solution)/shard_map/all_to_all | solution.py:718
  85.9 55.3 %copy-start = (s32[118]{0:T(128)S(1)}, s32[118]{0:T(128)}, u32[]{:S(2)}) copy-start(s32[118]{0:T(128)} %concatenate.17.scalars) | copy-start | bytes 1420
  85.9 55.3 %copy-start.1 = (f32[20,128]{1,0:T(8,128)S(1)}, f32[20,128]{1,0:T(8,128)}, u32[]{:S(2)}) copy-start(f32[20,128]{1,0:T(8,128)} %get-tuple-element.49.lse) | copy-start | bytes 30724
  124.7 16.5 %all-to-all-start.6 = ((bf16[8,264,128]{2,1,0:T(8,128)(2,1)}), bf16[8,264,128]{2,1,0:T(8,128)(2,1)S(1)}, u32[]{:S(2)}, u32[]{:S(2)}) async-start(bf16[8,264,128]{2,1,0:T(8,128)(2,1)} %broadcast_in_dim.15), calls=%async_computation.6 | async-start | bytes 1081344 | tf_op jit(solution)/shard_map/all_to_all | solution.py:466
  131.9 3.3 %collective-permute-start.1 = (bf16[656,128]{1,0:T(8,128)(2,1)S(1)}, bf16[656,128]{1,0:T(8,128)(2,1)S(1)}, u32[]{:S(2)}, u32[]{:S(2)}) collective-permute-start(bf16[656,128]{1,0:T(8,128)(2,1)S(1)} %fusion.6.own), channel_id=1, source_target_pairs={{0,4},{4,0},{1,5},{5,1},{2,6},{6,2},{3,7},{7,3},{8,12},{12,8},{9,1... | collective-permute-start | bytes 503816 | tf_op jit(solution)/shard_map/ppermute | solution.py:742

commit v10 on v8

--- a/solution.py
+++ b/solution.py
@@ -336,6 +336,17 @@
     )
     pieces = [pl.ds(i * GROUP, GROUP) for i in range(block_count // GROUP)]
     term_copies = fetch(term_sem, *[(terms_in.at[p], terms.at[p]) for p in pieces])
+    early[0].wait()
+    early[1].wait()
+    lse[...] = join([lses[i] for i in range(lses.shape[0])])
+    high[...] = jnp.exp(high[...] - lse[...])
+    early[2].wait()
+    widen(wide_weight, head_weight, clade)
+    group = block_count // 2
+    core = place[1]
+
+    act_grad[...] = jnp.zeros_like(act_grad)
+    term_copies[0].wait()
     late = fetch(
         fetch_sem.at[pl.ds(len(early), 8)],
         (hit_back_in, hit_back),
@@ -347,18 +358,9 @@
         (covariates_t_in, covariates_t),
         (hit_sum_in, hit_sum),
     )
-    early[0].wait()
-    early[1].wait()
-    lse[...] = join([lses[i] for i in range(lses.shape[0])])
-    high[...] = jnp.exp(high[...] - lse[...])
-    early[2].wait()
-    widen(wide_weight, head_weight, clade)
-    group = block_count // 2
-    core = place[1]
-
-    act_grad[...] = jnp.zeros_like(act_grad)
     for i, copy in enumerate(term_copies):
-        copy.wait()
+        if i > 0:
+            copy.wait()
         for b in range(i * GROUP, (i + 1) * GROUP):
             weights = terms[b].astype(F32) * high[b : b + 1, :]
             weight_cells[b] = weights.astype(BF16)

time: 144 us -> 143 us (level)
  transfers between devices with their start and end apart: 7 -> 7, of which waited for: 6 -> 6; matrix products, arithmetic and copies ran while one was open for 3% -> 3% of each run, Pallas kernels for 9% -> 8%
where the time goes in v10:
time: 143 us; the launch traced here: 142 us
  starting transfers between devices  40.3 us (28%)
  blocking collectives  36.8 us (26%)
  Pallas kernels  29.9 us (21%)
  waiting for transfers between devices  24.6 us (17%)
  local copies, waits for them, and re-layouts  6.4 us (4%)
  other arithmetic  2.72 us (2%)
    all_to_all x3, starting transfers between devices, spread(): lax.all_to_all(jnp.broadcast_to(value[None], (size, *value.shape)), axis,...  25.5 us
    all_to_all x1, blocking collectives, body(): lax.all_to_all(cut, ('y', 'z'), 0, 0).astype(F32)  19 us
    all_to_all x1, blocking collectives, spread(): lax.all_to_all(jnp.broadcast_to(value[None], (size, *value.shape)), axis,...  17.8 us
    all_to_all x3, waiting for transfers between devices, spread(): lax.all_to_all(jnp.broadcast_to(value[None], (size, *value.shape)), axis,...  12.1 us
    all_to_all x1, waiting for transfers between devices, body(): trunk = jnp.sum(lax.all_to_all(trunk, ('c', 'x'), 0, 0).astype(F32), axis=0)  8.43 us
    pallas_call x1, Pallas kernels, forward(): pl.pallas_call(forward_kernel, name='forward', out_shape=(shape(by_clade,...  8.34 us
    pallas_call x1, Pallas kernels, backward(): pl.pallas_call(backward_kernel, name='backward', out_shape=(shape((2 * nx...  7.91 us
    pallas_call x1, Pallas kernels, middle(): pl.pallas_call(middle_kernel, name='middle', out_shape=(shape(by_block, B...  6.94 us
  transfers between devices with their start and end apart: 7, of which 6 were waited for; matrix products, arithmetic and copies ran while one was open for 3% of the time, Pallas kernels for 8%

profile of v10, /device:TPU:1, one launch (start us, length us, event | category | flops | bytes accessed | tf_op | source)
XLA Modules:
  0.0 141.5 jit_solution(14265799075754903354)
XLA Ops:
  0.6 1.6 %broadcast_in_dim.11 = bf16[4,128,256]{2,1,0:T(8,128)(2,1)} broadcast(bf16[128,256]{1,0:T(8,128)(2,1)} %param.10), dimensions={1,2} | broadcast | bytes 327680 | tf_op jit(solution)/shard_map/broadcast_in_dim | solution.py:451
  2.2 4.8 %all-to-all-start = ((bf16[4,128,256]{2,1,0:T(8,128)(2,1)}), bf16[4,128,256]{2,1,0:T(8,128)(2,1)S(1)}, u32[]{:S(2)}, u32[]{:S(2)}) async-start(bf16[4,128,256]{2,1,0:T(8,128)(2,1)} %broadcast_in_dim.11), calls=%async_computation | async-start | bytes 524288 | tf_op jit(solution)/shard_map/all_to_all | solution.py:451
  7.0 1.0 compare_reduce_fusion.3
  8.1 0.1 bitcast_reduce_fusion.2
  8.2 0.1 bitcast_reduce_fusion
  8.3 0.1 copy.26
  8.4 0.1 reshape.69
  8.5 1.4 concatenate.17.scalars
  9.9 2.7 %all-to-all-done = bf16[4,128,256]{2,1,0:T(8,128)(2,1)S(1)} async-done(((bf16[4,128,256]{2,1,0:T(8,128)(2,1)}), bf16[4,128,256]{2,1,0:T(8,128)(2,1)S(1)}, u32[]{:S(2)}, u32[]{:S(2)}) %all-to-all-start) | async-done | bytes 262176 | tf_op jit(solution)/shard_map/all_to_all | solution.py:451
  12.6 0.0 copy-start.2
  12.6 0.7 copy-done.2
  13.3 8.3 %forward.1 = (bf16[20,512,128]{2,1,0:T(8,128)(2,1)}, bf16[4,8,512,128]{3,2,1,0:T(8,128)(2,1)}, f32[8,20,128]{2,1,0:T(8,128)}, f32[20,128]{1,0:T(8,128)}) custom-call(s32[118]{0:T(128)} %concatenate.17.scalars, bf16[512,256]{1,0:T(8,128)(2,1)} %bitcast.67, bf16[8,128,128]{2,1,0:T(8,128)(2,1)} %first_weight_in.1, f32[8,128]{1,0:T(8,128)} %bitcast.73, ...), custom_call_target="tpu_custom_call" | custom-call | tf_op jit(solution)/shard_map/forward/pallas_call | solution.py:470
  21.6 6.9 %all-to-all-start.1 = ((f32[8,20,128]{2,1,0:T(8,128)}), f32[8,20,128]{2,1,0:T(8,128)S(1)}, u32[]{:S(2)}, u32[]{:S(2)}) async-start(f32[8,20,128]{2,1,0:T(8,128)} %get-tuple-element.34), calls=%async_computation.1 | async-start | bytes 196608 | tf_op jit(solution)/shard_map/all_to_all | solution.py:681
  28.5 4.9 %early.1 = (bf16[2,128,512]{2,1,0:T(8,128)(2,1)}, bf16[8,128,512]{2,1,0:T(8,128)(2,1)}, f32[20,64,128]{2,1,0:T(8,128)}) custom-call(s32[118]{0:T(128)} %concatenate.17.scalars, bf16[512,256]{1,0:T(8,128)(2,1)} %bitcast.68, bf16[4,8,512,128]{3,2,1,0:T(8,128)(2,1)} %get-tuple-element.32.trunk_in, bf16[20,512,128]{2,1,0:T(8,128)(2,1)} %get-tuple-element.31.terms_in), custom_call_target="tpu_custom_call" | custom-call | flops 335544320 | bytes 7864320 | tf_op jit(solution)/shard_map/early/pallas_call | solution.py:514
  33.4 2.8 %all-to-all-done.1 = f32[8,20,128]{2,1,0:T(8,128)S(1)} async-done(((f32[8,20,128]{2,1,0:T(8,128)}), f32[8,20,128]{2,1,0:T(8,128)S(1)}, u32[]{:S(2)}, u32[]{:S(2)}) %all-to-all-start.1) | async-done | bytes 81952 | tf_op jit(solution)/shard_map/all_to_all | solution.py:681
  36.2 0.7 broadcast_in_dim.12
  36.9 13.7 %all-to-all-start.2 = ((f32[16,20,128]{2,1,0:T(8,128)}), f32[16,20,128]{2,1,0:T(8,128)S(1)}, u32[]{:S(2)}, u32[]{:S(2)}) async-start(f32[16,20,128]{2,1,0:T(8,128)} %broadcast_in_dim.12), calls=%async_computation.2 | async-start | bytes 393216 | tf_op jit(solution)/shard_map/all_to_all | solution.py:451
  50.6 6.9 %middle.1 = (bf16[8,512,128]{2,1,0:T(8,128)(2,1)}, f32[20,128,128]{2,1,0:T(8,128)}, f32[20,128]{1,0:T(8,128)}) custom-call(s32[118]{0:T(128)} %concatenate.17.scalars, s32[16,2560]{1,0:T(8,128)} %bitcast.71, bf16[20,64,128]{2,1,0:T(8,128)(2,1)} %head_weight_in.5, bf16[4,8,512,128]{3,2,1,0:T(8,128)(2,1)} %get-tuple-element.32.trunk_in), custom_call_target="tpu_custom_call" | custom-call | flops 1342177280 | bytes 4194304 | tf_op jit(solution)/shard_map/middle/pallas_call | solution.py:545
  57.6 3.4 %all-to-all-done.2.lses_in = f32[16,20,128]{2,1,0:T(8,128)S(1)} async-done(((f32[16,20,128]{2,1,0:T(8,128)}), f32[16,20,128]{2,1,0:T(8,128)S(1)}, u32[]{:S(2)}, u32[]{:S(2)}) %all-to-all-start.2) | async-done | bytes 163872 | tf_op jit(solution)/shard_map/all_to_all | solution.py:451
  60.9 0.0 copy-start.3
  61.0 0.7 copy-done.3
  61.6 7.9 %backward.1 = (bf16[8,264,128]{2,1,0:T(8,128)(2,1)}, f32[656,128]{1,0:T(8,128)}, f32[656,128]{1,0:T(8,128)}, f32[20,128]{1,0:T(8,128)}) custom-call(s32[118]{0:T(128)} %concatenate.17.scalars, bf16[8,128,128]{2,1,0:T(8,128)(2,1)} %second_weight_in.3, bf16[20,64,128]{2,1,0:T(8,128)(2,1)} %head_weight_in.5, bf16[20,512,128]{2,1,0:T(8,128)(2,1)} %get-tuple-element.31.terms_in, ...), custom_call_target="tpu_custom_call" | custom-call | tf_op jit(solution)/shard_map/backward/pallas_call | solution.py:586
  69.6 1.9 %collective-permute-start = (f32[656,128]{1,0:T(8,128)}, f32[656,128]{1,0:T(8,128)S(1)}, u32[]{:S(2)}, u32[]{:S(2)}) collective-permute-start(f32[656,128]{1,0:T(8,128)} %get-tuple-element.48), channel_id=1, source_target_pairs={{0,4},{4,0},{1,5},{5,1},{2,6},{6,2},{3,7},{7,3},{8,12},{12,8},{9,1... | collective-permute-start | bytes 1007624 | tf_op jit(solution)/shard_map/ppermute | solution.py:702
  71.5 4.0 %all-to-all-start.3 = ((bf16[8,264,128]{2,1,0:T(8,128)(2,1)}), bf16[8,264,128]{2,1,0:T(8,128)(2,1)S(1)}, u32[]{:S(2)}, u32[]{:S(2)}) async-start(bf16[8,264,128]{2,1,0:T(8,128)(2,1)} %get-tuple-element.46), calls=%async_computation.3 | async-start | bytes 1081344 | tf_op jit(solution)/shard_map/all_to_all | solution.py:703
  75.5 0.0 collective-permute-done
  75.5 1.0 add_convert_fusion
  76.5 0.1 reshape.63
  76.6 8.4 %all-to-all-done.3 = bf16[8,264,128]{2,1,0:T(8,128)(2,1)S(1)} async-done(((bf16[8,264,128]{2,1,0:T(8,128)(2,1)}), bf16[8,264,128]{2,1,0:T(8,128)(2,1)S(1)}, u32[]{:S(2)}, u32[]{:S(2)}) %all-to-all-start.3) | async-done | bytes 540704 | tf_op jit(solution)/shard_map/all_to_all | solution.py:703
  85.0 0.1 reduce.9
  85.2 0.0 copy-start
  85.2 0.0 copy-start.1
  85.2 0.2 fusion.5
  85.4 19.0 %all_to_all.35 = bf16[64,16,128]{2,1,0:T(8,128)(2,1)S(1)} all-to-all(bf16[64,16,128]{2,1,0:T(8,128)(2,1)S(1)} %fusion.5), channel_id=1, replica_groups=mesh['y'=8,'z'=8,'c'=2,'x'=4] {'y','z'}, dimensions={0} | all-to-all | bytes 524288 | tf_op jit(solution)/shard_map/all_to_all | solution.py:717
  104.3 0.1 reduce_sum.22
  104.5 17.8 %all_to_all.36 = bf16[64,16,128]{2,1,0:T(8,128)(2,1)S(1)} all-to-all(bf16[64,16,128]{2,1,0:T(8,128)(2,1)S(1)} %broadcast_in_dim.14), channel_id=1, replica_groups=mesh['y'=8,'z'=8,'c'=2,'x'=4] {'y','z'}, dimensions={0} | all-to-all | bytes 524288 | tf_op jit(solution)/shard_map/all_to_all | solution.py:451
  122.3 0.9 broadcast_in_dim.15
  123.2 7.0 %all-to-all-start.6 = ((bf16[8,264,128]{2,1,0:T(8,128)(2,1)}), bf16[8,264,128]{2,1,0:T(8,128)(2,1)S(1)}, u32[]{:S(2)}, u32[]{:S(2)}) async-start(bf16[8,264,128]{2,1,0:T(8,128)(2,1)} %broadcast_in_dim.15), calls=%async_computation.6 | async-start | bytes 1081344 | tf_op jit(solution)/shard_map/all_to_all | solution.py:451
  130.2 0.1 slice.103
  130.3 0.1 reshape.65
  130.4 2.0 %collective-permute-start.1 = (bf16[656,128]{1,0:T(8,128)(2,1)S(1)}, bf16[656,128]{1,0:T(8,128)(2,1)S(1)}, u32[]{:S(2)}, u32[]{:S(2)}) collective-permute-start(bf16[656,128]{1,0:T(8,128)(2,1)S(1)} %fusion.6.own), channel_id=1, source_target_pairs={{0,4},{4,0},{1,5},{5,1},{2,6},{6,2},{3,7},{7,3},{8,12},{12,8},{9,1... | collective-permute-start | bytes 503816 | tf_op jit(solution)/shard_map/ppermute | solution.py:727
  132.4 1.3 collective-permute-done.1.other
  133.7 6.0 %all-to-all-done.6.trunk = bf16[8,264,128]{2,1,0:T(8,128)(2,1)S(1)} async-done(((bf16[8,264,128]{2,1,0:T(8,128)(2,1)}), bf16[8,264,128]{2,1,0:T(8,128)(2,1)S(1)}, u32[]{:S(2)}, u32[]{:S(2)}) %all-to-all-start.6) | async-done | bytes 540704 | tf_op jit(solution)/shard_map/all_to_all | solution.py:451
  139.7 0.0 copy-done
  139.7 0.0 copy-done.1
  139.7 1.8 %finish.1 = (f32[20,128]{1,0:T(8,128)}, f32[20,64,128]{2,1,0:T(8,128)}, f32[8,128,128]{2,1,0:T(8,128)}, f32[8,128]{1,0:T(8,128)}, f32[8,128,128]{2,1,0:T(8,128)}, /*index=5*/f32[8,128]{1,0:T(8,128)}) custom-call(s32[118]{0:T(128)S(1)} %copy-done, bf16[8,264,128]{2,1,0:T(8,128)(2,1)S(1)} %all-to-all-done.6.trunk, bf16[656,128]{1,0:T(8,128)(2,1)S(1)} %fusion.6.own, ...), custom_call_target="tpu_custom_call" | custom-call | tf_op jit(solution)/shard_map/finish/pallas_call | solution.py:737
  (16 shorter events, 0.2 us)
Async XLA Ops:
  2.2 10.4 %all-to-all-start = ((bf16[4,128,256]{2,1,0:T(8,128)(2,1)}), bf16[4,128,256]{2,1,0:T(8,128)(2,1)S(1)}, u32[]{:S(2)}, u32[]{:S(2)}) async-start(bf16[4,128,256]{2,1,0:T(8,128)(2,1)} %broadcast_in_dim.11), calls=%async_computation | async-start | bytes 524288 | tf_op jit(solution)/shard_map/all_to_all | solution.py:451
  12.6 0.7 copy-start.2
  21.6 14.5 %all-to-all-start.1 = ((f32[8,20,128]{2,1,0:T(8,128)}), f32[8,20,128]{2,1,0:T(8,128)S(1)}, u32[]{:S(2)}, u32[]{:S(2)}) async-start(f32[8,20,128]{2,1,0:T(8,128)} %get-tuple-element.34), calls=%async_computation.1 | async-start | bytes 196608 | tf_op jit(solution)/shard_map/all_to_all | solution.py:681
  36.9 24.1 %all-to-all-start.2 = ((f32[16,20,128]{2,1,0:T(8,128)}), f32[16,20,128]{2,1,0:T(8,128)S(1)}, u32[]{:S(2)}, u32[]{:S(2)}) async-start(f32[16,20,128]{2,1,0:T(8,128)} %broadcast_in_dim.12), calls=%async_computation.2 | async-start | bytes 393216 | tf_op jit(solution)/shard_map/all_to_all | solution.py:451
  60.9 0.7 copy-start.3
  69.6 5.9 %collective-permute-start = (f32[656,128]{1,0:T(8,128)}, f32[656,128]{1,0:T(8,128)S(1)}, u32[]{:S(2)}, u32[]{:S(2)}) collective-permute-start(f32[656,128]{1,0:T(8,128)} %get-tuple-element.48), channel_id=1, source_target_pairs={{0,4},{4,0},{1,5},{5,1},{2,6},{6,2},{3,7},{7,3},{8,12},{12,8},{9,1... | collective-permute-start | bytes 1007624 | tf_op jit(solution)/shard_map/ppermute | solution.py:702
  71.5 13.5 %all-to-all-start.3 = ((bf16[8,264,128]{2,1,0:T(8,128)(2,1)}), bf16[8,264,128]{2,1,0:T(8,128)(2,1)S(1)}, u32[]{:S(2)}, u32[]{:S(2)}) async-start(bf16[8,264,128]{2,1,0:T(8,128)(2,1)} %get-tuple-element.46), calls=%async_computation.3 | async-start | bytes 1081344 | tf_op jit(solution)/shard_map/all_to_all | solution.py:703
  85.2 54.5 %copy-start = (s32[118]{0:T(128)S(1)}, s32[118]{0:T(128)}, u32[]{:S(2)}) copy-start(s32[118]{0:T(128)} %concatenate.17.scalars) | copy-start | bytes 1420
  85.2 54.5 %copy-start.1 = (f32[20,128]{1,0:T(8,128)S(1)}, f32[20,128]{1,0:T(8,128)}, u32[]{:S(2)}) copy-start(f32[20,128]{1,0:T(8,128)} %get-tuple-element.49.lse) | copy-start | bytes 30724
  123.2 16.5 %all-to-all-start.6 = ((bf16[8,264,128]{2,1,0:T(8,128)(2,1)}), bf16[8,264,128]{2,1,0:T(8,128)(2,1)S(1)}, u32[]{:S(2)}, u32[]{:S(2)}) async-start(bf16[8,264,128]{2,1,0:T(8,128)(2,1)} %broadcast_in_dim.15), calls=%async_computation.6 | async-start | bytes 1081344 | tf_op jit(solution)/shard_map/all_to_all | solution.py:451
  130.4 3.3 %collective-permute-start.1 = (bf16[656,128]{1,0:T(8,128)(2,1)S(1)}, bf16[656,128]{1,0:T(8,128)(2,1)S(1)}, u32[]{:S(2)}, u32[]{:S(2)}) collective-permute-start(bf16[656,128]{1,0:T(8,128)(2,1)S(1)} %fusion.6.own), channel_id=1, source_target_pairs={{0,4},{4,0},{1,5},{5,1},{2,6},{6,2},{3,7},{7,3},{8,12},{12,8},{9,1... | collective-permute-start | bytes 503816 | tf_op jit(solution)/shard_map/ppermute | solution.py:727
